TPU v7x, 32 devices: a whole 2x2x4 slice. The times are simulated.
32 devices in a mesh: frame: 4 (over y, core), row: 8 (over z, x).
Axes of the slice: x: 2, y: 2, z: 4, core: 2. Of those that a mesh axis runs over, the one named last changes fastest.
Arguments:
- tokens: bfloat16 [2, 8, 8, 32, 1536], P(None, 'frame', 'row'), may hold values from -6 to 6
- w_query: bfloat16 [1536, 1536], P(('frame', 'row')), may hold values from -0.15625 to 0.15625
- w_key: bfloat16 [1536, 1536], P(('frame', 'row')), may hold values from -0.15625 to 0.15625
- w_value: bfloat16 [1536, 1536], P(('frame', 'row')), may hold values from -0.15625 to 0.15625
- w_out: bfloat16 [1536, 1536], P(('frame', 'row')), may hold values from -0.15625 to 0.15625
- w_gate: bfloat16 [1536, 4096], P(('frame', 'row')), may hold values from -0.15625 to 0.15625
- w_up: bfloat16 [1536, 4096], P(('frame', 'row')), may hold values from -0.15625 to 0.15625
- w_down: bfloat16 [4096, 1536], P(('frame', 'row')), may hold values from -0.09375 to 0.09375
- w_cap_key: bfloat16 [1536, 1536], P(None, ('frame', 'row')), may hold values from -0.15625 to 0.15625
- w_cap_value: bfloat16 [1536, 1536], P(None, ('frame', 'row')), may hold values from -0.15625 to 0.15625
- w_mod: bfloat16 [1536, 6144], P(None, ('frame', 'row')), may hold values from -0.3125 to 0.3125
- norm_gains: float32 [7, 1536], replicated, may hold values from 0.1 to 1.9
- mix_coefs: float32 [3, 1536], replicated, may hold values from -0.9 to 0.9
- caption: bfloat16 [2, 256, 1536], replicated, may hold values from -6 to 6
- cap_len: int32 [2], replicated, may hold values from 64 to 256, as said below
- cap_mask: int32 [2, 256], replicated, may hold values from 0 to 1, as said below
- timesteps: int32 [2], replicated, may hold values from 0 to 999
- frame_pos: int32 [2, 8], P(None, 'frame'), may hold values from 0 to 63
- row_pos: int32 [8], P('row'), may hold values from 0 to 63
- col_pos: int32 [32], replicated, may hold values from 0 to 63
- grad_out: bfloat16 [2, 8, 8, 32, 1536], P(None, 'frame', 'row'), may hold values from -6 to 6
Outputs:
- output: bfloat16 [2, 8, 8, 32, 1536], P(None, 'frame', 'row')
- grad_tokens: float32 [2, 8, 8, 32, 1536], P(None, 'frame', 'row')
- d_w_query: float32 [1536, 1536], P('row', 'frame')
- d_w_key: float32 [1536, 1536], P('row', 'frame')
- d_w_value: float32 [1536, 1536], P('row', 'frame')
- d_w_out: float32 [1536, 1536], P('row', 'frame')
- d_w_gate: float32 [1536, 4096], P('row', 'frame')
- d_w_up: float32 [1536, 4096], P('row', 'frame')
- d_w_down: float32 [4096, 1536], P('row', 'frame')
- d_w_cap_key: float32 [1536, 1536], P(None, ('frame', 'row'))
- d_w_cap_value: float32 [1536, 1536], P(None, ('frame', 'row'))
- d_w_mod: float32 [1536, 6144], P(None, ('frame', 'row'))
- d_norm_gains: float32 [7, 1536], P(None, ('frame', 'row'))
- d_mix_coefs: float32 [3, 1536], P(None, ('frame', 'row'))
Inputs may be any that keep to these rules, and one draw needn't show every extreme that they name: `cap_len`: every clip has 64 to 256 caption tokens, and some clip has all 256. `cap_mask`: the first caption token of every clip is kept.
All inputs are finite; a program needn't handle non-finite values.
Results may differ from a plain program's by a relative error of at most 0.023.
Values may be sent and summed in bfloat16 or wider, within the bound.
No kernel may reach another device: no remote copies, remote signals or barrier semaphores. Data moves between devices by JAX's collectives and lax.ppermute only.
A program may use at most 704 MiB of HBM per device.

v0:
```python
import math

import jax
import jax.numpy as jnp
from jax import lax
from jax.sharding import PartitionSpec as P

D = 1536
HDIM = 64


EPS = 1e-05
THETA = 10000.0
NEG = -1000000000.0
FLOOR = -1e30


def extended(block, sides, width):
    for axis, dim in sides:
        count = lax.axis_size(axis)
        forward = [(i, i + 1) for i in range(count - 1)]
        backward = [(target, source) for source, target in forward]
        low = lax.ppermute(
            lax.slice_in_dim(block, block.shape[dim] - width, None, axis=dim), axis, forward
        )
        high = lax.ppermute(lax.slice_in_dim(block, 0, width, axis=dim), axis, backward)
        block = jnp.concatenate([low, block, high], axis=dim)
    return block


def rms_norm(tensor, gain):
    return tensor * lax.rsqrt(jnp.mean(tensor * tensor, axis=-1, keepdims=True) + EPS) * gain


def freq_table(size):
    return jnp.exp(-math.log(THETA) * 2.0 * jnp.arange(size // 2, dtype=jnp.float32) / size)


def rotary_tables(pos_frame, pos_row, pos_col, head_dim):
    leading = head_dim // 4
    remain = (head_dim - leading) // 2
    angles = jnp.concatenate(
        [
            pos_frame[..., None] * freq_table(leading),
            pos_row[..., None] * freq_table(remain),
            pos_col[..., None] * freq_table(remain),
        ],
        axis=-1,
    )
    return (jnp.cos(angles), jnp.sin(angles))


def rotate(tensor, cosine, sine_table):
    head_dim = tensor.shape[-1]
    leading = head_dim // 4
    remain = (head_dim - leading) // 2
    bounds = [(0, leading), (leading, leading + remain), (leading + remain, head_dim)]
    lower_half = jnp.concatenate([tensor[..., a : a + (b - a) // 2] for a, b in bounds], axis=-1)
    upper_half = jnp.concatenate([tensor[..., a + (b - a) // 2 : b] for a, b in bounds], axis=-1)
    turned_low = lower_half * cosine - upper_half * sine_table
    turned_high = lower_half * sine_table + upper_half * cosine
    pieces = []
    offset = 0
    for a, b in bounds:
        size_half = (b - a) // 2
        pieces.append(turned_low[..., offset : offset + size_half])
        pieces.append(turned_high[..., offset : offset + size_half])
        offset = offset + size_half
    return jnp.concatenate(pieces, axis=-1)


def split_heads(tensor):
    return tensor.reshape(tensor.shape[0], tensor.shape[1], tensor.shape[2] // HDIM, HDIM)


def score_step(queries4, running, gathered):
    score_scale = HDIM ** (-0.5)
    run_max, run_sum, run_acc = running
    key_rows = split_heads(gathered[0])
    value_rows = split_heads(gathered[1])
    scores = (
        jnp.einsum("cqhd,ckhd->cqhk", queries4, key_rows, preferred_element_type=jnp.float32)
        * score_scale
    )
    new_max = jnp.maximum(run_max, jnp.max(scores, axis=-1))
    weights = jnp.exp(scores - new_max[..., None])
    run_sum = jnp.sum(weights, axis=-1)
    run_acc = jnp.einsum(
        "cqhk,ckhd->cqhd",
        weights.astype(jnp.bfloat16),
        value_rows,
        preferred_element_type=jnp.float32,
    )
    return (new_max, run_sum, run_acc)


def fold_begin(queries4):
    stat_shape = queries4.shape[:3]
    return (
        jnp.full(stat_shape, FLOOR, jnp.float32),
        jnp.zeros(stat_shape, jnp.float32),
        jnp.zeros(queries4.shape, jnp.float32),
    )


def fold_end(running, full_shape):
    run_max, run_sum, run_acc = running
    result = (run_acc / run_sum[..., None]).reshape(full_shape)
    return (result, run_max + jnp.log(run_sum))


def attend_all(queries, key_rows, value_rows):
    queries4 = split_heads(queries)
    running = score_step(
        queries4,
        fold_begin(queries4),
        (
            lax.all_gather(key_rows, ("frame", "row"), axis=1, tiled=True),
            lax.all_gather(value_rows, ("frame", "row"), axis=1, tiled=True),
        ),
    )
    return fold_end(running, queries.shape)


def body(
    tokens,
    w_query,
    w_key,
    w_value,
    w_out,
    w_gate,
    w_up,
    w_down,
    w_cap_key,
    w_cap_value,
    w_mod,
    norm_gains,
    mix_coefs,
    caption,
    cap_len,
    cap_mask,
    timesteps,
    frame_pos,
    row_pos,
    col_pos,
    grad_out,
):
    ftype = jnp.float32
    btype = jnp.bfloat16
    score_scale = HDIM ** (-0.5)
    n_clips, n_frames, n_rows, n_cols, width_all = tokens.shape
    local_len = n_frames * n_rows * n_cols
    half_width = D // 2
    frequencies = jnp.exp(-math.log(THETA) * jnp.arange(half_width, dtype=ftype) / half_width)
    phases = timesteps.astype(ftype)[:, None] * frequencies[None, :]
    step_embed = jax.nn.silu(jnp.concatenate([jnp.cos(phases), jnp.sin(phases)], axis=1)).astype(
        btype
    )
    mod_local = jnp.dot(step_embed, w_mod, preferred_element_type=ftype).astype(btype)
    g_padded = extended(grad_out, (("row", 2),), 1).astype(ftype)
    gathered = (
        lax.all_gather(w_query, ("frame", "row"), axis=0, tiled=True),
        lax.all_gather(w_key, ("frame", "row"), axis=0, tiled=True),
        lax.all_gather(w_value, ("frame", "row"), axis=0, tiled=True),
        lax.all_gather(w_out, ("frame", "row"), axis=0, tiled=True),
        lax.all_gather(w_gate, ("frame", "row"), axis=0, tiled=True),
        lax.all_gather(w_up, ("frame", "row"), axis=0, tiled=True),
        lax.all_gather(w_down, ("frame", "row"), axis=0, tiled=True),
        lax.all_gather(w_cap_key, ("frame", "row"), axis=1, tiled=True),
        lax.all_gather(w_cap_value, ("frame", "row"), axis=1, tiled=True),
        lax.all_gather(mod_local, ("frame", "row"), axis=1, tiled=True),
    )
    wq_full, wk_full, wv_full, wo_full, w1_full, w3_full, w2_full, wkc_full, wvc_full, mod_full = (
        gathered
    )
    modulate = mod_full.astype(ftype)
    scale_a = modulate[:, :D]
    gate_a = modulate[:, D : 2 * D]
    scale_f = modulate[:, 2 * D : 3 * D]
    gate_f = modulate[:, 3 * D :]
    grid_shape = (n_clips, n_frames, n_rows, n_cols)
    pos_frame = jnp.broadcast_to(
        (frame_pos + cap_len[:, None]).astype(ftype)[:, :, None, None], grid_shape
    ).reshape(n_clips, local_len)
    pos_row = jnp.broadcast_to(row_pos.astype(ftype)[None, None, :, None], grid_shape).reshape(
        n_clips, local_len
    )
    pos_col = jnp.broadcast_to(col_pos.astype(ftype)[None, None, None, :], grid_shape).reshape(
        n_clips, local_len
    )
    cosine, sine_table = rotary_tables(pos_frame, pos_row, pos_col, HDIM)
    cosine = cosine[:, :, None, :]
    sine_table = sine_table[:, :, None, :]
    usable = (jnp.arange(caption.shape[1])[None, :] < cap_len[:, None]) & (cap_mask > 0)
    x_flat = tokens.reshape(n_clips, local_len, D).astype(ftype)

    def pre_piece(x_in, gain, scale_in):
        return rms_norm(x_in, gain) * (1.0 + scale_in[:, None, :])

    h_in32, pre_back = jax.vjp(pre_piece, x_flat, norm_gains[0], scale_a)
    h_in = h_in32.astype(btype)
    q_zero = jnp.dot(h_in, wq_full, preferred_element_type=ftype)
    k_zero = jnp.dot(h_in, wk_full, preferred_element_type=ftype)
    values_self = jnp.dot(h_in, wv_full, preferred_element_type=ftype).astype(btype)

    def rotary_piece(q_in, k_in, q_gain, k_gain):
        q_norm = rms_norm(q_in, q_gain)
        k_norm = rms_norm(k_in, k_gain)
        q_rot = rotate(split_heads(q_norm), cosine, sine_table).reshape(q_in.shape)
        k_rot = rotate(split_heads(k_norm), cosine, sine_table).reshape(k_in.shape)
        return (q_rot, q_norm, k_rot)

    (q_rot32, q_norm32, k_rot32), rotary_back = jax.vjp(
        rotary_piece, q_zero, k_zero, norm_gains[4], norm_gains[5]
    )
    queries_rot = q_rot32.astype(btype)
    queries_cap = q_norm32.astype(btype)
    keys_rot = k_rot32.astype(btype)
    cap_key_pre = jnp.dot(caption, wkc_full, preferred_element_type=ftype)
    cap_key32, cap_back = jax.vjp(rms_norm, cap_key_pre, norm_gains[6])
    cap_keys = split_heads(cap_key32.astype(btype))
    cap_values = split_heads(jnp.dot(caption, wvc_full, preferred_element_type=ftype).astype(btype))
    out_self, log_sum = attend_all(queries_rot, keys_rot, values_self)
    cap_queries4 = split_heads(queries_cap)
    cross_scores = (
        jnp.einsum("cqhd,ckhd->cqhk", cap_queries4, cap_keys, preferred_element_type=ftype)
        * score_scale
    )
    cross_scores = jnp.where(usable[:, None, None, :], cross_scores, NEG)
    cross_probs = jax.nn.softmax(cross_scores, axis=-1)
    cross_low = cross_probs.astype(btype)
    out_cross = jnp.einsum(
        "cqhk,ckhd->cqhd", cross_low, cap_values, preferred_element_type=ftype
    ).reshape(n_clips, local_len, D)

    def mix_piece(self_in, cross_in, gate_in):
        return self_in + jnp.tanh(gate_in) * cross_in

    attn32, mix_back = jax.vjp(mix_piece, out_self, out_cross, mix_coefs[0])
    attn_mix = attn32.astype(btype)
    y_one = jnp.dot(attn_mix, wo_full, preferred_element_type=ftype)

    def mid_piece(x_in, y_in, gain_two, gate_in, gain_three, scale_in):
        h_mid = x_in + jnp.tanh(gate_in)[:, None, :] * rms_norm(y_in, gain_two)
        return (h_mid, rms_norm(h_mid, gain_three) * (1.0 + scale_in[:, None, :]))

    (h_mid, f_in32), mid_back = jax.vjp(
        mid_piece, x_flat, y_one, norm_gains[1], gate_a, norm_gains[2], scale_f
    )
    f_in = f_in32.astype(btype)
    gate_pre = jnp.dot(f_in, w1_full, preferred_element_type=ftype)
    up_proj = jnp.dot(f_in, w3_full, preferred_element_type=ftype)

    def act_piece(gate_in, up_in):
        return jax.nn.silu(gate_in) * up_in

    hidden32, act_back = jax.vjp(act_piece, gate_pre, up_proj)
    hidden = hidden32.astype(btype)
    z_out = jnp.dot(hidden, w2_full, preferred_element_type=ftype)

    def end_piece(h_in_mid, z_in, gain_four, gate_in):
        return h_in_mid + jnp.tanh(gate_in)[:, None, :] * rms_norm(z_in, gain_four)

    y_all, end_back = jax.vjp(end_piece, h_mid, z_out, norm_gains[3], gate_f)
    y_grid = y_all.reshape(tokens.shape)
    y_padded = extended(y_grid.astype(jnp.bfloat16), (("row", 2),), 1).astype(y_grid.dtype)
    above = y_padded[:, :, :-2]
    below = y_padded[:, :, 2:]
    output = (y_grid + mix_coefs[1] * above + mix_coefs[2] * below).astype(btype)
    g_center = g_padded[:, :, 1:-1]
    d_y = g_center + mix_coefs[1] * g_padded[:, :, 2:] + mix_coefs[2] * g_padded[:, :, :-2]
    d_above = jnp.sum(g_center * above, axis=(0, 1, 2, 3))
    d_below = jnp.sum(g_center * below, axis=(0, 1, 2, 3))
    d_h_end, d_z, d_g_four, d_gate_f = end_back(d_y.reshape(n_clips, local_len, D))
    d_z_low = d_z.astype(btype)
    d_hidden = jnp.einsum("csd,fd->csf", d_z_low, w2_full, preferred_element_type=ftype)
    d_gate, d_up = act_back(d_hidden)
    d_gate_low = d_gate.astype(btype)
    d_up_low = d_up.astype(btype)
    d_f_in = jnp.einsum(
        "csf,df->csd", d_gate_low, w1_full, preferred_element_type=ftype
    ) + jnp.einsum("csf,df->csd", d_up_low, w3_full, preferred_element_type=ftype)
    d_x_mid, d_y_one, d_g_two, d_gate_a, d_g_three, d_scale_f = mid_back((d_h_end, d_f_in))
    d_y_low = d_y_one.astype(btype)
    d_attn = jnp.einsum("cse,de->csd", d_y_low, wo_full, preferred_element_type=ftype)
    d_self, d_cross, d_cross_gate = mix_back(d_attn)
    d_self_low = d_self.astype(btype)
    d_cross_low = d_cross.astype(btype)
    delta = jnp.sum(split_heads(d_self_low.astype(ftype) * out_self), axis=-1)
    queries4 = split_heads(queries_rot)
    d_out4 = split_heads(d_self_low)
    gathered = (
        lax.all_gather(keys_rot, ("frame", "row"), axis=1, tiled=True),
        lax.all_gather(values_self, ("frame", "row"), axis=1, tiled=True),
    )
    key_rows = split_heads(gathered[0])
    value_rows = split_heads(gathered[1])
    scores = (
        jnp.einsum("cqhd,ckhd->cqhk", queries4, key_rows, preferred_element_type=ftype)
        * score_scale
    )
    probs = jnp.exp(scores - log_sum[..., None])
    d_probs = jnp.einsum("cqhd,ckhd->cqhk", d_out4, value_rows, preferred_element_type=ftype)
    d_scores = (probs * (d_probs - delta[..., None])).astype(btype)
    d_q_self = score_scale * jnp.einsum(
        "cqhk,ckhd->cqhd", d_scores, key_rows, preferred_element_type=ftype
    )
    d_q_self = d_q_self.reshape(n_clips, local_len, D)
    lse_all, delta_all = (
        lax.all_gather(log_sum, ("frame", "row"), axis=1, tiled=True),
        lax.all_gather(delta, ("frame", "row"), axis=1, tiled=True),
    )
    keys4 = split_heads(keys_rot)
    values4 = split_heads(values_self)
    gathered = (
        lax.all_gather(queries_rot, ("frame", "row"), axis=1, tiled=True),
        lax.all_gather(d_self_low, ("frame", "row"), axis=1, tiled=True),
    )
    query_rows = split_heads(gathered[0])
    d_out_rows = split_heads(gathered[1])
    scores = (
        jnp.einsum("cqhd,ckhd->cqhk", query_rows, keys4, preferred_element_type=ftype) * score_scale
    )
    probs = jnp.exp(scores - lse_all[..., None])
    acc_values = jnp.einsum(
        "cqhk,cqhd->ckhd", probs.astype(btype), d_out_rows, preferred_element_type=ftype
    )
    d_probs = jnp.einsum("cqhd,ckhd->cqhk", d_out_rows, values4, preferred_element_type=ftype)
    d_scores = (probs * (d_probs - delta_all[..., None])).astype(btype)
    acc_keys = score_scale * jnp.einsum(
        "cqhk,cqhd->ckhd", d_scores, query_rows, preferred_element_type=ftype
    )
    d_cross4 = split_heads(d_cross_low)
    d_cross_probs = jnp.einsum(
        "cqhd,ckhd->cqhk", d_cross4, cap_values, preferred_element_type=ftype
    )
    d_cross_scores = (
        cross_probs * (d_cross_probs - jnp.sum(cross_probs * d_cross_probs, axis=-1, keepdims=True))
    ).astype(btype)
    d_q_cross = score_scale * jnp.einsum(
        "cqhk,ckhd->cqhd", d_cross_scores, cap_keys, preferred_element_type=ftype
    )
    d_cap_keys = score_scale * jnp.einsum(
        "cqhk,cqhd->ckhd", d_cross_scores, cap_queries4, preferred_element_type=ftype
    )
    d_cap_values = jnp.einsum("cqhk,cqhd->ckhd", cross_low, d_cross4, preferred_element_type=ftype)
    d_cap_pre, d_g_cap = cap_back(d_cap_keys.reshape(cap_key_pre.shape))
    d_q_zero, d_k_zero, d_g_query, d_g_key = rotary_back(
        (
            d_q_self,
            d_q_cross.reshape(n_clips, local_len, D),
            acc_keys.reshape(n_clips, local_len, D),
        )
    )
    d_q_low = d_q_zero.astype(btype)
    d_k_low = d_k_zero.astype(btype)
    d_v_low = acc_values.reshape(n_clips, local_len, D).astype(btype)
    d_h_in = (
        jnp.einsum("cse,de->csd", d_q_low, wq_full, preferred_element_type=ftype)
        + jnp.einsum("cse,de->csd", d_k_low, wk_full, preferred_element_type=ftype)
        + jnp.einsum("cse,de->csd", d_v_low, wv_full, preferred_element_type=ftype)
    )
    d_x_pre, d_g_zero, d_scale_a = pre_back(d_h_in)
    grad_tokens = (d_x_pre + d_x_mid).reshape(tokens.shape)
    acts = (
        lax.all_gather(hidden, "frame", axis=1, tiled=True),
        lax.all_gather(f_in, "frame", axis=1, tiled=True),
        lax.all_gather(attn_mix, "frame", axis=1, tiled=True),
        lax.all_gather(h_in, "frame", axis=1, tiled=True),
    )
    hid_group, fin_group, attn_group, hin_group = acts
    grads_ex = (
        lax.all_to_all(d_z_low, "frame", split_axis=2, concat_axis=1, tiled=True),
        lax.all_to_all(d_y_low, "frame", split_axis=2, concat_axis=1, tiled=True),
        lax.all_to_all(d_q_low, "frame", split_axis=2, concat_axis=1, tiled=True),
        lax.all_to_all(d_k_low, "frame", split_axis=2, concat_axis=1, tiled=True),
        lax.all_to_all(d_v_low, "frame", split_axis=2, concat_axis=1, tiled=True),
        lax.all_to_all(d_gate_low, "frame", split_axis=2, concat_axis=1, tiled=True),
        lax.all_to_all(d_up_low, "frame", split_axis=2, concat_axis=1, tiled=True),
    )
    dz_part, dy_part, dq_part, dk_part, dv_part, dgate_part, dup_part = grads_ex
    term_query = jnp.einsum("csd,cse->de", hin_group, dq_part, preferred_element_type=ftype)
    term_key = jnp.einsum("csd,cse->de", hin_group, dk_part, preferred_element_type=ftype)
    term_value = jnp.einsum("csd,cse->de", hin_group, dv_part, preferred_element_type=ftype)
    term_out = jnp.einsum("csd,cse->de", attn_group, dy_part, preferred_element_type=ftype)
    term_gate = jnp.einsum("csd,csf->df", fin_group, dgate_part, preferred_element_type=ftype)
    term_up = jnp.einsum("csd,csf->df", fin_group, dup_part, preferred_element_type=ftype)
    term_down = jnp.einsum("csf,csd->fd", hid_group, dz_part, preferred_element_type=ftype)
    weight_sums = (
        lax.psum_scatter(
            term_query.astype(jnp.bfloat16), "row", scatter_dimension=0, tiled=True
        ).astype(jnp.float32),
        lax.psum_scatter(
            term_key.astype(jnp.bfloat16), "row", scatter_dimension=0, tiled=True
        ).astype(jnp.float32),
        lax.psum_scatter(
            term_value.astype(jnp.bfloat16), "row", scatter_dimension=0, tiled=True
        ).astype(jnp.float32),
        lax.psum_scatter(
            term_out.astype(jnp.bfloat16), "row", scatter_dimension=0, tiled=True
        ).astype(jnp.float32),
        lax.psum_scatter(
            term_gate.astype(jnp.bfloat16), "row", scatter_dimension=0, tiled=True
        ).astype(jnp.float32),
        lax.psum_scatter(
            term_up.astype(jnp.bfloat16), "row", scatter_dimension=0, tiled=True
        ).astype(jnp.float32),
        lax.psum_scatter(
            term_down.astype(jnp.bfloat16), "row", scatter_dimension=0, tiled=True
        ).astype(jnp.float32),
    )
    d_modulate = jnp.concatenate([d_scale_a, d_gate_a, d_scale_f, d_gate_f], axis=1)
    d_gains = jnp.stack(
        [d_g_zero, d_g_two, d_g_three, d_g_four, d_g_query, d_g_key, d_g_cap], axis=0
    )
    d_mixes = jnp.stack([d_cross_gate, d_above, d_below], axis=0)
    side_sums = (
        lax.psum_scatter(d_cap_pre, ("frame", "row"), scatter_dimension=2, tiled=True),
        lax.psum_scatter(
            d_cap_values.reshape(cap_key_pre.shape),
            ("frame", "row"),
            scatter_dimension=2,
            tiled=True,
        ),
        lax.psum_scatter(d_modulate, ("frame", "row"), scatter_dimension=1, tiled=True),
        lax.psum_scatter(d_gains, ("frame", "row"), scatter_dimension=1, tiled=True),
        lax.psum_scatter(d_mixes, ("frame", "row"), scatter_dimension=1, tiled=True),
    )
    d_w_cap_key = jnp.einsum(
        "cjd,cje->de", caption, side_sums[0].astype(btype), preferred_element_type=ftype
    )
    d_w_cap_value = jnp.einsum(
        "cjd,cje->de", caption, side_sums[1].astype(btype), preferred_element_type=ftype
    )
    d_w_mod = jnp.dot(step_embed.T, side_sums[2].astype(btype), preferred_element_type=ftype)
    return (
        output,
        grad_tokens,
        weight_sums[0],
        weight_sums[1],
        weight_sums[2],
        weight_sums[3],
        weight_sums[4],
        weight_sums[5],
        weight_sums[6],
        d_w_cap_key,
        d_w_cap_value,
        d_w_mod,
        side_sums[3],
        side_sums[4],
    )


def solution(mesh):
    placed = (
        P(None, "frame", "row", None, None),
        P(("frame", "row"), None),
        P(("frame", "row"), None),
        P(("frame", "row"), None),
        P(("frame", "row"), None),
        P(("frame", "row"), None),
        P(("frame", "row"), None),
        P(("frame", "row"), None),
        P(None, ("frame", "row")),
        P(None, ("frame", "row")),
        P(None, ("frame", "row")),
        P(),
        P(),
        P(),
        P(),
        P(),
        P(),
        P(None, "frame"),
        P("row"),
        P(),
        P(None, "frame", "row", None, None),
    )
    return jax.shard_map(
        body,
        mesh=mesh,
        in_specs=placed,
        out_specs=(
            P(None, "frame", "row", None, None),
            P(None, "frame", "row", None, None),
            P("row", "frame"),
            P("row", "frame"),
            P("row", "frame"),
            P("row", "frame"),
            P("row", "frame"),
            P("row", "frame"),
            P("row", "frame"),
            P(None, ("frame", "row")),
            P(None, ("frame", "row")),
            P(None, ("frame", "row")),
            P(None, ("frame", "row")),
            P(None, ("frame", "row")),
        ),
        check_vma=False,
    )
```

profile of v0, /device:TPU:2, one launch (start us, length us, event | category | flops | bytes accessed | tf_op | source)
XLA Modules:
  0.0 2160.3 jit_solution(3739392188052779993)
XLA Ops:
  12.8 64.3 %all-gather = bf16[32,192,2]{1,2,0:T(2,128)(2,1)S(1)} all-gather(bf16[1,192,2]{1,2,0:T(2,128)(2,1)S(1)} %fusion.103), channel_id=1, replica_groups=mesh['frame'=4,'row'=8] {'frame','row'}, dimensions={0}, use_global_device_ids=true | all-gather | bytes 25344 | tf_op jit(solution)/shard_map/all_gather | solution.py:171
  85.6 56.1 %all-gather.23.cloned.1.call-done = bf16[1536,1536]{1,0:T(8,128)(2,1)} async-done(((bf16[48,1536]{1,0:T(8,128)(2,1)}), bf16[1536,1536]{1,0:T(8,128)(2,1)}) %all-gather.23.cloned.1.call-update) | async-done | bytes 4718608 | tf_op jit(solution)/shard_map/all_gather | solution.py:163
  170.7 36.5 %all-gather.27.cloned.1.call-done = bf16[1536,1536]{1,0:T(8,128)(2,1)} async-done(((bf16[48,1536]{1,0:T(8,128)(2,1)}), bf16[1536,1536]{1,0:T(8,128)(2,1)}) %all-gather.27.cloned.1.call-update) | async-done | bytes 4718608 | tf_op jit(solution)/shard_map/all_gather | solution.py:162
  224.2 48.4 %all-gather.29.cloned.1.call-done = bf16[1536,1536]{0,1:T(8,128)(2,1)} async-done(((bf16[1536,48]{0,1:T(8,128)(2,1)}), bf16[1536,1536]{0,1:T(8,128)(2,1)}) %all-gather.29.cloned.1.call-update) | async-done | bytes 4718608 | tf_op jit(solution)/shard_map/all_gather | solution.py:170
  281.3 56.6 %all-gather.31.cloned.1.call-done = bf16[1536,1536]{0,1:T(8,128)(2,1)} async-done(((bf16[1536,48]{0,1:T(8,128)(2,1)}), bf16[1536,1536]{0,1:T(8,128)(2,1)}) %all-gather.31.cloned.1.call-update) | async-done | bytes 4718608 | tf_op jit(solution)/shard_map/all_gather | solution.py:169
  371.7 63.8 %all-gather.21.cloned.1.call-done = bf16[2,2048,1536]{2,1,0:T(8,128)(2,1)} async-done(((bf16[2,64,1536]{2,1,0:T(8,128)(2,1)}), bf16[2,2048,1536]{2,1,0:T(8,128)(2,1)}) %all-gather.21.cloned.1.call-update) | async-done | bytes 12582928 | tf_op jit(solution)/shard_map/all_gather | solution.py:119
  435.5 16.8 copy.256
  452.3 80.4 %all-gather.25.cloned.1.call-done = bf16[2,2048,1536]{2,1,0:T(8,128)(2,1)} async-done(((bf16[2,64,1536]{2,1,0:T(8,128)(2,1)}), bf16[2,2048,1536]{2,1,0:T(8,128)(2,1)}) %all-gather.25.cloned.1.call-update) | async-done | bytes 12582928 | tf_op jit(solution)/shard_map/all_gather | solution.py:118
  532.6 16.6 copy.264
  549.2 16.5 bitcast_reduce_fusion
  576.6 16.2 bitcast_divide_fusion
  613.1 88.0 %all-gather.35.cloned.1.call-done = bf16[1536,4096]{1,0:T(8,128)(2,1)} async-done(((bf16[48,4096]{1,0:T(8,128)(2,1)}), bf16[1536,4096]{1,0:T(8,128)(2,1)}) %all-gather.35.cloned.1.call-update) | async-done | bytes 12582928 | tf_op jit(solution)/shard_map/all_gather | solution.py:166
  708.8 89.4 %all-gather.37.cloned.1.call-done = bf16[1536,4096]{1,0:T(8,128)(2,1)} async-done(((bf16[48,4096]{1,0:T(8,128)(2,1)}), bf16[1536,4096]{1,0:T(8,128)(2,1)}) %all-gather.37.cloned.1.call-update) | async-done | bytes 12582928 | tf_op jit(solution)/shard_map/all_gather | solution.py:167
  807.2 88.2 %all-gather.39.cloned.1.call-done = bf16[4096,1536]{1,0:T(8,128)(2,1)} async-done(((bf16[128,1536]{1,0:T(8,128)(2,1)}), bf16[4096,1536]{1,0:T(8,128)(2,1)}) %all-gather.39.cloned.1.call-update) | async-done | bytes 12582928 | tf_op jit(solution)/shard_map/all_gather | solution.py:168
  1007.5 21.6 all_to_all.127
  1047.0 16.0 copy.286
  1075.6 16.7 fusion.165
  1093.0 99.8 %all_gather.75 = f32[2,2048,24]{2,0,1:T(2,128)} all-gather(f32[2,64,24]{2,0,1:T(2,128)S(1)} %copy.287), channel_id=1, replica_groups=mesh['frame'=4,'row'=8] {'frame','row'}, dimensions={1}, use_global_device_ids=true | all-gather | bytes 405504 | tf_op jit(solution)/shard_map/all_gather | solution.py:310
  1215.1 19.5 multiply_bitcast_fusion.1
  1270.3 83.8 %all_gather.77 = f32[2,2048,24]{2,0,1:T(2,128)} all-gather(f32[2,64,24]{2,0,1:T(2,128)S(1)} %copy-done.48), channel_id=1, replica_groups=mesh['frame'=4,'row'=8] {'frame','row'}, dimensions={1}, use_global_device_ids=true | all-gather | bytes 405504 | tf_op jit(solution)/shard_map/all_gather | solution.py:311
  1375.4 15.8 copy.289
  1391.2 20.0 multiply_bitcast_fusion
  1444.3 14.4 fusion.96
  1480.2 11.8 all_to_all.128
  1526.3 96.1 %all-reduce.24 = bf16[2,256,1536]{1,0,2:T(2,128)(2,1)} all-reduce(f32[2,256,1536]{1,0,2:T(2,128)} %copy.312), channel_id=9, replica_groups=mesh['frame'=4,'row'=8] {'frame','row'}, use_global_device_ids=true, to_apply=%region_27.28.clone | all-reduce | flops 786432 | bytes 4718592
  1631.5 38.3 %reduce-scatter.28.cloned.1.call-done = bf16[192,1024]{1,0:T(8,128)(2,1)} async-done(((bf16[1536,1024]{1,0:T(8,128)(2,1)}), bf16[192,1024]{1,0:T(8,128)(2,1)}) %reduce-scatter.28.cloned.1.call-update) | async-done | bytes 393232 | tf_op jit(solution)/shard_map/reduce_scatter | solution.py:405
  1671.7 75.2 %reduce-scatter.30.cloned.1.call-done = bf16[512,384]{1,0:T(8,128)(2,1)} async-done(((bf16[4096,384]{1,0:T(8,128)(2,1)}), bf16[512,384]{1,0:T(8,128)(2,1)}) %reduce-scatter.30.cloned.1.call-update) | async-done | bytes 393232 | tf_op jit(solution)/shard_map/reduce_scatter | solution.py:408
  1751.3 95.3 %reduce-scatter.36.cloned.1.call-done = f32[48,7]{1,0:T(8,128)} async-done(((f32[1536,7]{1,0:T(8,128)}), f32[48,7]{1,0:T(8,128)}) %reduce-scatter.36.cloned.1.call-update) | async-done | bytes 1360
  1848.0 104.6 %reduce-scatter.34.cloned.1.call-done = f32[192,2]{1,0:T(8,128)} async-done(((f32[6144,2]{1,0:T(8,128)}), f32[192,2]{1,0:T(8,128)}) %reduce-scatter.34.cloned.1.call-update) | async-done | bytes 1552
  1955.7 62.9 %reduce-scatter.18.cloned.1.call-done = bf16[192,384]{1,0:T(8,128)(2,1)} async-done(((bf16[1536,384]{1,0:T(8,128)(2,1)}), bf16[192,384]{1,0:T(8,128)(2,1)}) %reduce-scatter.18.cloned.1.call-update) | async-done | bytes 147472 | tf_op jit(solution)/shard_map/reduce_scatter | solution.py:390
  2020.2 64.7 %reduce-scatter.20.cloned.1.call-done = bf16[192,384]{1,0:T(8,128)(2,1)} async-done(((bf16[1536,384]{1,0:T(8,128)(2,1)}), bf16[192,384]{1,0:T(8,128)(2,1)}) %reduce-scatter.20.cloned.1.call-update) | async-done | bytes 147472 | tf_op jit(solution)/shard_map/reduce_scatter | solution.py:393
  2086.6 64.8 %reduce-scatter.22.cloned.1.call-done = bf16[192,384]{1,0:T(8,128)(2,1)} async-done(((bf16[1536,384]{1,0:T(8,128)(2,1)}), bf16[192,384]{1,0:T(8,128)(2,1)}) %reduce-scatter.22.cloned.1.call-update) | async-done | bytes 147472 | tf_op jit(solution)/shard_map/reduce_scatter | solution.py:396
  (572 shorter events, 483.7 us)
Async XLA Ops:
  7.2 72.0 %all-gather.19.cloned.1.call-start = ((), (), s32[]{:S(2)}) async-start(), calls=%async_computation.18 | async-start | bytes 4866048 | tf_op jit(solution)/shard_map/all_gather | solution.py:164
  8.0 133.7 %all-gather.23.cloned.1.call-start = ((), (), s32[]{:S(2)}) async-start(), calls=%async_computation.20 | async-start | bytes 4866048 | tf_op jit(solution)/shard_map/all_gather | solution.py:163
  8.7 198.5 %all-gather.27.cloned.1.call-start = ((), (), s32[]{:S(2)}) async-start(), calls=%async_computation.22 | async-start | bytes 4866048 | tf_op jit(solution)/shard_map/all_gather | solution.py:162
  9.4 263.1 %all-gather.29.cloned.1.call-start = ((), (), s32[]{:S(2)}) async-start(), calls=%async_computation.23 | async-start | bytes 4866048 | tf_op jit(solution)/shard_map/all_gather | solution.py:170
  10.0 327.9 %all-gather.31.cloned.1.call-start = ((), (), s32[]{:S(2)}) async-start(), calls=%async_computation.24 | async-start | bytes 4866048 | tf_op jit(solution)/shard_map/all_gather | solution.py:169
  10.6 424.9 %all-gather.21.cloned.1.call-start = ((), (), s32[]{:S(2)}) async-start(), calls=%async_computation.19 | async-start | bytes 12976128 | tf_op jit(solution)/shard_map/all_gather | solution.py:119
  83.3 449.4 %all-gather.25.cloned.1.call-start = ((), (), s32[]{:S(2)}) async-start(), calls=%async_computation.21 | async-start | bytes 12976128 | tf_op jit(solution)/shard_map/all_gather | solution.py:118
  166.3 431.2 %all-gather.33.cloned.1.call-start = ((), (), s32[]{:S(2)}) async-start(), calls=%async_computation.25 | async-start | bytes 4866048 | tf_op jit(solution)/shard_map/all_gather | solution.py:165
  167.1 534.0 %all-gather.35.cloned.1.call-start = ((), (), s32[]{:S(2)}) async-start(), calls=%async_computation.26 | async-start | bytes 12976128 | tf_op jit(solution)/shard_map/all_gather | solution.py:166
  167.8 630.4 %all-gather.37.cloned.1.call-start = ((), (), s32[]{:S(2)}) async-start(), calls=%async_computation.27 | async-start | bytes 12976128 | tf_op jit(solution)/shard_map/all_gather | solution.py:167
  168.4 727.0 %all-gather.39.cloned.1.call-start = ((), (), s32[]{:S(2)}) async-start(), calls=%async_computation.28 | async-start | bytes 12976128 | tf_op jit(solution)/shard_map/all_gather | solution.py:168
  169.1 824.3 %all-gather.47.cloned.1.call-start = ((), (), s32[]{:S(2)}) async-start(), calls=%async_computation.35 | async-start | bytes 1966080 | tf_op jit(solution)/shard_map/all_gather | solution.py:368
  596.4 442.9 %all-gather.49.cloned.1.call-start = ((), (), s32[]{:S(2)}) async-start(), calls=%async_computation.37 | async-start | bytes 1966080 | tf_op jit(solution)/shard_map/all_gather | solution.py:367
  603.3 443.7 %all-gather.41.cloned.1.call-start = ((), (), s32[]{:S(2)}) async-start(), calls=%async_computation.29 | async-start | bytes 12976128 | tf_op jit(solution)/shard_map/all_gather | solution.py:316
  606.3 762.8 %all-gather.51.cloned.1.call-start = ((), (), s32[]{:S(2)}) async-start(), calls=%async_computation.40 | async-start | bytes 5242880 | tf_op jit(solution)/shard_map/all_gather | solution.py:366
  606.3 304.4 %collective-permute-start.3 = (bf16[2,2,1,32,1536]{4,3,2,1,0:T(8,128)(2,1)}, bf16[2,2,1,32,1536]{4,3,2,1,0:T(8,128)(2,1)}, u32[]{:S(2)}, u32[]{:S(2)}) collective-permute-start(bf16[2,2,1,32,1536]{4,3,2,1,0:T(8,128)(2,1)} %param.41), channel_id=1, source_target_pairs={{1,0},{2,1},{3,2},{4,3},{5,4},{6,5},{7,6},{9,8},{10,9},{11,10},{12... | collective-permute-start | bytes 1179656 | tf_op jit(solution)/shard_map/ppermute | solution.py:26
  608.8 301.9 %collective-permute-start.2 = (bf16[2,2,1,32,1536]{4,3,2,1,0:T(8,128)(2,1)}, bf16[2,2,1,32,1536]{4,3,2,1,0:T(8,128)(2,1)}, u32[]{:S(2)}, u32[]{:S(2)}) collective-permute-start(bf16[2,2,1,32,1536]{4,3,2,1,0:T(8,128)(2,1)} %param.41), channel_id=1, source_target_pairs={{0,1},{1,2},{2,3},{3,4},{4,5},{5,6},{6,7},{8,9},{9,10},{10,11},{11... | collective-permute-start | bytes 1179656 | tf_op jit(solution)/shard_map/ppermute | solution.py:23
  913.5 462.0 %all-gather.43.cloned.1.call-start = ((), (), s32[]{:S(2)}) async-start(), calls=%async_computation.30 | async-start | bytes 12976128 | tf_op jit(solution)/shard_map/all_gather | solution.py:317
  967.7 505.5 %all-gather.45.cloned.1.call-start = ((), (), s32[]{:S(2)}) async-start(), calls=%async_computation.31 | async-start | bytes 1966080 | tf_op jit(solution)/shard_map/all_gather | solution.py:369
  968.3 656.1 %reduce-scatter.38.cloned.1.call-start = ((), (), s32[]{:S(2)}) async-start(), calls=%async_computation.45 | async-start | bytes 811008
  971.5 654.2 %reduce-scatter.32.cloned.1.call-start = ((), (), s32[]{:S(2)}) async-start(), calls=%async_computation.42 | async-start | bytes 3244032 | tf_op jit(solution)/shard_map/reduce_scatter | solution.py:419
  976.1 651.6 %reduce-scatter.24.cloned.1.call-start = ((), (), s32[]{:S(2)}) async-start(), calls=%async_computation.36 | async-start | bytes 1327104 | tf_op jit(solution)/shard_map/reduce_scatter | solution.py:399
  997.5 631.9 %reduce-scatter.26.cloned.1.call-start = ((), (), s32[]{:S(2)}) async-start(), calls=%async_computation.38 | async-start | bytes 3538944 | tf_op jit(solution)/shard_map/reduce_scatter | solution.py:402
  1071.2 130.0 %all-to-all-start.5 = ((bf16[4,2,65536]{2,1,0:T(2,128)(2,1)}), bf16[4,2,65536]{2,1,0:T(2,128)(2,1)}, u32[]{:S(2)}, u32[]{:S(2)}) async-start(bf16[4,2,65536]{2,1,0:T(2,128)(2,1)} %reshape.458), calls=%async_computation.10 | async-start | bytes 2097152 | tf_op jit(solution)/shard_map/all_to_all | solution.py:379
  1075.6 594.2 %reduce-scatter.28.cloned.1.call-start = ((), (), s32[]{:S(2)}) async-start(), calls=%async_computation.39 | async-start | bytes 3538944 | tf_op jit(solution)/shard_map/reduce_scatter | solution.py:405
  1259.2 107.7 %all-to-all-start.6 = ((bf16[4,2,24576]{2,1,0:T(2,128)(2,1)}), bf16[4,2,24576]{2,1,0:T(2,128)(2,1)}, u32[]{:S(2)}, u32[]{:S(2)}) async-start(bf16[4,2,24576]{2,1,0:T(2,128)(2,1)} %reshape.460), calls=%async_computation.12 | async-start | bytes 786432 | tf_op jit(solution)/shard_map/all_to_all | solution.py:373
  1263.3 483.6 %reduce-scatter.30.cloned.1.call-start = ((), (), s32[]{:S(2)}) async-start(), calls=%async_computation.41 | async-start | bytes 3538944 | tf_op jit(solution)/shard_map/reduce_scatter | solution.py:408
  1435.4 411.3 %reduce-scatter.36.cloned.1.call-start = ((), (), s32[]{:S(2)}) async-start(), calls=%async_computation.44 | async-start | bytes 811008
  1466.0 486.6 %reduce-scatter.34.cloned.1.call-start = ((), (), s32[]{:S(2)}) async-start(), calls=%async_computation.43 | async-start | bytes 3244032
  1468.4 550.2 %reduce-scatter.18.cloned.1.call-start = ((), (), s32[]{:S(2)}) async-start(), calls=%async_computation.32 | async-start | bytes 1327104 | tf_op jit(solution)/shard_map/reduce_scatter | solution.py:390
  1476.7 608.3 %reduce-scatter.20.cloned.1.call-start = ((), (), s32[]{:S(2)}) async-start(), calls=%async_computation.33 | async-start | bytes 1327104 | tf_op jit(solution)/shard_map/reduce_scatter | solution.py:393
  1510.7 640.6 %reduce-scatter.22.cloned.1.call-start = ((), (), s32[]{:S(2)}) async-start(), calls=%async_computation.34 | async-start | bytes 1327104 | tf_op jit(solution)/shard_map/reduce_scatter | solution.py:396
  (138 other events, 2116.8 us)
Sparse Core Ops, SparseCore 0:
  11.0 64.9 all-gather.18
  79.0 62.5 all-gather.22
  144.6 62.4 all-gather.26
  210.0 62.4 all-gather.28
  275.4 62.4 all-gather.30
  340.6 94.8 all-gather.20
  438.3 94.2 all-gather.24
  535.6 61.9 all-gather.32
  600.5 100.5 all-gather.34
  703.9 94.2 all-gather.36
  801.2 94.2 all-gather.38
  896.9 17.9 all-gather.46
  916.4 19.6 all-gather.48
  938.8 98.5 all-gather.40
  1038.8 37.8 all-gather.50
  1079.5 123.1 all-gather.42
  1204.1 21.0 all-gather.44
  1230.1 96.8 reduce-scatter.37
  1332.4 100.8 reduce-scatter.31
  1437.1 62.7 reduce-scatter.23
  1503.5 85.7 reduce-scatter.25
  1592.9 76.8 reduce-scatter.27
  1673.4 73.4 reduce-scatter.29
  1751.8 94.7 reduce-scatter.35
  1852.0 100.5 reduce-scatter.33
  1955.9 62.6 reduce-scatter.17
  2021.8 63.0 reduce-scatter.19
  2088.3 62.9 reduce-scatter.21
where the time goes:
time: 2180 us; the launch traced here: 2160 us
  waiting for transfers between devices  1130 us (52%)
  blocking collectives  388 us (18%)
  local copies, waits for them, and re-layouts  258 us (12%)
  matrix products  254 us (12%)
  other arithmetic  77.5 us (4%)
  starting transfers between devices  31.6 us (1%)
    unnamed x31, waiting for transfers between devices  206 us
    all_gather x1, blocking collectives, body(): lax.all_gather(log_sum, ('frame', 'row'), axis=1, tiled=True)  99.8 us
    unnamed x1, blocking collectives  96.1 us
    all_gather x1, waiting for transfers between devices, body(): lax.all_gather(w_up, ('frame', 'row'), axis=0, tiled=True)  89.4 us
    all_gather x1, waiting for transfers between devices, body(): lax.all_gather(w_down, ('frame', 'row'), axis=0, tiled=True)  88.2 us
    all_gather x1, waiting for transfers between devices, body(): lax.all_gather(w_gate, ('frame', 'row'), axis=0, tiled=True)  88 us
    all_gather x1, blocking collectives, body(): lax.all_gather(delta, ('frame', 'row'), axis=1, tiled=True)  83.8 us
    all_gather x1, waiting for transfers between devices, attend_all(): lax.all_gather(key_rows, ('frame', 'row'), axis=1, tiled=True)  80.4 us
  transfers between devices with their start and end apart: 36, of which 19 were waited for; matrix products, arithmetic and copies ran while one was open for 27% of the time, Pallas kernels for 0%

commit v1 on v0

v1 whole, which is shorter than its diff:
```python
import functools
import math

import jax
import jax.numpy as jnp
from jax import lax
from jax.experimental import pallas as pl
from jax.experimental.pallas import tpu as pltpu
from jax.sharding import Mesh
from jax.sharding import PartitionSpec as P

HDIM = 64
EPS = 1e-05
THETA = 10000.0
NEG = -1000000000.0
F32 = jnp.float32
BF16 = jnp.bfloat16
RING = 8
ROW = ("far", "row")
ALL = ("frame", "far", "row")


def swap(value, bits):
    return lax.ppermute(value, "frame", [(i, i ^ bits) for i in range(lax.axis_size("frame"))])


def frame_sum(value):
    value = value + swap(value, 1)
    return value + swap(value, 2)


def token_sum(value):
    blocks = value.reshape(value.shape[0], 4, -1)
    got = swap(blocks, 1).reshape(value.shape[0], 2, 2, -1)
    blocks = blocks + got[:, :, ::-1].reshape(blocks.shape)
    got = swap(blocks, 2)
    blocks = blocks + jnp.concatenate([got[:, 2:], got[:, :2]], axis=1)
    return blocks.reshape(value.shape)


def frame_gather(value):
    over = swap(value, 2)
    pair = swap(jnp.stack([value, over]), 1)
    return jnp.stack([value, pair[0], over, pair[1]])


def frame_scatter(terms):
    low = terms.astype(BF16)
    got = swap(jnp.stack([low[1], low[3]]), 1).astype(F32)
    far = (terms[2] + got[1]).astype(BF16)
    return terms[0] + got[0] + swap(far, 2).astype(F32)


def row_neighbours(block):
    count = lax.axis_size(ROW)
    forward = [(i, i + 1) for i in range(count - 1)]
    above = lax.ppermute(block, ROW, forward)
    below = lax.ppermute(block, ROW, [(b, a) for a, b in forward])
    return above, below


def row_gather(block):
    return lax.all_gather(block, ROW, axis=0, tiled=True)


def row_scatter(terms):
    return lax.psum_scatter(terms, ROW, scatter_dimension=0, tiled=True)


def to_owner(block):
    frames, rows = lax.axis_size("frame"), lax.axis_size(ROW)
    part = rows // frames
    pairs = []
    for f in range(frames):
        for c in range(frames):
            for h in range(part):
                pairs.append((f * rows + c * part + h, c * rows + f * part + h))
    return lax.ppermute(block, ALL, pairs)


def owners(pair):
    j, k = divmod(pair, 3)
    if k == 1:
        return [(2 * j, 1, (0, 1)), (2 * j + 1, 1, (2, 3))]
    return [(2 * j + k // 2, 0, (0, 1, 2, 3))]


def q_rows(slot, chunk):
    if slot == 0:
        return 64 * (chunk % 2), chunk // 2
    return 128, chunk % 2


def lanes(shape):
    return lax.broadcasted_iota(jnp.int32, shape, len(shape) - 1)


def half(value, source, target):
    return value if source == target else pltpu.roll(value, 64, 1)


def partner(value):
    lane = lanes(value.shape) % 64
    up8, dn8 = pltpu.roll(value, 120, 1), pltpu.roll(value, 8, 1)
    up12, dn12 = pltpu.roll(value, 116, 1), pltpu.roll(value, 12, 1)
    lower = ((lane >= 16) & (lane < 28)) | ((lane >= 40) & (lane < 52))
    return jnp.where(lane < 8, up8, jnp.where(lane < 16, dn8, jnp.where(lower, up12, dn12)))


def store_queries(out_ref, base, tile, clip, pair_of_heads):
    lane = lanes((64, 128))
    for e in range(2):
        pair = 6 * clip + 2 * pair_of_heads + e
        chunk = [tile[128 * k + 64 * clip : 128 * k + 64 * clip + 64] for k in range(4)]
        for dev, slot, chunks in owners(pair):
            for lo in chunks[: len(chunks) // 2]:
                row, _ = q_rows(slot, lo)
                hi = lo + len(chunks) // 2
                value = jnp.where(lane < 64, half(chunk[lo], e, 0), half(chunk[hi], e, 1))
                out_ref[dev, base + row : base + row + 64, :] = value.astype(out_ref.dtype)


def load_queries(in_ref, base, clip, pair_of_heads):
    lane = lanes((64, 128))
    parts = []
    for e in range(2):
        pair = 6 * clip + 2 * pair_of_heads + e
        found = [None] * 4
        for dev, slot, chunks in owners(pair):
            for c in chunks:
                row, source = q_rows(slot, c)
                value = in_ref[dev, base + row : base + row + 64, :].astype(F32)
                found[c] = half(value, source, e)
        parts.append(found)
    return [jnp.where(lane < 64, a, b) for a, b in zip(*parts)]


def send_kernel(qkv_ref, rs_ref, gain_ref, cos_ref, sin_ref, send_ref, qc_ref):
    lane = lanes((64, 128))
    cosine, sine = cos_ref[...], sin_ref[...]
    rq, rk = rs_ref[:, 0:1], rs_ref[:, 1:2]
    width = 384
    for hp in range(3):
        cut = slice(128 * hp, 128 * hp + 128)
        qn = qkv_ref[:, cut] * rq * gain_ref[0:1, cut]
        kn = qkv_ref[:, width + 128 * hp : width + 128 * hp + 128] * rk * gain_ref[1:2, cut]
        vv = qkv_ref[:, 2 * width + 128 * hp : 2 * width + 128 * hp + 128]
        qc_ref[:, cut] = qn.astype(BF16)
        qr = qn * cosine + partner(qn) * sine
        kr = kn * cosine + partner(kn) * sine
        for clip in range(2):
            store_queries(send_ref, 512, qr, clip, hp)
            for e in range(2):
                for k in range(4):
                    row = 128 * k + 64 * clip
                    kc, vc = kr[row : row + 64], vv[row : row + 64]
                    value = jnp.where(lane < 64, half(kc, e, 0), half(vc, e, 1)).astype(BF16)
                    for dev, slot, _ in owners(6 * clip + 2 * hp + e):
                        at = 256 * slot + 64 * k
                        send_ref[dev, at : at + 64, :] = value


def mix_kernel(o_ref, oc_ref, gate_ref, attn_ref):
    for hp in range(3):
        cut = slice(128 * hp, 128 * hp + 128)
        gate = gate_ref[0:1, cut]
        for clip in range(2):
            for k, chunk in enumerate(load_queries(o_ref, 0, clip, hp)):
                rows = slice(128 * k + 64 * clip, 128 * k + 64 * clip + 64)
                attn_ref[rows, cut] = (chunk + gate * oc_ref[rows, cut]).astype(BF16)


def split_kernel(d_ref, gate_ref, do_ref, doc_ref):
    for hp in range(3):
        cut = slice(128 * hp, 128 * hp + 128)
        tile = d_ref[:, cut]
        doc_ref[:, cut] = (tile * gate_ref[0:1, cut]).astype(BF16)
        for clip in range(2):
            store_queries(do_ref, 0, tile, clip, hp)


def back_kernel(d_ref, dqc_ref, cos_ref, sin_ref, dqn_ref, dkn_ref, dv_ref):
    lane = lanes((64, 128))
    for hp in range(3):
        cut = slice(128 * hp, 128 * hp + 128)
        for clip in range(2):
            queries = load_queries(d_ref, 512, clip, hp)
            for k in range(4):
                rows = slice(128 * k + 64 * clip, 128 * k + 64 * clip + 64)
                cosine, sine = cos_ref[rows, :], sin_ref[rows, :]
                heads = []
                for e in range(2):
                    total = None
                    for dev, slot, _ in owners(6 * clip + 2 * hp + e):
                        at = 256 * slot + 64 * k
                        term = d_ref[dev, at : at + 64, :].astype(F32)
                        total = term if total is None else total + term
                    heads.append(total)
                dk = jnp.where(lane < 64, heads[0], half(heads[1], 0, 1))
                dv = jnp.where(lane < 64, half(heads[0], 1, 0), heads[1])
                dq = queries[k]
                dqn_ref[rows, cut] = dq * cosine + partner(dq * sine) + dqc_ref[rows, cut]
                dkn_ref[rows, cut] = dk * cosine + partner(dk * sine)
                dv_ref[rows, cut] = dv.astype(BF16)


def dot_nt(a, b):
    return lax.dot_general(a, b, (((1,), (1,)), ((), ())), preferred_element_type=F32)


def dot_nn(a, b):
    return lax.dot_general(a, b, (((1,), (0,)), ((), ())), preferred_element_type=F32)


def dot_tn(a, b):
    return lax.dot_general(a, b, (((0,), (0,)), ((), ())), preferred_element_type=F32)


def query_block(ref, slot, i, base):
    if slot == 0:
        return ref[pl.ds(i, 1), base : base + 128, :].reshape(128, 128).astype(F32)
    return ref[pl.ds(2 * i, 2), base + 128 : base + 192, :].reshape(128, 128).astype(F32)


def put_block(ref, slot, i, base, value):
    if slot == 0:
        ref[pl.ds(i, 1), base : base + 128, :] = value.reshape(1, 128, 128).astype(ref.dtype)
    else:
        ref[pl.ds(2 * i, 2), base + 128 : base + 192, :] = value.reshape(2, 64, 128).astype(ref.dtype)


def self_kernel(kv_ref, q_ref, o_ref, ot_ref, lse_ref):
    lane = lanes((128, 128))
    for slot in range(2):
        kv = kv_ref[:, 256 * slot : 256 * slot + 256, :].reshape(-1, 128)
        kvt = kv.astype(F32).T.astype(BF16)

        def step(i, carry):
            q = query_block(q_ref, slot, i, 512) * (HDIM ** (-0.5))
            qa = jnp.where(lane < 64, q, 0.0)
            qb = jnp.where(lane < 64, pltpu.roll(q, 64, 1), 0.0)
            q2 = jnp.concatenate([qa, qb], axis=0).astype(BF16)
            s = dot_nt(kv, q2)
            top = jnp.max(s, axis=0, keepdims=True)
            p = jnp.exp(s - top)
            total = jnp.sum(p, axis=0, keepdims=True)
            ot = dot_nn(kvt, p.astype(BF16)) / total
            o = ot.T
            packed = jnp.where(lane < 64, pltpu.roll(o[:128], 64, 1), o[128:])
            put_block(o_ref, slot, i, 0, packed)
            ot_ref[pl.ds(8 * slot + i, 1)] = ot[64:].reshape(1, 64, 256)
            lse_ref[pl.ds(8 * slot + i, 1)] = (top + jnp.log(total)).reshape(1, 1, 256)
            return carry

        lax.fori_loop(0, 8 if slot == 0 else 4, step, 0)


def self_back_kernel(merged, kv_ref, q_ref, do_ref, ot_ref, lse_ref, *rest):
    if merged:
        dkv_ref, acc_ref = rest
        dq_ref, base = dkv_ref, 512
    else:
        dkv_ref, dq_ref, acc_ref = rest
        base = 0
    lane = lanes((128, 128))
    for slot in range(2):
        kv = kv_ref[:, 256 * slot : 256 * slot + 256, :].reshape(-1, 128)
        kvt = kv.astype(F32).T.astype(BF16)
        acc_ref[...] = jnp.zeros_like(acc_ref)

        def step(i, carry):
            q = query_block(q_ref, slot, i, 512) * (HDIM ** (-0.5))
            d = query_block(do_ref, slot, i, 0)
            qa = jnp.where(lane < 64, q, 0.0)
            qb = jnp.where(lane < 64, pltpu.roll(q, 64, 1), 0.0)
            q2 = jnp.concatenate([qa, qb], axis=0).astype(BF16)
            da = jnp.where(lane < 64, 0.0, pltpu.roll(d, 64, 1))
            db = jnp.where(lane < 64, 0.0, d)
            d2 = jnp.concatenate([da, db], axis=0)
            delta = jnp.sum(d2.T[64:] * ot_ref[pl.ds(8 * slot + i, 1)].reshape(64, 256), axis=0, keepdims=True)
            d2 = d2.astype(BF16)
            s = dot_nt(kv, q2)
            p = jnp.exp(s - lse_ref[pl.ds(8 * slot + i, 1)].reshape(1, 256))
            dp = dot_nt(kv, d2)
            ds = (p * (dp - delta)).astype(BF16)
            acc_ref[...] += dot_nn(ds, q2) + dot_nn(p.astype(BF16), d2)
            dq = dot_nn(kvt, ds).T * (HDIM ** (-0.5))
            packed = jnp.where(lane < 64, dq[:128], pltpu.roll(dq[128:], 64, 1))
            put_block(dq_ref, slot, i, base, packed)
            return carry

        lax.fori_loop(0, 8 if slot == 0 else 4, step, 0)
        dkv_ref[:, 256 * slot : 256 * slot + 256, :] = (
            acc_ref[...].reshape(-1, 256, 128).astype(dkv_ref.dtype)
        )


def cross_probs(kc, q, bias, lane, e):
    qm = jnp.where((lane < 64) == (e == 0), q, jnp.zeros_like(q))
    s = jnp.where(bias > 0.0, dot_nt(kc, qm) * (HDIM ** (-0.5)), NEG)
    p = jnp.exp(s - jnp.max(s, axis=0, keepdims=True))
    return p / jnp.sum(p, axis=0, keepdims=True), qm


def cross_kernel(q_ref, kc_ref, vc_ref, bias_ref, o_ref):
    q = q_ref[...].reshape(256, 128)
    lane = lanes((256, 128))
    bias = bias_ref[...]
    outs = []
    for e in range(2):
        p, _ = cross_probs(kc_ref[...], q, bias, lane, e)
        outs.append(dot_tn(p.astype(BF16), vc_ref[...]))
    o_ref[...] = jnp.where(lane < 64, outs[0], outs[1]).reshape(4, 1, 64, 128)


def cross_back_kernel(q_ref, kc_ref, vc_ref, bias_ref, do_ref, dq_ref, dk_ref, dv_ref):
    q = q_ref[...].reshape(256, 128)
    d = do_ref[...].reshape(256, 128)
    lane = lanes((256, 128))
    bias = bias_ref[...]
    kc, vc = kc_ref[...], vc_ref[...]
    dqs, dk, dv = [], 0.0, 0.0
    for e in range(2):
        p, qm = cross_probs(kc, q, bias, lane, e)
        dm = jnp.where((lane < 64) == (e == 0), d, jnp.zeros_like(d))
        dp = dot_nt(vc, dm)
        dt = (p * (dp - jnp.sum(p * dp, axis=0, keepdims=True))).astype(BF16)
        dqs.append(dot_tn(dt, kc))
        dk = dk + lax.dot_general(qm, dt, (((0,), (1,)), ((), ())), preferred_element_type=F32)
        dv = dv + lax.dot_general(
            dm, p.astype(BF16), (((0,), (1,)), ((), ())), preferred_element_type=F32
        )
    dq = jnp.where(lane < 64, dqs[0], dqs[1]) * (HDIM ** (-0.5))
    dq_ref[...] = dq.reshape(4, 1, 64, 128)
    dk_ref[...] = dk * (HDIM ** (-0.5))
    dv_ref[...] = dv


def call(kernel, outs, *args, scratch=(), flops=0):
    size = sum(math.prod(a.shape) * a.dtype.itemsize for a in (*args, *outs))
    spec = pl.BlockSpec(memory_space=pltpu.VMEM)
    return pl.pallas_call(
        kernel,
        out_shape=outs,
        in_specs=[spec] * len(args),
        out_specs=[spec] * len(outs),
        scratch_shapes=list(scratch),
        compiler_params=pltpu.CompilerParams(vmem_limit_bytes=56 << 20),
        cost_estimate=pl.CostEstimate(flops=flops, bytes_accessed=size, transcendentals=flops // 256),
    )(*args)


def cross_call(kernel, outs, specs, *args):
    token = pl.BlockSpec((4, 1, 64, 128), lambda c, h: (0, c, 0, h))
    key = pl.BlockSpec((256, 128), lambda c, h: (c, h))
    bias = pl.BlockSpec((256, 1), lambda c, h: (c, 0))
    back = pl.BlockSpec((128, 256), lambda c, h: (h, c))
    kinds = {"t": token, "k": key, "b": bias, "o": back}
    return pl.pallas_call(
        kernel,
        grid=(2, 3),
        out_shape=outs,
        in_specs=[kinds[c] for c in specs[0]],
        out_specs=[kinds[c] for c in specs[1]],
        compiler_params=pltpu.CompilerParams(vmem_limit_bytes=40 << 20),
        cost_estimate=pl.CostEstimate(
            flops=12 * len(args) * 256 * 256 * 128, bytes_accessed=4 << 20, transcendentals=12 << 16
        ),
    )(*args)


def shaped(shape, dtype=F32):
    return jax.ShapeDtypeStruct(shape, dtype)


def rms_norm(tensor, gain):
    return tensor * lax.rsqrt(jnp.mean(tensor * tensor, axis=-1, keepdims=True) + EPS) * gain


def rotary_lanes():
    parts = ((0, 16), (1, 24), (2, 24))
    freqs = [[], [], []]
    signs = []
    for which, size in parts:
        for upper in range(2):
            for i in range(size // 2):
                for p in range(3):
                    freqs[p].append(math.exp(-math.log(THETA) * 2.0 * i / size) if p == which else 0.0)
                signs.append(1.0 if upper else -1.0)
    return [jnp.array(f, F32) for f in freqs], jnp.array(signs, F32)


def mm(a, b):
    return jnp.dot(a, b, preferred_element_type=F32)


def body(
    tokens,
    w_query,
    w_key,
    w_value,
    w_out,
    w_gate,
    w_up,
    w_down,
    w_cap_key,
    w_cap_value,
    w_mod,
    norm_gains,
    mix_coefs,
    caption,
    cap_len,
    cap_mask,
    timesteps,
    frame_pos,
    row_pos,
    col_pos,
    grad_out,
):
    clips, frames, rows_here, cols, width = tokens.shape
    local = frames * rows_here * cols
    group = lax.axis_size("frame")
    n_rows = lax.axis_size(ROW)
    n_far = lax.axis_size("far")
    n_all = group * n_rows
    me = lax.axis_index("frame")
    my_row = lax.axis_index(ROW)
    heads_w = width // group
    ff_w = w_gate.shape[1] // group
    count = group * clips * local
    caps = caption.shape[1]
    share = width // n_all

    def by_columns(parts):
        rows = parts[0].shape[0]
        cut = jnp.concatenate([w.reshape(rows, group, -1) for w in parts], axis=2)
        cut = lax.all_to_all(cut.transpose(1, 0, 2), "frame", 0, 0)
        full = row_gather(cut.reshape(group * rows, -1))
        full = full.reshape(n_rows, group, rows, -1).transpose(1, 0, 2, 3)
        return full.reshape(n_rows * group * rows, -1)

    w_qkv = by_columns([w_query, w_key, w_value])
    stack = jnp.concatenate([w_cap_key.T, w_cap_value.T, w_out], axis=0)
    stack = row_gather(stack).reshape(n_rows, 3, -1, width).transpose(1, 0, 2, 3)
    w_ck, w_cv, w_o = stack.reshape(3, heads_w, width)
    w_gu = by_columns([w_gate, w_up])
    w_dn = row_gather(w_down)

    half_width = width // 2
    frequencies = jnp.exp(-math.log(THETA) * jnp.arange(half_width, dtype=F32) / half_width)
    phases = timesteps.astype(F32)[:, None] * frequencies[None, :]
    step_embed = jax.nn.silu(jnp.concatenate([jnp.cos(phases), jnp.sin(phases)], axis=1)).astype(BF16)
    mod_local = mm(step_embed, w_mod).astype(BF16).astype(F32)
    mod_cols = mod_local.shape[1]
    note = jnp.concatenate([mod_local.reshape(-1), frame_pos.astype(F32).reshape(-1)])
    used = note.shape[0]
    note = jnp.pad(note, (0, -used % 512)).reshape(1, -1, 128)
    note = lax.all_to_all(jnp.broadcast_to(note, (n_all,) + note.shape[1:]), ALL, 0, 0)
    note = note.reshape(n_all, -1)
    mod_full = note[:, : clips * mod_cols].reshape(n_all, clips, mod_cols)
    mod_full = mod_full.transpose(1, 0, 2).reshape(clips, 4, width)
    scale_a, gate_a, scale_f, gate_f = (mod_full[:, i] for i in range(4))
    positions = note[:, clips * mod_cols : used].reshape(group, n_rows, clips, frames)[:, 0]
    order = jnp.arange(group)
    pick = (order[None, :] == (me ^ order)[:, None]).astype(F32)
    positions = jnp.sum(pick[:, :, None, None] * positions[None], axis=1)

    above_g, below_g = row_neighbours(grad_out)
    gains = norm_gains
    own_gains = lax.dynamic_slice(gains, (4, me * heads_w), (3, heads_w))
    own_gate = jnp.tanh(lax.dynamic_slice(mix_coefs, (0, me * heads_w), (1, heads_w)))

    full = (group, clips, frames, cols)
    pos_a = jnp.broadcast_to((positions + cap_len.astype(F32)[None, :, None])[..., None], full)
    pos_b = jnp.broadcast_to(row_pos.astype(F32)[0], full)
    pos_e = jnp.broadcast_to(col_pos.astype(F32), full)
    (fa, fb, fe), sign = rotary_lanes()
    angle = (
        pos_a.reshape(count, 1) * fa + pos_b.reshape(count, 1) * fb + pos_e.reshape(count, 1) * fe
    )
    cosine = jnp.tile(jnp.cos(angle), (1, 2))
    sine = jnp.tile(jnp.sin(angle) * sign, (1, 2))

    x_own = tokens.reshape(clips, local, width)
    x_flat = x_own.astype(F32)
    x_group = frame_gather(x_own)

    def pre_piece(x_in, gain, scale_in):
        return rms_norm(x_in, gain) * (1.0 + scale_in[:, None, :])

    h_in = pre_piece(x_group.astype(F32), gains[0], scale_a).astype(BF16).reshape(count, width)
    _, pre_back = jax.vjp(pre_piece, x_flat, gains[0], scale_a)
    qkv = mm(h_in, w_qkv)
    q_zero, k_zero = qkv[:, :heads_w], qkv[:, heads_w : 2 * heads_w]
    squares = jnp.stack([jnp.sum(q_zero * q_zero, axis=1), jnp.sum(k_zero * k_zero, axis=1)])
    rsq = lax.rsqrt(token_sum(squares) / width + EPS).T
    send, q_cap = call(
        send_kernel,
        [shaped((RING, 704, 128), BF16), shaped((count, heads_w), BF16)],
        qkv,
        rsq,
        own_gains,
        cosine,
        sine,
    )
    got = lax.all_to_all(send, "row", 0, 0)
    kv_all = got
    if n_far > 1:
        kv_all = lax.all_gather(got, "far", axis=0, tiled=True)
    keys = kv_all.shape[0] * 256
    work = 12 * keys * 256 * 128 * 2
    o_pack, o_t, lse = call(
        self_kernel,
        [shaped((RING, 192, 128), BF16), shaped((12, 64, 256)), shaped((12, 1, 256))],
        kv_all,
        got,
        flops=2 * work,
    )
    o_back = lax.all_to_all(o_pack, "row", 0, 0)

    cap2 = caption.reshape(clips * caps, width)
    usable = (jnp.arange(caps)[None, :] < cap_len[:, None]) & (cap_mask > 0)
    bias = usable.astype(F32).reshape(clips * caps, 1)
    k_pre = lax.dot_general(cap2, w_ck, (((1,), (1,)), ((), ())), preferred_element_type=F32)
    v_cap = lax.dot_general(cap2, w_cv, (((1,), (1,)), ((), ())), preferred_element_type=F32).astype(BF16)
    r_cap = lax.rsqrt(frame_sum(jnp.sum(k_pre * k_pre, axis=1)[None]) / width + EPS)
    k_cap = (k_pre * r_cap.T * own_gains[2]).astype(BF16)
    q_cap4 = q_cap.reshape(group, clips, local, heads_w)
    (out_cross,) = cross_call(
        cross_kernel, [shaped(q_cap4.shape)], ("tkkb", "t"), q_cap4, k_cap, v_cap, bias
    )
    out_cross = out_cross.reshape(count, heads_w)
    (attn_mix,) = call(mix_kernel, [shaped((count, heads_w), BF16)], o_back, out_cross, own_gate)

    y_one = frame_scatter(mm(attn_mix, w_o).reshape(group, clips, local, width))

    def mid_piece(x_in, y_in, gain_two, gate_in, gain_three, scale_in):
        h_mid = x_in + jnp.tanh(gate_in)[:, None, :] * rms_norm(y_in, gain_two)
        return (h_mid, rms_norm(h_mid, gain_three) * (1.0 + scale_in[:, None, :]))

    (h_mid, f_in32), mid_back = jax.vjp(mid_piece, x_flat, y_one, gains[1], gate_a, gains[2], scale_f)
    f_in = frame_gather(f_in32.astype(BF16)).reshape(count, width)
    gate_up = mm(f_in, w_gu)

    def act_piece(gate_in, up_in):
        return jax.nn.silu(gate_in) * up_in

    hidden32, act_back = jax.vjp(act_piece, gate_up[:, :ff_w], gate_up[:, ff_w:])
    hidden = hidden32.astype(BF16)
    z_out = frame_scatter(mm(hidden, w_dn).reshape(group, clips, local, width))

    def end_piece(h_in_mid, z_in, gain_four, gate_in):
        return h_in_mid + jnp.tanh(gate_in)[:, None, :] * rms_norm(z_in, gain_four)

    y_all, end_back = jax.vjp(end_piece, h_mid, z_out, gains[3], gate_f)
    y_grid = y_all.reshape(tokens.shape)
    above, below = (v.astype(F32) for v in row_neighbours(y_grid.astype(BF16)))
    output = (y_grid + mix_coefs[1] * above + mix_coefs[2] * below).astype(BF16)

    g_center = grad_out.astype(F32)
    d_y = g_center + mix_coefs[1] * below_g.astype(F32) + mix_coefs[2] * above_g.astype(F32)
    d_above = jnp.sum(g_center * above, axis=(0, 1, 2, 3))
    d_below = jnp.sum(g_center * below, axis=(0, 1, 2, 3))
    d_h_end, d_z, d_g_four, d_gate_f = end_back(d_y.reshape(clips, local, width))
    d_z_all = frame_gather(d_z.astype(BF16)).reshape(count, width)
    d_hidden = lax.dot_general(d_z_all, w_dn, (((1,), (1,)), ((), ())), preferred_element_type=F32)
    d_gu = jnp.concatenate([d.astype(BF16) for d in act_back(d_hidden)], axis=1)
    d_f_in = lax.dot_general(d_gu, w_gu, (((1,), (1,)), ((), ())), preferred_element_type=F32)
    d_f_in = frame_scatter(d_f_in.reshape(group, clips, local, width))

    def term(left, right):
        return lax.dot_general(left, right, (((0,), (0,)), ((), ())), preferred_element_type=F32).astype(BF16)

    def term_by_owner(left, right):
        return jnp.concatenate(
            [term(left, right[:, c * heads_w : (c + 1) * heads_w]) for c in range(group)], axis=0
        )

    sum_down = to_owner(row_scatter(term_by_owner(hidden, d_z_all)))
    sum_gu = row_scatter(term(f_in, d_gu))

    d_x_mid, d_y_one, d_g_two, d_gate_a, d_g_three, d_scale_f = mid_back((d_h_end, d_f_in))
    d_y_group = frame_gather(d_y_one.astype(BF16)).reshape(count, width)
    d_attn = lax.dot_general(d_y_group, w_o, (((1,), (1,)), ((), ())), preferred_element_type=F32)
    sum_out = to_owner(row_scatter(term_by_owner(attn_mix, d_y_group)))

    d_pack, d_cross = call(
        split_kernel, [shaped((RING, 192, 128), BF16), shaped((count, heads_w), BF16)], d_attn, own_gate
    )
    d_got = lax.all_to_all(d_pack, "row", 0, 0)
    d_mix_gate = jnp.sum(d_attn * out_cross, axis=0) * (1.0 - own_gate[0] * own_gate[0])
    d_q_cross, d_k_cap, d_v_cap = cross_call(
        cross_back_kernel,
        [shaped(q_cap4.shape), shaped((heads_w, clips * caps)), shaped((heads_w, clips * caps))],
        ("tkkbt", "too"),
        q_cap4,
        k_cap,
        v_cap,
        bias,
        d_cross.reshape(q_cap4.shape),
    )
    back_scratch = [pltpu.VMEM((keys, 128), F32)]
    if n_far == 1:
        (d_send,) = call(
            functools.partial(self_back_kernel, True),
            [shaped((RING, 704, 128), BF16)],
            kv_all,
            got,
            d_got,
            o_t,
            lse,
            scratch=back_scratch,
            flops=5 * work,
        )
    else:
        d_kv, d_q = call(
            functools.partial(self_back_kernel, False),
            [shaped((kv_all.shape[0], 512, 128), BF16), shaped((RING, 192, 128), BF16)],
            kv_all,
            got,
            d_got,
            o_t,
            lse,
            scratch=back_scratch,
            flops=5 * work,
        )
        d_kv = lax.psum_scatter(d_kv, "far", scatter_dimension=0, tiled=True)
        d_send = jnp.concatenate([d_kv, d_q], axis=1)
    d_recv = lax.all_to_all(d_send, "row", 0, 0)
    d_qn, d_kn, d_v = call(
        back_kernel,
        [shaped((count, heads_w)), shaped((count, heads_w)), shaped((count, heads_w), BF16)],
        d_recv,
        d_q_cross.reshape(count, heads_w),
        cosine,
        sine,
    )
    rq, rk = rsq[:, 0:1], rsq[:, 1:2]
    d_g_query = jnp.sum(d_qn * q_zero * rq, axis=0)
    d_g_key = jnp.sum(d_kn * k_zero * rk, axis=0)
    a_q, a_k = d_qn * own_gains[0], d_kn * own_gains[1]
    dots = token_sum(jnp.stack([jnp.sum(a_q * q_zero, axis=1), jnp.sum(a_k * k_zero, axis=1)])).T / width
    d_q_low = (rq * a_q - q_zero * (rq * rq * rq * dots[:, 0:1])).astype(BF16)
    d_k_low = (rk * a_k - k_zero * (rk * rk * rk * dots[:, 1:2])).astype(BF16)
    d_qkv = jnp.concatenate([d_q_low, d_k_low, d_v], axis=1)
    d_h_in = lax.dot_general(d_qkv, w_qkv, (((1,), (1,)), ((), ())), preferred_element_type=F32)
    d_h_in = frame_scatter(d_h_in.reshape(group, clips, local, width))
    sum_qkv = row_scatter(term(h_in, d_qkv))
    d_x_pre, d_g_zero, d_scale_a = pre_back(d_h_in)
    grad_tokens = (d_x_pre + d_x_mid).reshape(tokens.shape)

    k_pre_t = k_pre.T
    gain_cap = own_gains[2][:, None]
    cap_dot = frame_sum(jnp.sum(d_k_cap * gain_cap * k_pre_t, axis=0, keepdims=True))
    wide = heads_w // n_rows
    cap_terms = jnp.stack([d_k_cap, d_v_cap]).reshape(2, n_rows, wide, clips * caps)
    cap_terms = cap_terms.transpose(1, 0, 2, 3).reshape(n_rows, 2 * wide, clips * caps)
    extra = jnp.broadcast_to(jnp.pad(cap_dot, ((0, 7), (0, 0)))[None], (n_rows, 8, clips * caps))
    cap_terms = jnp.concatenate([cap_terms, extra], axis=1).reshape(n_rows * (2 * wide + 8), -1)
    cap_sum = row_scatter(cap_terms)
    d_k_own, d_v_own, cap_dot = cap_sum[:wide], cap_sum[wide : 2 * wide], cap_sum[2 * wide : 2 * wide + 1]
    k_own = lax.dynamic_slice(k_pre_t, (my_row * wide, 0), (wide, clips * caps))
    g_own = lax.dynamic_slice(own_gains, (2, my_row * wide), (1, wide)).T
    d_g_cap = jnp.sum(d_k_own * k_own * r_cap, axis=1)
    d_k_zero_cap = (r_cap * g_own * d_k_own - k_own * (r_cap * r_cap * r_cap * cap_dot / width)).astype(BF16)

    def cap_weight(d):
        return lax.dot_general(cap2, d, (((0,), (1,)), ((), ())), preferred_element_type=F32)

    d_w_cap_key = cap_weight(d_k_zero_cap)
    d_w_cap_value = cap_weight(d_v_own.astype(BF16))

    def spread(block):
        return lax.dynamic_update_slice(jnp.zeros((width,), F32), block, (me * heads_w,))

    d_mod = jnp.concatenate([d_scale_a, d_gate_a, d_scale_f, d_gate_f], axis=1)
    d_mod = d_mod.reshape(clips, n_all, mod_cols).transpose(1, 0, 2).reshape(n_all, -1)
    rest = jnp.stack(
        [
            d_g_zero,
            d_g_two,
            d_g_three,
            d_g_four,
            spread(d_g_query),
            spread(d_g_key),
            spread(d_mix_gate),
            d_above,
            d_below,
        ]
    )
    rest = rest.reshape(9, n_all, share).transpose(1, 0, 2).reshape(n_all, -1)
    small = jnp.concatenate([d_mod, rest], axis=1)
    small = jnp.pad(small, ((0, 0), (0, -small.shape[1] % 128))).reshape(n_all, -1, 128)
    small = jnp.sum(lax.all_to_all(small, ALL, 0, 0), axis=0).reshape(-1)
    d_mod = small[: clips * mod_cols].reshape(clips, mod_cols)
    rest = small[clips * mod_cols : clips * mod_cols + 9 * share].reshape(9, share)
    d_w_mod = lax.dot_general(
        step_embed, d_mod.astype(BF16), (((0,), (0,)), ((), ())), preferred_element_type=F32
    )
    d_gains = jnp.concatenate([rest[:6], d_g_cap[None]], axis=0)
    d_mixes = rest[6:]

    sum_qkv = sum_qkv.astype(F32)
    sum_gu = sum_gu.astype(F32)
    return (
        output,
        grad_tokens,
        sum_qkv[:, :heads_w],
        sum_qkv[:, heads_w : 2 * heads_w],
        sum_qkv[:, 2 * heads_w :],
        sum_out.astype(F32),
        sum_gu[:, :ff_w],
        sum_gu[:, ff_w:],
        sum_down.astype(F32),
        d_w_cap_key,
        d_w_cap_value,
        d_w_mod,
        d_gains,
        d_mixes,
    )


def solution(mesh):
    frame, row = mesh.shape["frame"], mesh.shape["row"]
    fine = Mesh(mesh.devices.reshape(frame, row // RING, RING), ("frame", "far", "row"))
    grid = P(None, "frame", ROW, None, None)
    rows, columns = P(ALL, None), P(None, ALL)
    tile = P(ROW, "frame")
    return jax.shard_map(
        body,
        mesh=fine,
        in_specs=(
            (grid,)
            + (rows,) * 7
            + (columns,) * 3
            + (P(),) * 6
            + (P(None, "frame"), P(ROW), P(), grid)
        ),
        out_specs=(grid, grid) + (tile,) * 7 + (columns,) * 5,
        check_vma=False,
    )
```

time: 2180 us -> 898 us (0.41)
  waiting for transfers between devices: 1130 us -> 472 us
  blocking collectives: 388 us -> 29.1 us
  matrix products: 254 us -> 54.7 us
  local copies, waits for them, and re-layouts: 258 us -> 77.9 us
  Pallas kernels: 0 us -> 72.7 us
  starting transfers between devices: 31.6 us -> 91.7 us
    all_gather x17 -> x4, waiting for transfers between devices: 608 us -> 160 us  [row_gather(): return lax.all_gather(block, ROW, axis=0, tiled=True)]
    all_gather x3 -> x0, blocking collectives: 248 us -> none  [the longest x1 99.8 us: body(): lax.all_gather(log_sum, ('frame', 'row'), axis=1, tiled=True)]
    unnamed x31 -> x9, waiting for transfers between devices: 206 us -> 0.8 us
    dot_general x38 -> x24, matrix products: 249 us -> 54.7 us  [the longest x10 16.9 us: term(): lax.dot_general(left, right, (((0,), (0,)), ((), ())), preferred_element_...]
    reduce_scatter x8 -> x5, waiting for transfers between devices: 306 us -> 164 us  [row_scatter(): return lax.psum_scatter(terms, ROW, scatter_dimension=0, tiled=True)]
    unnamed x1 -> x0, blocking collectives: 96.1 us -> none
    ppermute x4 -> x30, waiting for transfers between devices: 12.8 us -> 93.3 us  [the longest x24 80.5 us: swap(): lax.ppermute(value, 'frame', [(i, i ^ bits) for i in range(lax.axis_size(...]
    pallas_call x0 -> x8, Pallas kernels: none -> 72.7 us  [the longest x6 59.9 us: call(): pl.pallas_call(kernel, out_shape=outs, in_specs=[spec] * len(args), out_s...]
  transfers between devices with their start and end apart: 36 -> 45, of which waited for: 19 -> 28; matrix products, arithmetic and copies ran while one was open for 27% -> 18% of each run, Pallas kernels for 0% -> 8%
where the time goes in v1:
time: 898 us; the launch traced here: 887 us
  waiting for transfers between devices  472 us (53%)
  starting transfers between devices  91.7 us (10%)
  local copies, waits for them, and re-layouts  77.9 us (9%)
  Pallas kernels  72.7 us (8%)
  other arithmetic  71.7 us (8%)
  matrix products  54.7 us (6%)
  blocking collectives  29.1 us (3%)
  between operations  16.8 us (2%)
    reduce_scatter x5, waiting for transfers between devices, row_scatter(): return lax.psum_scatter(terms, ROW, scatter_dimension=0, tiled=True)  164 us
    all_gather x4, waiting for transfers between devices, row_gather(): return lax.all_gather(block, ROW, axis=0, tiled=True)  160 us
    ppermute x24, waiting for transfers between devices, swap(): lax.ppermute(value, 'frame', [(i, i ^ bits) for i in range(lax.axis_size(...  80.5 us
    pallas_call x6, Pallas kernels, call(): pl.pallas_call(kernel, out_shape=outs, in_specs=[spec] * len(args), out_s...  59.9 us
    all_to_all x1, waiting for transfers between devices, body(): d_recv = lax.all_to_all(d_send, 'row', 0, 0)  33.2 us
    all_to_all x1, starting transfers between devices, body(): small = jnp.sum(lax.all_to_all(small, ALL, 0, 0), axis=0).reshape(-1)  30.2 us
    unnamed x216, local copies, waits for them, and re-layouts  22.4 us
    ppermute x24, starting transfers between devices, swap(): lax.ppermute(value, 'frame', [(i, i ^ bits) for i in range(lax.axis_size(...  19.4 us
  transfers between devices with their start and end apart: 45, of which 28 were waited for; matrix products, arithmetic and copies ran while one was open for 18% of the time, Pallas kernels for 8%

profile of v1, /device:TPU:2, one launch (start us, length us, event | category | flops | bytes accessed | tf_op | source)
XLA Modules:
  0.0 886.7 jit_solution(11338957361591986154)
XLA Ops:
  10.5 11.2 %all_to_all.40 = bf16[4,48,1152]{2,1,0:T(8,128)(2,1)} all-to-all(bf16[4,48,1152]{2,1,0:T(8,128)(2,1)S(1)} %copy.185), channel_id=1, replica_groups=mesh['frame'=4,'row'=8] {'frame'}, dimensions={0} | all-to-all | bytes 884736 | tf_op jit(solution)/shard_map/all_to_all | solution.py:437
  32.4 9.6 %all-to-all-done.4 = bf16[4,48,2048]{2,1,0:T(8,128)(2,1)S(1)} async-done(((bf16[4,48,2048]{2,1,0:T(8,128)(2,1)}), bf16[4,48,2048]{2,1,0:T(8,128)(2,1)S(1)}, u32[]{:S(2)}, u32[]{:S(2)}) %all-to-all-start.4) | async-done | bytes 786464 | tf_op jit(solution)/shard_map/all_to_all | solution.py:437
  42.7 5.2 all-to-all-start
  58.5 27.9 %all-gather.5.cloned.1.call-done = bf16[1536,1152]{1,0:T(8,128)(2,1)} async-done(((bf16[192,1152]{1,0:T(8,128)(2,1)}), bf16[1536,1152]{1,0:T(8,128)(2,1)}) %all-gather.5.cloned.1.call-update) | async-done | bytes 3538960 | tf_op jit(solution)/shard_map/all_gather | solution.py:63
  100.1 5.4 shard_map.344
  105.5 5.4 all-to-all-start.2
  111.0 64.0 %all-gather.7.cloned.1.call-done = bf16[1152,1536]{1,0:T(8,128)(2,1)} async-done(((bf16[144,1536]{1,0:T(8,128)(2,1)}), bf16[1152,1536]{1,0:T(8,128)(2,1)}) %all-gather.7.cloned.1.call-update) | async-done | bytes 3538960 | tf_op jit(solution)/shard_map/all_gather | solution.py:63
  184.7 21.3 %shard_map.345 = (bf16[8,192,128]{2,1,0:T(8,128)(2,1)}, f32[12,64,256]{2,1,0:T(8,128)}, f32[12,1,256]{2,1,0:T(1,128)}) custom-call(bf16[8,704,128]{2,1,0:T(8,128)(2,1)} %copy-done.48, bf16[8,704,128]{2,1,0:T(8,128)(2,1)} %copy-done.48), custom_call_target="tpu_custom_call" | custom-call | flops 3221225472 | bytes 4075520 | tf_op jit(solution)/shard_map/pallas_call | solution.py:342
  216.9 5.7 shard_map.346
  234.4 10.2 %collective-permute-done.7 = bf16[2,64,1536]{2,1,0:T(8,128)(2,1)} collective-permute-done((bf16[2,64,1536]{2,1,0:T(8,128)(2,1)}, bf16[2,64,1536]{2,1,0:T(8,128)(2,1)}, u32[]{:S(2)}, u32[]{:S(2)}) %collective-permute-start.7) | collective-permute-done | bytes 393248 | tf_op jit(solution)/shard_map/ppermute | solution.py:24
  249.4 9.0 %collective-permute-done.8 = bf16[2,64,1536]{2,1,0:T(8,128)(2,1)S(1)} collective-permute-done((bf16[2,64,1536]{2,1,0:T(8,128)(2,1)S(1)}, bf16[2,64,1536]{2,1,0:T(8,128)(2,1)S(1)}, u32[]{:S(2)}, u32[]{:S(2)}) %collective-permute-start.8) | collective-permute-done | bytes 393248 | tf_op jit(solution)/shard_map/ppermute | solution.py:24
  266.6 16.7 %all-gather.9.cloned.1.call-done = bf16[1536,2048]{1,0:T(8,128)(2,1)} async-done(((bf16[192,2048]{1,0:T(8,128)(2,1)}), bf16[1536,2048]{1,0:T(8,128)(2,1)}) %all-gather.9.cloned.1.call-update) | async-done | bytes 6291472 | tf_op jit(solution)/shard_map/all_gather | solution.py:63
  296.6 50.9 %all-gather.11.cloned.1.call-done = bf16[1024,1536]{1,0:T(8,128)(2,1)} async-done(((bf16[128,1536]{1,0:T(8,128)(2,1)}), bf16[1024,1536]{1,0:T(8,128)(2,1)}) %all-gather.11.cloned.1.call-update) | async-done | bytes 3145744 | tf_op jit(solution)/shard_map/all_gather | solution.py:63
  355.8 9.6 %collective-permute-done.11 = bf16[2,64,1536]{2,1,0:T(8,128)(2,1)S(1)} collective-permute-done((bf16[2,64,1536]{2,1,0:T(8,128)(2,1)S(1)}, bf16[2,64,1536]{2,1,0:T(8,128)(2,1)S(1)}, u32[]{:S(2)}, u32[]{:S(2)}) %collective-permute-start.11) | collective-permute-done | bytes 393248 | tf_op jit(solution)/shard_map/ppermute | solution.py:24
  369.7 8.9 collective-permute-done.16
  394.3 9.7 %collective-permute-done.19 = bf16[2,64,1536]{2,1,0:T(8,128)(2,1)S(1)} collective-permute-done((bf16[2,64,1536]{2,1,0:T(8,128)(2,1)S(1)}, bf16[2,64,1536]{2,1,0:T(8,128)(2,1)S(1)}, u32[]{:S(2)}, u32[]{:S(2)}) %collective-permute-start.19) | collective-permute-done | bytes 393248 | tf_op jit(solution)/shard_map/ppermute | solution.py:24
  409.3 8.9 collective-permute-done.20
  432.0 7.0 shard_map.350
  455.4 10.8 %pad_maximum_fusion = bf16[4096,384]{1,0:T(8,128)(2,1)} fusion(bf16[1024,384]{1,0:T(8,128)(2,1)S(1)} %convolution_convert_fusion.2, bf16[1024,384]{1,0:T(8,128)(2,1)S(1)} %convolution_convert_fusion.3, bf16[1024,384]{1,0:T(8,128)(2,1)S(1)} %convolution_convert_fusion.4, bf16[1024,384]{1,0:T(8,128)(2,1)S(1)} %convolution_convert_fusion.5), kind=kLoop, calls=%fused_computation.2 | loop fusion | flops 12582912 | bytes 6291456 | tf_op jit(solution)/shard_map/concatenate | solution.py:575
  467.7 6.9 convolution_convert_fusion
  475.6 17.9 %all_to_all.41.do_ref = bf16[8,192,128]{2,1,0:T(8,128)(2,1)} all-to-all(bf16[8,192,128]{2,1,0:T(8,128)(2,1)S(1)} %copy-done.54), channel_id=1, replica_groups=mesh['frame'=4,'row'=8] {'row'}, dimensions={0} | all-to-all | bytes 786432 | tf_op jit(solution)/shard_map/all_to_all | solution.py:590
  493.5 23.1 %shard_map.349 = bf16[8,704,128]{2,1,0:T(8,128)(2,1)} custom-call(bf16[8,704,128]{2,1,0:T(8,128)(2,1)} %copy-done.48, bf16[8,704,128]{2,1,0:T(8,128)(2,1)} %copy-done.48, bf16[8,192,128]{2,1,0:T(8,128)(2,1)} %all_to_all.41.do_ref, f32[12,64,256]{2,1,0:T(8,128)} %get-tuple-element.31.ot_ref, f32[12,1,256]{2,1,0:T(1,128)} %get-tuple-element.32.lse_ref), custom_call_target="tpu_custom_call" | custom-call | flops 8053063680 | bytes 5517312 | tf_op jit(solution)/shard_map/pallas_call | solution.py:342
  516.6 5.1 all-to-all-start.6
  522.0 33.2 %all-to-all-done.6.d_ref = bf16[8,704,128]{2,1,0:T(8,128)(2,1)} async-done(((bf16[8,704,128]{2,1,0:T(8,128)(2,1)}), bf16[8,704,128]{2,1,0:T(8,128)(2,1)}, u32[]{:S(2)}, u32[]{:S(2)}) %all-to-all-start.6) | async-done | bytes 1441824 | tf_op jit(solution)/shard_map/all_to_all | solution.py:629
  555.2 5.9 shard_map.351
  599.8 12.8 %collective-permute-done.12 = bf16[2,2,1,32,1536]{4,3,2,1,0:T(8,128)(2,1)} collective-permute-done((bf16[2,2,1,32,1536]{4,3,2,1,0:T(8,128)(2,1)}, bf16[2,2,1,32,1536]{4,3,2,1,0:T(8,128)(2,1)}, u32[]{:S(2)}, u32[]{:S(2)}) %collective-permute-start.12) | collective-permute-done | bytes 393248 | tf_op jit(solution)/shard_map/ppermute | solution.py:57
  630.4 29.8 %reduce-scatter.12.cloned.1.call-done = bf16[512,384]{1,0:T(8,128)(2,1)} async-done(((bf16[4096,384]{1,0:T(8,128)(2,1)}), bf16[512,384]{1,0:T(8,128)(2,1)}) %reduce-scatter.12.cloned.1.call-update) | async-done | bytes 393232 | tf_op jit(solution)/shard_map/reduce_scatter | solution.py:67
  671.3 8.9 %collective-permute-done.25 = bf16[2,64,1536]{2,1,0:T(8,128)(2,1)S(1)} collective-permute-done((bf16[2,64,1536]{2,1,0:T(8,128)(2,1)S(1)}, bf16[2,64,1536]{2,1,0:T(8,128)(2,1)S(1)}, u32[]{:S(2)}, u32[]{:S(2)}) %collective-permute-start.25) | collective-permute-done | bytes 393248 | tf_op jit(solution)/shard_map/ppermute | solution.py:24
  695.0 30.2 %all-to-all-start.7 = ((f32[32,7,128]{2,1,0:T(8,128)}), f32[32,7,128]{2,1,0:T(8,128)}, u32[]{:S(2)}, u32[]{:S(2)}) async-start(f32[32,7,128]{2,1,0:T(8,128)} %reshape.739), calls=%async_computation.12 | async-start | bytes 262144 | tf_op jit(solution)/shard_map/all_to_all | solution.py:694
  727.8 7.7 all-to-all-done.7
  740.7 54.7 %reduce-scatter.10.cloned.1.call-done = bf16[192,2048]{1,0:T(8,128)(2,1)} async-done(((bf16[1536,2048]{1,0:T(8,128)(2,1)}), bf16[192,2048]{1,0:T(8,128)(2,1)}) %reduce-scatter.10.cloned.1.call-update) | async-done | bytes 786448 | tf_op jit(solution)/shard_map/reduce_scatter | solution.py:67
  797.9 79.8 %reduce-scatter.6.cloned.1.call-done = bf16[192,1152]{1,0:T(8,128)(2,1)} async-done(((bf16[1536,1152]{1,0:T(8,128)(2,1)}), bf16[192,1152]{1,0:T(8,128)(2,1)}) %reduce-scatter.6.cloned.1.call-update) | async-done | bytes 442384 | tf_op jit(solution)/shard_map/reduce_scatter | solution.py:67
  (526 shorter events, 256.6 us)
Async XLA Ops:
  7.2 79.2 %all-gather.5.cloned.1.call-start = ((), (), s32[]{:S(2)}) async-start(), calls=%async_computation.13 | async-start | bytes 3981312 | tf_op jit(solution)/shard_map/all_gather | solution.py:63
  21.7 153.3 %all-gather.7.cloned.1.call-start = ((), (), s32[]{:S(2)}) async-start(), calls=%async_computation.14 | async-start | bytes 3981312 | tf_op jit(solution)/shard_map/all_gather | solution.py:63
  22.7 26.1 %collective-permute-start = (bf16[2,64,1536]{2,1,0:T(8,128)(2,1)S(1)}, bf16[2,64,1536]{2,1,0:T(8,128)(2,1)S(1)}, u32[]{:S(2)}, u32[]{:S(2)}) collective-permute-start(bf16[2,64,1536]{2,1,0:T(8,128)(2,1)S(1)} %bitcast.272), channel_id=1, source_target_pairs={{0,16},{8,24},{16,0},{24,8},{1,17},{9,25},{17,1},{25,9},{2,18},{10... | collective-permute-start | bytes 1179656 | tf_op jit(solution)/shard_map/ppermute | solution.py:24
  25.5 16.5 %all-to-all-start.4 = ((bf16[4,48,2048]{2,1,0:T(8,128)(2,1)}), bf16[4,48,2048]{2,1,0:T(8,128)(2,1)S(1)}, u32[]{:S(2)}, u32[]{:S(2)}) async-start(bf16[4,48,2048]{2,1,0:T(8,128)(2,1)} %copy.196), calls=%async_computation.4 | async-start | bytes 1572864 | tf_op jit(solution)/shard_map/all_to_all | solution.py:437
  42.7 11.5 %all-to-all-start = ((f32[32,4,128]{2,1,0:T(4,128)}), f32[32,4,128]{2,1,0:T(4,128)S(1)}, u32[]{:S(2)}, u32[]{:S(2)}) async-start(f32[32,4,128]{2,1,0:T(4,128)} %broadcast_in_dim.25), calls=%async_computation | async-start | bytes 131072 | tf_op jit(solution)/shard_map/all_to_all | solution.py:458
  47.9 235.5 %all-gather.9.cloned.1.call-start = ((), (), s32[]{:S(2)}) async-start(), calls=%async_computation.15 | async-start | bytes 7077888 | tf_op jit(solution)/shard_map/all_gather | solution.py:63
  105.5 78.0 %all-to-all-start.2 = ((bf16[8,704,128]{2,1,0:T(8,128)(2,1)}), bf16[8,704,128]{2,1,0:T(8,128)(2,1)S(1)}, u32[]{:S(2)}, u32[]{:S(2)}) async-start(bf16[8,704,128]{2,1,0:T(8,128)(2,1)} %get-tuple-element.27), calls=%async_computation.2 | async-start | bytes 2883584 | tf_op jit(solution)/shard_map/all_to_all | solution.py:506
  182.0 33.6 %collective-permute-start.5 = (f32[1,512]{1,0:T(1,128)S(1)}, f32[1,512]{1,0:T(1,128)S(1)}, u32[]{:S(2)}, u32[]{:S(2)}) collective-permute-start(f32[1,512]{1,0:T(1,128)S(1)} %add.258), channel_id=1, source_target_pairs={{0,16},{8,24},{16,0},{24,8},{1,17},{9,25},{17,1},{25,9},{2,18},{10... | collective-permute-start | bytes 6152 | tf_op jit(solution)/shard_map/ppermute | solution.py:24
  206.0 17.5 %all-to-all-start.3 = ((bf16[8,192,128]{2,1,0:T(8,128)(2,1)}), bf16[8,192,128]{2,1,0:T(8,128)(2,1)S(1)}, u32[]{:S(2)}, u32[]{:S(2)}) async-start(bf16[8,192,128]{2,1,0:T(8,128)(2,1)} %get-tuple-element.28), calls=%async_computation.3 | async-start | bytes 786432 | tf_op jit(solution)/shard_map/all_to_all | solution.py:519
  210.9 136.6 %all-gather.11.cloned.1.call-start = ((), (), s32[]{:S(2)}) async-start(), calls=%async_computation.16 | async-start | bytes 3538944 | tf_op jit(solution)/shard_map/all_gather | solution.py:63
  233.2 11.5 %collective-permute-start.7 = (bf16[2,64,1536]{2,1,0:T(8,128)(2,1)}, bf16[2,64,1536]{2,1,0:T(8,128)(2,1)}, u32[]{:S(2)}, u32[]{:S(2)}) collective-permute-start(bf16[2,64,1536]{2,1,0:T(8,128)(2,1)} %fusion.37), channel_id=1, source_target_pairs={{0,16},{8,24},{16,0},{24,8},{1,17},{9,25},{17,1},{25,9},{2,18},{10... | collective-permute-start | bytes 1179656 | tf_op jit(solution)/shard_map/ppermute | solution.py:24
  234.4 363.5 %reduce-scatter.8.cloned.1.call-start = ((), (), s32[]{:S(2)}) async-start(), calls=%async_computation.18 | async-start | bytes 1327104 | tf_op jit(solution)/shard_map/reduce_scatter | solution.py:67
  248.0 10.4 %collective-permute-start.8 = (bf16[2,64,1536]{2,1,0:T(8,128)(2,1)S(1)}, bf16[2,64,1536]{2,1,0:T(8,128)(2,1)S(1)}, u32[]{:S(2)}, u32[]{:S(2)}) collective-permute-start(bf16[2,64,1536]{2,1,0:T(8,128)(2,1)S(1)} %multiply_convert_fusion.3), channel_id=1, source_target_pairs={{0,16},{8,24},{16,0},{24,8},{1,17},{9,25},{17,1},{25,9},{2,18},{10... | collective-permute-start | bytes 1179656 | tf_op jit(solution)/shard_map/ppermute | solution.py:24
  259.4 27.4 %collective-permute-start.9 = (bf16[2,2,64,1536]{3,2,1,0:T(8,128)(2,1)}, bf16[2,2,64,1536]{3,2,1,0:T(8,128)(2,1)}, u32[]{:S(2)}, u32[]{:S(2)}) collective-permute-start(bf16[2,2,64,1536]{3,2,1,0:T(8,128)(2,1)} %pad_maximum_fusion.13), channel_id=1, source_target_pairs={{0,8},{8,0},{16,24},{24,16},{1,9},{9,1},{17,25},{25,17},{2,10},{10... | collective-permute-start | bytes 2359304 | tf_op jit(solution)/shard_map/ppermute | solution.py:24
  259.4 92.3 %collective-permute-start.14 = (bf16[2,2,1,32,1536]{4,3,2,1,0:T(8,128)(2,1)}, bf16[2,2,1,32,1536]{4,3,2,1,0:T(8,128)(2,1)}, u32[]{:S(2)}, u32[]{:S(2)}) collective-permute-start(bf16[2,2,1,32,1536]{4,3,2,1,0:T(8,128)(2,1)} %param.45), channel_id=1, source_target_pairs={{1,0},{2,1},{3,2},{4,3},{5,4},{6,5},{7,6},{9,8},{10,9},{11,10},{12... | collective-permute-start | bytes 1179656 | tf_op jit(solution)/shard_map/ppermute | solution.py:58
  261.5 90.2 %collective-permute-start.15 = (bf16[2,2,1,32,1536]{4,3,2,1,0:T(8,128)(2,1)}, bf16[2,2,1,32,1536]{4,3,2,1,0:T(8,128)(2,1)}, u32[]{:S(2)}, u32[]{:S(2)}) collective-permute-start(bf16[2,2,1,32,1536]{4,3,2,1,0:T(8,128)(2,1)} %param.45), channel_id=1, source_target_pairs={{0,1},{1,2},{2,3},{3,4},{4,5},{5,6},{6,7},{8,9},{9,10},{10,11},{11... | collective-permute-start | bytes 1179656 | tf_op jit(solution)/shard_map/ppermute | solution.py:57
  354.2 11.2 %collective-permute-start.11 = (bf16[2,64,1536]{2,1,0:T(8,128)(2,1)S(1)}, bf16[2,64,1536]{2,1,0:T(8,128)(2,1)S(1)}, u32[]{:S(2)}, u32[]{:S(2)}) collective-permute-start(bf16[2,64,1536]{2,1,0:T(8,128)(2,1)S(1)} %fusion.33), channel_id=1, source_target_pairs={{0,16},{8,24},{16,0},{24,8},{1,17},{9,25},{17,1},{25,9},{2,18},{10... | collective-permute-start | bytes 1179656 | tf_op jit(solution)/shard_map/ppermute | solution.py:24
  368.1 10.4 %collective-permute-start.16 = (bf16[2,64,1536]{2,1,0:T(8,128)(2,1)S(1)}, bf16[2,64,1536]{2,1,0:T(8,128)(2,1)S(1)}, u32[]{:S(2)}, u32[]{:S(2)}) collective-permute-start(bf16[2,64,1536]{2,1,0:T(8,128)(2,1)S(1)} %fusion.20), channel_id=1, source_target_pairs={{0,16},{8,24},{16,0},{24,8},{1,17},{9,25},{17,1},{25,9},{2,18},{10... | collective-permute-start | bytes 1179656 | tf_op jit(solution)/shard_map/ppermute | solution.py:24
  392.7 11.2 %collective-permute-start.19 = (bf16[2,64,1536]{2,1,0:T(8,128)(2,1)S(1)}, bf16[2,64,1536]{2,1,0:T(8,128)(2,1)S(1)}, u32[]{:S(2)}, u32[]{:S(2)}) collective-permute-start(bf16[2,64,1536]{2,1,0:T(8,128)(2,1)S(1)} %fusion.29), channel_id=1, source_target_pairs={{0,16},{8,24},{16,0},{24,8},{1,17},{9,25},{17,1},{25,9},{2,18},{10... | collective-permute-start | bytes 1179656 | tf_op jit(solution)/shard_map/ppermute | solution.py:24
  407.8 10.4 %collective-permute-start.20 = (bf16[2,64,1536]{2,1,0:T(8,128)(2,1)S(1)}, bf16[2,64,1536]{2,1,0:T(8,128)(2,1)S(1)}, u32[]{:S(2)}, u32[]{:S(2)}) collective-permute-start(bf16[2,64,1536]{2,1,0:T(8,128)(2,1)S(1)} %fusion.21), channel_id=1, source_target_pairs={{0,16},{8,24},{16,0},{24,8},{1,17},{9,25},{17,1},{25,9},{2,18},{10... | collective-permute-start | bytes 1179656 | tf_op jit(solution)/shard_map/ppermute | solution.py:24
  424.4 204.0 %reduce-scatter.14.cloned.1.call-start = ((), (), s32[]{:S(2)}) async-start(), calls=%async_computation.21 | async-start | bytes 1916928 | tf_op jit(solution)/shard_map/reduce_scatter | solution.py:67
  449.7 210.6 %reduce-scatter.12.cloned.1.call-start = ((), (), s32[]{:S(2)}) async-start(), calls=%async_computation.20 | async-start | bytes 3538944 | tf_op jit(solution)/shard_map/reduce_scatter | solution.py:67
  466.3 329.1 %reduce-scatter.10.cloned.1.call-start = ((), (), s32[]{:S(2)}) async-start(), calls=%async_computation.19 | async-start | bytes 7077888 | tf_op jit(solution)/shard_map/reduce_scatter | solution.py:67
  516.6 38.6 %all-to-all-start.6 = ((bf16[8,704,128]{2,1,0:T(8,128)(2,1)}), bf16[8,704,128]{2,1,0:T(8,128)(2,1)}, u32[]{:S(2)}, u32[]{:S(2)}) async-start(bf16[8,704,128]{2,1,0:T(8,128)(2,1)} %shard_map.349), calls=%async_computation.6 | async-start | bytes 2883584 | tf_op jit(solution)/shard_map/all_to_all | solution.py:629
  521.7 356.0 %reduce-scatter.6.cloned.1.call-start = ((), (), s32[]{:S(2)}) async-start(), calls=%async_computation.17 | async-start | bytes 3981312 | tf_op jit(solution)/shard_map/reduce_scatter | solution.py:67
  587.4 25.3 %collective-permute-start.12 = (bf16[2,2,1,32,1536]{4,3,2,1,0:T(8,128)(2,1)}, bf16[2,2,1,32,1536]{4,3,2,1,0:T(8,128)(2,1)}, u32[]{:S(2)}, u32[]{:S(2)}) collective-permute-start(bf16[2,2,1,32,1536]{4,3,2,1,0:T(8,128)(2,1)} %convert_element_type.264), channel_id=1, source_target_pairs={{0,1},{1,2},{2,3},{3,4},{4,5},{5,6},{6,7},{8,9},{9,10},{10,11},{11... | collective-permute-start | bytes 1179656 | tf_op jit(solution)/shard_map/ppermute | solution.py:57
  589.4 23.2 %collective-permute-start.13 = (bf16[2,2,1,32,1536]{4,3,2,1,0:T(8,128)(2,1)}, bf16[2,2,1,32,1536]{4,3,2,1,0:T(8,128)(2,1)}, u32[]{:S(2)}, u32[]{:S(2)}) collective-permute-start(bf16[2,2,1,32,1536]{4,3,2,1,0:T(8,128)(2,1)} %convert_element_type.264), channel_id=1, source_target_pairs={{1,0},{2,1},{3,2},{4,3},{5,4},{6,5},{7,6},{9,8},{10,9},{11,10},{12... | collective-permute-start | bytes 1179656 | tf_op jit(solution)/shard_map/ppermute | solution.py:58
  597.9 22.7 %collective-permute-start.26 = (bf16[192,384]{1,0:T(8,128)(2,1)}, bf16[192,384]{1,0:T(8,128)(2,1)S(1)}, u32[]{:S(2)}, u32[]{:S(2)}) collective-permute-start(bf16[192,384]{1,0:T(8,128)(2,1)} %reduce-scatter.8.cloned.1.call-done), channel_id=1, source_target_pairs={{0,0},{1,1},{2,8},{3,9},{4,16},{5,17},{6,24},{7,25},{8,2},{9,3},{1... | collective-permute-start | bytes 442376 | tf_op jit(solution)/shard_map/ppermute | solution.py:78
  628.3 33.6 %collective-permute-start.24 = (bf16[2,2,64,1536]{3,2,1,0:T(8,128)(2,1)}, bf16[2,2,64,1536]{3,2,1,0:T(8,128)(2,1)}, u32[]{:S(2)}, u32[]{:S(2)}) collective-permute-start(bf16[2,2,64,1536]{3,2,1,0:T(8,128)(2,1)} %pad_maximum_fusion.18), channel_id=1, source_target_pairs={{0,8},{8,0},{16,24},{24,16},{1,9},{9,1},{17,25},{25,17},{2,10},{10... | collective-permute-start | bytes 2359304 | tf_op jit(solution)/shard_map/ppermute | solution.py:24
  660.3 10.1 %collective-permute-start.27 = (bf16[512,384]{1,0:T(8,128)(2,1)}, bf16[512,384]{1,0:T(8,128)(2,1)S(1)}, u32[]{:S(2)}, u32[]{:S(2)}) collective-permute-start(bf16[512,384]{1,0:T(8,128)(2,1)} %reduce-scatter.12.cloned.1.call-done), channel_id=1, source_target_pairs={{0,0},{1,1},{2,8},{3,9},{4,16},{5,17},{6,24},{7,25},{8,2},{9,3},{1... | collective-permute-start | bytes 1179656 | tf_op jit(solution)/shard_map/ppermute | solution.py:78
  663.4 16.8 %collective-permute-start.25 = (bf16[2,64,1536]{2,1,0:T(8,128)(2,1)S(1)}, bf16[2,64,1536]{2,1,0:T(8,128)(2,1)S(1)}, u32[]{:S(2)}, u32[]{:S(2)}) collective-permute-start(bf16[2,64,1536]{2,1,0:T(8,128)(2,1)S(1)} %fusion.25), channel_id=1, source_target_pairs={{0,16},{8,24},{16,0},{24,8},{1,17},{9,25},{17,1},{25,9},{2,18},{10... | collective-permute-start | bytes 1179656 | tf_op jit(solution)/shard_map/ppermute | solution.py:24
  695.0 40.5 %all-to-all-start.7 = ((f32[32,7,128]{2,1,0:T(8,128)}), f32[32,7,128]{2,1,0:T(8,128)}, u32[]{:S(2)}, u32[]{:S(2)}) async-start(f32[32,7,128]{2,1,0:T(8,128)} %reshape.739), calls=%async_computation.12 | async-start | bytes 262144 | tf_op jit(solution)/shard_map/all_to_all | solution.py:694
  (117 other events, 2505.6 us)
Sparse Core Ops, SparseCore 0:
  21.9 64.5 all-gather.4
  89.2 85.7 all-gather.6
  177.2 106.1 all-gather.8
  285.4 62.0 all-gather.10
  424.6 65.0 reduce-scatter.7
  493.0 77.0 reduce-scatter.13
  574.1 86.1 reduce-scatter.11
  664.3 131.1 reduce-scatter.9
  799.5 78.1 reduce-scatter.5

commit v2 on v1

--- a/solution.py
+++ b/solution.py
@@ -38,17 +38,22 @@
     return blocks.reshape(value.shape)
 
 
-def frame_gather(value):
-    over = swap(value, 2)
+def beside(moved, work):
+    return (moved, None) if work is None else lax.optimization_barrier((moved, work))
+
+
+def frame_gather(value, work=None):
+    over, work = beside(swap(value, 2), work)
     pair = swap(jnp.stack([value, over]), 1)
-    return jnp.stack([value, pair[0], over, pair[1]])
-
-
-def frame_scatter(terms):
+    return jnp.stack([value, pair[0], over, pair[1]]), work
+
+
+def frame_scatter(terms, work=None):
     low = terms.astype(BF16)
     got = swap(jnp.stack([low[1], low[3]]), 1).astype(F32)
     far = (terms[2] + got[1]).astype(BF16)
-    return terms[0] + got[0] + swap(far, 2).astype(F32)
+    far, work = beside(swap(far, 2), work)
+    return terms[0] + got[0] + far.astype(F32), work
 
 
 def row_neighbours(block):
@@ -65,6 +70,61 @@
 
 def row_scatter(terms):
     return lax.psum_scatter(terms, ROW, scatter_dimension=0, tiled=True)
+
+
+def pick(blocks, index):
+    return lax.dynamic_index_in_dim(blocks, index, 0, keepdims=False)
+
+
+def line_scatter(terms):
+    if lax.axis_size("far") > 1:
+        return row_scatter(terms.reshape(-1, terms.shape[-1])).astype(F32)
+    place = lax.axis_index("row")
+    z, x = place // 2, place % 2
+    last = RING // 2 - 1
+    blocks = terms.reshape(last + 1, 2, -1, terms.shape[-1])
+    mine = lax.dynamic_index_in_dim(blocks, x, 1, keepdims=False)
+    other = lax.dynamic_index_in_dim(blocks, 1 - x, 1, keepdims=False)
+    got = lax.ppermute(other, "row", [(i, i ^ 1) for i in range(RING)])
+    both = (mine.astype(F32) + got.astype(F32)).astype(BF16)
+    up = down = None
+    for k in range(last, 0, -1):
+        send_up = pick(both, jnp.minimum(z + k, last))
+        send_down = pick(both, jnp.maximum(z - k, 0))
+        if up is not None:
+            send_up = (send_up.astype(F32) + up.astype(F32)).astype(BF16)
+            send_down = (send_down.astype(F32) + down.astype(F32)).astype(BF16)
+        up = lax.ppermute(send_up, "row", [(i, i + 2) for i in range(RING) if i // 2 + k <= last])
+        down = lax.ppermute(send_down, "row", [(i, i - 2) for i in range(RING) if i // 2 - k >= 0])
+    return pick(both, z).astype(F32) + up.astype(F32) + down.astype(F32)
+
+
+def line_gather(block):
+    if lax.axis_size("far") > 1:
+        return row_gather(block)
+    place = lax.axis_index("row")
+    z, x = place // 2, place % 2
+    last = RING // 2 - 1
+    other = lax.ppermute(block, "row", [(i, i ^ 1) for i in range(RING)])
+    pair = jnp.where(x == 0, jnp.stack([block, other]), jnp.stack([other, block]))
+    below, above = [pair], [pair]
+    for k in range(1, last + 1):
+        below.append(lax.ppermute(below[-1], "row", [(i, i + 2) for i in range(RING - 2) if i // 2 >= k - 1]))
+        above.append(lax.ppermute(above[-1], "row", [(i, i - 2) for i in range(2, RING) if i // 2 + k - 1 <= last]))
+    line = jnp.stack(below[:0:-1] + above)
+    line = lax.dynamic_slice_in_dim(line, last - z, last + 1, 0)
+    return line.reshape(-1, block.shape[1])
+
+
+def to_chunks(value, size):
+    blocks, rows, columns = value.shape
+    value = value.reshape(blocks, rows, columns // size, size).transpose(0, 2, 1, 3)
+    return value.reshape(blocks, -1, size)
+
+
+def from_chunks(value, rows):
+    blocks, _, size = value.shape
+    return value.reshape(blocks, -1, rows, size).transpose(0, 2, 1, 3).reshape(blocks * rows, -1)
 
 
 def to_owner(block):
@@ -212,8 +272,63 @@
     return lax.dot_general(a, b, (((1,), (0,)), ((), ())), preferred_element_type=F32)
 
 
-def dot_tn(a, b):
-    return lax.dot_general(a, b, (((0,), (0,)), ((), ())), preferred_element_type=F32)
+def turned(value):
+    return value.astype(F32).T.astype(BF16)
+
+
+def ff_kernel(hidden_ref, dz_ref, f_in_ref, dgu_ref, out_ref):
+    n_rows = out_ref.shape[0]
+    part = n_rows // 4
+    left = turned(hidden_ref[...])
+    tile = left.shape[0] // part
+    for c in range(4):
+        for j in range(3):
+            cut = 384 * c + 128 * j
+            block = dot_nn(left, dz_ref[:, cut : cut + 128]).astype(BF16)
+            for h in range(part):
+                out_ref[c * part + h, tile * j : tile * j + tile, :] = block[tile * h : tile * h + tile]
+    base = 3 * tile
+    left = turned(f_in_ref[...])
+    tile = left.shape[0] // n_rows
+    for j in range(0, dgu_ref.shape[1] // 128, 2):
+        block = dot_nn(left, dgu_ref[:, 128 * j : 128 * j + 256]).astype(BF16)
+        for r in range(n_rows):
+            for e in range(2):
+                at = base + tile * (j + e)
+                out_ref[r, at : at + tile, :] = block[tile * r : tile * r + tile, 128 * e : 128 * e + 128]
+
+
+def out_kernel(attn_ref, dy_ref, dk_ref, dv_ref, dot_ref, out_ref):
+    n_rows = out_ref.shape[0]
+    part = n_rows // 4
+    wide = dk_ref.shape[0] // n_rows
+    tall = 2 * wide + 16
+    chunks = dk_ref.shape[1] // 128
+    for r in range(n_rows):
+        for j in range(chunks):
+            cut = slice(128 * j, 128 * j + 128)
+            block = jnp.concatenate(
+                [
+                    dk_ref[wide * r : wide * r + wide, cut],
+                    dv_ref[wide * r : wide * r + wide, cut],
+                    jnp.broadcast_to(dot_ref[:, cut], (16, 128)),
+                ]
+            )
+            out_ref[r, tall * j : tall * j + tall, :] = block.astype(BF16)
+    base = tall * chunks
+    left = turned(attn_ref[...])
+    tile = left.shape[0] // part
+    for c in range(4):
+        for j in range(3):
+            cut = 384 * c + 128 * j
+            block = dot_nn(left, dy_ref[:, cut : cut + 128]).astype(BF16)
+            for h in range(part):
+                at = base + tile * j
+                out_ref[c * part + h, at : at + tile, :] = block[tile * h : tile * h + tile]
+
+
+def dot_tt(a, b):
+    return lax.dot_general(a, b, (((0,), (1,)), ((), ())), preferred_element_type=F32)
 
 
 def query_block(ref, slot, i, base):
@@ -297,7 +412,7 @@
 
 def cross_probs(kc, q, bias, lane, e):
     qm = jnp.where((lane < 64) == (e == 0), q, jnp.zeros_like(q))
-    s = jnp.where(bias > 0.0, dot_nt(kc, qm) * (HDIM ** (-0.5)), NEG)
+    s = jnp.where(bias > 0.0, dot_tt(kc, qm) * (HDIM ** (-0.5)), NEG)
     p = jnp.exp(s - jnp.max(s, axis=0, keepdims=True))
     return p / jnp.sum(p, axis=0, keepdims=True), qm
 
@@ -309,7 +424,7 @@
     outs = []
     for e in range(2):
         p, _ = cross_probs(kc_ref[...], q, bias, lane, e)
-        outs.append(dot_tn(p.astype(BF16), vc_ref[...]))
+        outs.append(dot_tt(p.astype(BF16), vc_ref[...]))
     o_ref[...] = jnp.where(lane < 64, outs[0], outs[1]).reshape(4, 1, 64, 128)
 
 
@@ -323,13 +438,11 @@
     for e in range(2):
         p, qm = cross_probs(kc, q, bias, lane, e)
         dm = jnp.where((lane < 64) == (e == 0), d, jnp.zeros_like(d))
-        dp = dot_nt(vc, dm)
+        dp = dot_tt(vc, dm)
         dt = (p * (dp - jnp.sum(p * dp, axis=0, keepdims=True))).astype(BF16)
-        dqs.append(dot_tn(dt, kc))
-        dk = dk + lax.dot_general(qm, dt, (((0,), (1,)), ((), ())), preferred_element_type=F32)
-        dv = dv + lax.dot_general(
-            dm, p.astype(BF16), (((0,), (1,)), ((), ())), preferred_element_type=F32
-        )
+        dqs.append(dot_tt(dt, kc))
+        dk = dk + dot_tt(qm, dt)
+        dv = dv + dot_tt(dm, p.astype(BF16))
     dq = jnp.where(lane < 64, dqs[0], dqs[1]) * (HDIM ** (-0.5))
     dq_ref[...] = dq.reshape(4, 1, 64, 128)
     dk_ref[...] = dk * (HDIM ** (-0.5))
@@ -352,10 +465,9 @@
 
 def cross_call(kernel, outs, specs, *args):
     token = pl.BlockSpec((4, 1, 64, 128), lambda c, h: (0, c, 0, h))
-    key = pl.BlockSpec((256, 128), lambda c, h: (c, h))
     bias = pl.BlockSpec((256, 1), lambda c, h: (c, 0))
     back = pl.BlockSpec((128, 256), lambda c, h: (h, c))
-    kinds = {"t": token, "k": key, "b": bias, "o": back}
+    kinds = {"t": token, "b": bias, "o": back}
     return pl.pallas_call(
         kernel,
         grid=(2, 3),
@@ -431,20 +543,25 @@
     caps = caption.shape[1]
     share = width // n_all
 
+    rows = w_query.shape[0]
+    cap2 = caption.reshape(clips * caps, width)
+
     def by_columns(parts):
-        rows = parts[0].shape[0]
         cut = jnp.concatenate([w.reshape(rows, group, -1) for w in parts], axis=2)
         cut = lax.all_to_all(cut.transpose(1, 0, 2), "frame", 0, 0)
         full = row_gather(cut.reshape(group * rows, -1))
         full = full.reshape(n_rows, group, rows, -1).transpose(1, 0, 2, 3)
         return full.reshape(n_rows * group * rows, -1)
 
+    def cap_columns(weight):
+        return lax.dot_general(weight, cap2, (((0,), (1,)), ((), ())), preferred_element_type=F32).astype(BF16)
+
+    w_dn = line_gather(w_down)
     w_qkv = by_columns([w_query, w_key, w_value])
-    stack = jnp.concatenate([w_cap_key.T, w_cap_value.T, w_out], axis=0)
-    stack = row_gather(stack).reshape(n_rows, 3, -1, width).transpose(1, 0, 2, 3)
-    w_ck, w_cv, w_o = stack.reshape(3, heads_w, width)
+    side = row_gather(jnp.concatenate([cap_columns(w_cap_key), cap_columns(w_cap_value), w_out], axis=1))
+    tokens_c = clips * caps
+    k_pre_t, v_cap_t, w_o = side[:, :tokens_c], side[:, tokens_c : 2 * tokens_c], side[:, 2 * tokens_c :]
     w_gu = by_columns([w_gate, w_up])
-    w_dn = row_gather(w_down)
 
     half_width = width // 2
     frequencies = jnp.exp(-math.log(THETA) * jnp.arange(half_width, dtype=F32) / half_width)
@@ -483,12 +600,13 @@
 
     x_own = tokens.reshape(clips, local, width)
     x_flat = x_own.astype(F32)
-    x_group = frame_gather(x_own)
+    x_group, _ = frame_gather(x_own)
 
     def pre_piece(x_in, gain, scale_in):
         return rms_norm(x_in, gain) * (1.0 + scale_in[:, None, :])
 
     h_in = pre_piece(x_group.astype(F32), gains[0], scale_a).astype(BF16).reshape(count, width)
+    h_in = lax.optimization_barrier(h_in)
     _, pre_back = jax.vjp(pre_piece, x_flat, gains[0], scale_a)
     qkv = mm(h_in, w_qkv)
     q_zero, k_zero = qkv[:, :heads_w], qkv[:, heads_w : 2 * heads_w]
@@ -518,28 +636,29 @@
     )
     o_back = lax.all_to_all(o_pack, "row", 0, 0)
 
-    cap2 = caption.reshape(clips * caps, width)
     usable = (jnp.arange(caps)[None, :] < cap_len[:, None]) & (cap_mask > 0)
     bias = usable.astype(F32).reshape(clips * caps, 1)
-    k_pre = lax.dot_general(cap2, w_ck, (((1,), (1,)), ((), ())), preferred_element_type=F32)
-    v_cap = lax.dot_general(cap2, w_cv, (((1,), (1,)), ((), ())), preferred_element_type=F32).astype(BF16)
-    r_cap = lax.rsqrt(frame_sum(jnp.sum(k_pre * k_pre, axis=1)[None]) / width + EPS)
-    k_cap = (k_pre * r_cap.T * own_gains[2]).astype(BF16)
+    k_pre_t = k_pre_t.astype(F32)
+    gain_cap = own_gains[2][:, None]
+    r_cap = lax.rsqrt(frame_sum(jnp.sum(k_pre_t * k_pre_t, axis=0, keepdims=True)) / width + EPS)
+    k_cap_t = (k_pre_t * r_cap * gain_cap).astype(BF16)
     q_cap4 = q_cap.reshape(group, clips, local, heads_w)
     (out_cross,) = cross_call(
-        cross_kernel, [shaped(q_cap4.shape)], ("tkkb", "t"), q_cap4, k_cap, v_cap, bias
-    )
+        cross_kernel, [shaped(q_cap4.shape)], ("toob", "t"), q_cap4, k_cap_t, v_cap_t, bias
+    )
+    o_back, out_cross = beside(o_back, out_cross)
     out_cross = out_cross.reshape(count, heads_w)
     (attn_mix,) = call(mix_kernel, [shaped((count, heads_w), BF16)], o_back, out_cross, own_gate)
 
-    y_one = frame_scatter(mm(attn_mix, w_o).reshape(group, clips, local, width))
+    y_one, _ = frame_scatter(mm(attn_mix, w_o).reshape(group, clips, local, width))
 
     def mid_piece(x_in, y_in, gain_two, gate_in, gain_three, scale_in):
         h_mid = x_in + jnp.tanh(gate_in)[:, None, :] * rms_norm(y_in, gain_two)
         return (h_mid, rms_norm(h_mid, gain_three) * (1.0 + scale_in[:, None, :]))
 
     (h_mid, f_in32), mid_back = jax.vjp(mid_piece, x_flat, y_one, gains[1], gate_a, gains[2], scale_f)
-    f_in = frame_gather(f_in32.astype(BF16)).reshape(count, width)
+    f_in, _ = frame_gather(f_in32.astype(BF16))
+    f_in = f_in.reshape(count, width)
     gate_up = mm(f_in, w_gu)
 
     def act_piece(gate_in, up_in):
@@ -547,7 +666,7 @@
 
     hidden32, act_back = jax.vjp(act_piece, gate_up[:, :ff_w], gate_up[:, ff_w:])
     hidden = hidden32.astype(BF16)
-    z_out = frame_scatter(mm(hidden, w_dn).reshape(group, clips, local, width))
+    z_out, _ = frame_scatter(mm(hidden, w_dn).reshape(group, clips, local, width))
 
     def end_piece(h_in_mid, z_in, gain_four, gate_in):
         return h_in_mid + jnp.tanh(gate_in)[:, None, :] * rms_norm(z_in, gain_four)
@@ -562,27 +681,30 @@
     d_above = jnp.sum(g_center * above, axis=(0, 1, 2, 3))
     d_below = jnp.sum(g_center * below, axis=(0, 1, 2, 3))
     d_h_end, d_z, d_g_four, d_gate_f = end_back(d_y.reshape(clips, local, width))
-    d_z_all = frame_gather(d_z.astype(BF16)).reshape(count, width)
+    d_z_all, _ = frame_gather(d_z.astype(BF16))
+    d_z_all = d_z_all.reshape(count, width)
     d_hidden = lax.dot_general(d_z_all, w_dn, (((1,), (1,)), ((), ())), preferred_element_type=F32)
     d_gu = jnp.concatenate([d.astype(BF16) for d in act_back(d_hidden)], axis=1)
     d_f_in = lax.dot_general(d_gu, w_gu, (((1,), (1,)), ((), ())), preferred_element_type=F32)
-    d_f_in = frame_scatter(d_f_in.reshape(group, clips, local, width))
-
     def term(left, right):
         return lax.dot_general(left, right, (((0,), (0,)), ((), ())), preferred_element_type=F32).astype(BF16)
 
-    def term_by_owner(left, right):
-        return jnp.concatenate(
-            [term(left, right[:, c * heads_w : (c + 1) * heads_w]) for c in range(group)], axis=0
-        )
-
-    sum_down = to_owner(row_scatter(term_by_owner(hidden, d_z_all)))
-    sum_gu = row_scatter(term(f_in, d_gu))
-
+    ff_rows = (w_down.shape[0] * group * (heads_w // 128), width // n_rows * (2 * ff_w // 128))
+    (ff_terms,) = call(
+        ff_kernel,
+        [shaped((n_rows, sum(ff_rows), 128), BF16)],
+        hidden,
+        d_z_all,
+        f_in,
+        d_gu,
+        flops=6 * count * width * ff_w,
+    )
+    d_f_in, ff_terms = frame_scatter(d_f_in.reshape(group, clips, local, width), ff_terms)
+    ff_sum = row_scatter(ff_terms.reshape(-1, 128))
     d_x_mid, d_y_one, d_g_two, d_gate_a, d_g_three, d_scale_f = mid_back((d_h_end, d_f_in))
-    d_y_group = frame_gather(d_y_one.astype(BF16)).reshape(count, width)
+    d_y_group, _ = frame_gather(d_y_one.astype(BF16))
+    d_y_group = d_y_group.reshape(count, width)
     d_attn = lax.dot_general(d_y_group, w_o, (((1,), (1,)), ((), ())), preferred_element_type=F32)
-    sum_out = to_owner(row_scatter(term_by_owner(attn_mix, d_y_group)))
 
     d_pack, d_cross = call(
         split_kernel, [shaped((RING, 192, 128), BF16), shaped((count, heads_w), BF16)], d_attn, own_gate
@@ -592,13 +714,14 @@
     d_q_cross, d_k_cap, d_v_cap = cross_call(
         cross_back_kernel,
         [shaped(q_cap4.shape), shaped((heads_w, clips * caps)), shaped((heads_w, clips * caps))],
-        ("tkkbt", "too"),
+        ("toobt", "too"),
         q_cap4,
-        k_cap,
-        v_cap,
+        k_cap_t,
+        v_cap_t,
         bias,
         d_cross.reshape(q_cap4.shape),
     )
+    d_got, (d_q_cross, d_k_cap, d_v_cap) = beside(d_got, (d_q_cross, d_k_cap, d_v_cap))
     back_scratch = [pltpu.VMEM((keys, 128), F32)]
     if n_far == 1:
         (d_send,) = call(
@@ -626,7 +749,24 @@
         )
         d_kv = lax.psum_scatter(d_kv, "far", scatter_dimension=0, tiled=True)
         d_send = jnp.concatenate([d_kv, d_q], axis=1)
-    d_recv = lax.all_to_all(d_send, "row", 0, 0)
+    cap_dot = frame_sum(jnp.sum(d_k_cap * gain_cap * k_pre_t, axis=0, keepdims=True))
+    wide = heads_w // n_rows
+    tile = width // n_rows
+    cut = (2 * wide + 16) * (clips * caps // 128)
+    (out_terms,) = call(
+        out_kernel,
+        [shaped((n_rows, cut + tile * (heads_w // 128), 128), BF16)],
+        attn_mix,
+        d_y_group,
+        d_k_cap,
+        d_v_cap,
+        cap_dot,
+        flops=2 * count * width * heads_w,
+    )
+    d_recv, (out_terms, output, d_above, d_below) = beside(
+        lax.all_to_all(d_send, "row", 0, 0), (out_terms, output, d_above, d_below)
+    )
+    out_sum = line_scatter(out_terms)
     d_qn, d_kn, d_v = call(
         back_kernel,
         [shaped((count, heads_w)), shaped((count, heads_w)), shaped((count, heads_w), BF16)],
@@ -644,31 +784,10 @@
     d_k_low = (rk * a_k - k_zero * (rk * rk * rk * dots[:, 1:2])).astype(BF16)
     d_qkv = jnp.concatenate([d_q_low, d_k_low, d_v], axis=1)
     d_h_in = lax.dot_general(d_qkv, w_qkv, (((1,), (1,)), ((), ())), preferred_element_type=F32)
-    d_h_in = frame_scatter(d_h_in.reshape(group, clips, local, width))
-    sum_qkv = row_scatter(term(h_in, d_qkv))
+    qkv_sum = line_scatter(term(h_in, d_qkv).reshape(n_rows, -1, 3 * heads_w))
+    d_h_in, _ = frame_scatter(d_h_in.reshape(group, clips, local, width))
     d_x_pre, d_g_zero, d_scale_a = pre_back(d_h_in)
     grad_tokens = (d_x_pre + d_x_mid).reshape(tokens.shape)
-
-    k_pre_t = k_pre.T
-    gain_cap = own_gains[2][:, None]
-    cap_dot = frame_sum(jnp.sum(d_k_cap * gain_cap * k_pre_t, axis=0, keepdims=True))
-    wide = heads_w // n_rows
-    cap_terms = jnp.stack([d_k_cap, d_v_cap]).reshape(2, n_rows, wide, clips * caps)
-    cap_terms = cap_terms.transpose(1, 0, 2, 3).reshape(n_rows, 2 * wide, clips * caps)
-    extra = jnp.broadcast_to(jnp.pad(cap_dot, ((0, 7), (0, 0)))[None], (n_rows, 8, clips * caps))
-    cap_terms = jnp.concatenate([cap_terms, extra], axis=1).reshape(n_rows * (2 * wide + 8), -1)
-    cap_sum = row_scatter(cap_terms)
-    d_k_own, d_v_own, cap_dot = cap_sum[:wide], cap_sum[wide : 2 * wide], cap_sum[2 * wide : 2 * wide + 1]
-    k_own = lax.dynamic_slice(k_pre_t, (my_row * wide, 0), (wide, clips * caps))
-    g_own = lax.dynamic_slice(own_gains, (2, my_row * wide), (1, wide)).T
-    d_g_cap = jnp.sum(d_k_own * k_own * r_cap, axis=1)
-    d_k_zero_cap = (r_cap * g_own * d_k_own - k_own * (r_cap * r_cap * r_cap * cap_dot / width)).astype(BF16)
-
-    def cap_weight(d):
-        return lax.dot_general(cap2, d, (((0,), (1,)), ((), ())), preferred_element_type=F32)
-
-    d_w_cap_key = cap_weight(d_k_zero_cap)
-    d_w_cap_value = cap_weight(d_v_own.astype(BF16))
 
     def spread(block):
         return lax.dynamic_update_slice(jnp.zeros((width,), F32), block, (me * heads_w,))
@@ -697,21 +816,40 @@
     d_w_mod = lax.dot_general(
         step_embed, d_mod.astype(BF16), (((0,), (0,)), ((), ())), preferred_element_type=F32
     )
+    ff_sum, d_w_mod = beside(ff_sum, d_w_mod)
+    mine = w_down.shape[0] * group
+    sum_down = to_owner(from_chunks(ff_sum[None, : ff_rows[0]], mine)).astype(F32)
+    sum_gate, sum_up = jnp.split(ff_sum[ff_rows[0] :], 2)
+    cap_sum = from_chunks(out_sum[None, :cut], 2 * wide + 16)
+    sum_out = to_owner(from_chunks(out_sum[None, cut:].astype(BF16), tile)).astype(F32)
+
+    def result(block):
+        return from_chunks(block[None], tile).astype(F32)
+
+    d_k_own, d_v_own, cap_dot = cap_sum[:wide], cap_sum[wide : 2 * wide], cap_sum[2 * wide : 2 * wide + 1]
+    k_own = lax.dynamic_slice(k_pre_t, (my_row * wide, 0), (wide, clips * caps))
+    g_own = lax.dynamic_slice(gain_cap, (my_row * wide, 0), (wide, 1))
+    d_g_cap = jnp.sum(d_k_own * k_own * r_cap, axis=1)
+    d_k_zero_cap = (r_cap * g_own * d_k_own - k_own * (r_cap * r_cap * r_cap * cap_dot / width)).astype(BF16)
+
+    def cap_weight(d):
+        return lax.dot_general(cap2, d, (((0,), (1,)), ((), ())), preferred_element_type=F32)
+
+    d_w_cap_key = cap_weight(d_k_zero_cap)
+    d_w_cap_value = cap_weight(d_v_own.astype(BF16))
     d_gains = jnp.concatenate([rest[:6], d_g_cap[None]], axis=0)
     d_mixes = rest[6:]
 
-    sum_qkv = sum_qkv.astype(F32)
-    sum_gu = sum_gu.astype(F32)
     return (
         output,
         grad_tokens,
-        sum_qkv[:, :heads_w],
-        sum_qkv[:, heads_w : 2 * heads_w],
-        sum_qkv[:, 2 * heads_w :],
-        sum_out.astype(F32),
-        sum_gu[:, :ff_w],
-        sum_gu[:, ff_w:],
-        sum_down.astype(F32),
+        qkv_sum[:, :heads_w],
+        qkv_sum[:, heads_w : 2 * heads_w],
+        qkv_sum[:, 2 * heads_w :],
+        sum_out,
+        result(sum_gate),
+        result(sum_up),
+        sum_down,
         d_w_cap_key,
         d_w_cap_value,
         d_w_mod,

time: 898 us -> 700 us (0.78)
  the two profiles are of different devices: /device:TPU:2 before, /device:TPU:6 now
where the time goes in v2:
time: 700 us; the launch traced here: 688 us
  waiting for transfers between devices  244 us (35%)
  starting transfers between devices  142 us (20%)
  local copies, waits for them, and re-layouts  90.1 us (13%)
  Pallas kernels  89 us (13%)
  other arithmetic  67.8 us (10%)
  matrix products  28.8 us (4%)
  between operations  16.9 us (2%)
  blocking collectives  10 us (1%)
    pallas_call x8, Pallas kernels, call(): pl.pallas_call(kernel, out_shape=outs, in_specs=[spec] * len(args), out_s...  78.1 us
    ppermute x24, waiting for transfers between devices, swap(): lax.ppermute(value, 'frame', [(i, i ^ bits) for i in range(lax.axis_size(...  58.1 us
    all_to_all x1, waiting for transfers between devices, body(): got = lax.all_to_all(send, 'row', 0, 0)  33.9 us
    unnamed x245, local copies, waits for them, and re-layouts  31.3 us
    ppermute x3, waiting for transfers between devices, line_gather(): lax.ppermute(below[-1], 'row', [(i, i + 2) for i in range(RING - 2) if i...  30.5 us
    ppermute x2, waiting for transfers between devices, line_scatter(): got = lax.ppermute(other, 'row', [(i, i ^ 1) for i in range(RING)])  28.9 us
    all_to_all x1, starting transfers between devices, body(): got = lax.all_to_all(send, 'row', 0, 0)  26.6 us
    ppermute x2, waiting for transfers between devices, row_neighbours(): below = lax.ppermute(block, ROW, [(b, a) for a, b in forward])  21.9 us
  transfers between devices with their start and end apart: 62, of which 26 were waited for; matrix products, arithmetic and copies ran while one was open for 22% of the time, Pallas kernels for 13%

profile of v2, /device:TPU:6, one launch (start us, length us, event | category | flops | bytes accessed | tf_op | source)
XLA Modules:
  0.0 687.9 jit_solution(10453943235618125001)
XLA Ops:
  10.6 10.0 %all_to_all.40 = bf16[4,48,1152]{2,1,0:T(8,128)(2,1)} all-to-all(bf16[4,48,1152]{2,1,0:T(8,128)(2,1)S(1)} %copy.194), channel_id=1, replica_groups=mesh['frame'=4,'row'=8] {'frame'}, dimensions={0} | all-to-all | bytes 884736 | tf_op jit(solution)/shard_map/all_to_all | solution.py:551
  22.5 6.3 all-to-all-start
  41.5 5.9 all-to-all-start.4
  55.7 5.5 collective-permute-start.13
  64.6 30.5 %collective-permute-done.13 = bf16[2,128,1536]{2,1,0:T(8,128)(2,1)} collective-permute-done((bf16[2,128,1536]{2,1,0:T(8,128)(2,1)}, bf16[2,128,1536]{2,1,0:T(8,128)(2,1)}, u32[]{:S(2)}, u32[]{:S(2)}) %collective-permute-start.13) | collective-permute-done | bytes 786464 | tf_op jit(solution)/shard_map/ppermute | solution.py:112
  96.6 6.5 all-gather.4.cloned.1.call-done
  119.6 5.4 shard_map.344
  125.1 26.6 %all-to-all-start.2 = ((bf16[8,704,128]{2,1,0:T(8,128)(2,1)}), bf16[8,704,128]{2,1,0:T(8,128)(2,1)S(1)}, u32[]{:S(2)}, u32[]{:S(2)}) async-start(bf16[8,704,128]{2,1,0:T(8,128)(2,1)} %get-tuple-element.42), calls=%async_computation.2 | async-start | bytes 2883584 | tf_op jit(solution)/shard_map/all_to_all | solution.py:624
  173.3 33.9 %all-to-all-done.2.kv_ref.q_ref = bf16[8,704,128]{2,1,0:T(8,128)(2,1)S(1)} async-done(((bf16[8,704,128]{2,1,0:T(8,128)(2,1)}), bf16[8,704,128]{2,1,0:T(8,128)(2,1)S(1)}, u32[]{:S(2)}, u32[]{:S(2)}) %all-to-all-start.2) | async-done | bytes 1441824 | tf_op jit(solution)/shard_map/all_to_all | solution.py:624
  208.3 21.0 %shard_map.345 = (bf16[8,192,128]{2,1,0:T(8,128)(2,1)}, f32[12,64,256]{2,1,0:T(8,128)}, f32[12,1,256]{2,1,0:T(1,128)}) custom-call(bf16[8,704,128]{2,1,0:T(8,128)(2,1)} %copy-done.42, bf16[8,704,128]{2,1,0:T(8,128)(2,1)} %copy-done.42), custom_call_target="tpu_custom_call" | custom-call | flops 3221225472 | bytes 4075520 | tf_op jit(solution)/shard_map/pallas_call | solution.py:455
  229.4 7.8 %all-to-all-start.3 = ((bf16[8,192,128]{2,1,0:T(8,128)(2,1)}), bf16[8,192,128]{2,1,0:T(8,128)(2,1)S(1)}, u32[]{:S(2)}, u32[]{:S(2)}) async-start(bf16[8,192,128]{2,1,0:T(8,128)(2,1)} %get-tuple-element.43), calls=%async_computation.3 | async-start | bytes 786432 | tf_op jit(solution)/shard_map/all_to_all | solution.py:637
  245.4 13.2 %all-to-all-done.3.o_ref = bf16[8,192,128]{2,1,0:T(8,128)(2,1)S(1)} async-done(((bf16[8,192,128]{2,1,0:T(8,128)(2,1)}), bf16[8,192,128]{2,1,0:T(8,128)(2,1)S(1)}, u32[]{:S(2)}, u32[]{:S(2)}) %all-to-all-start.3) | async-done | bytes 393248 | tf_op jit(solution)/shard_map/all_to_all | solution.py:637
  268.9 9.3 %collective-permute-done.9 = bf16[2,64,1536]{2,1,0:T(8,128)(2,1)S(1)} collective-permute-done((bf16[2,64,1536]{2,1,0:T(8,128)(2,1)S(1)}, bf16[2,64,1536]{2,1,0:T(8,128)(2,1)S(1)}, u32[]{:S(2)}, u32[]{:S(2)}) %collective-permute-start.9) | collective-permute-done | bytes 393248 | tf_op jit(solution)/shard_map/ppermute | solution.py:24
  279.9 10.3 %collective-permute-done.10 = bf16[2,64,1536]{2,1,0:T(8,128)(2,1)S(1)} collective-permute-done((bf16[2,64,1536]{2,1,0:T(8,128)(2,1)S(1)}, bf16[2,64,1536]{2,1,0:T(8,128)(2,1)S(1)}, u32[]{:S(2)}, u32[]{:S(2)}) %collective-permute-start.10) | collective-permute-done | bytes 393248 | tf_op jit(solution)/shard_map/ppermute | solution.py:24
  314.1 10.8 %collective-permute-done.20 = bf16[2,64,1536]{2,1,0:T(8,128)(2,1)S(1)} collective-permute-done((bf16[2,64,1536]{2,1,0:T(8,128)(2,1)S(1)}, bf16[2,64,1536]{2,1,0:T(8,128)(2,1)S(1)}, u32[]{:S(2)}, u32[]{:S(2)}) %collective-permute-start.20) | collective-permute-done | bytes 393248 | tf_op jit(solution)/shard_map/ppermute | solution.py:24
  328.2 10.1 %collective-permute-done.21 = bf16[2,64,1536]{2,1,0:T(8,128)(2,1)S(1)} collective-permute-done((bf16[2,64,1536]{2,1,0:T(8,128)(2,1)S(1)}, bf16[2,64,1536]{2,1,0:T(8,128)(2,1)S(1)}, u32[]{:S(2)}, u32[]{:S(2)}) %collective-permute-start.21) | collective-permute-done | bytes 393248 | tf_op jit(solution)/shard_map/ppermute | solution.py:24
  350.4 13.3 %shard_map.348 = bf16[8,4608,128]{2,1,0:T(8,128)(2,1)} custom-call(bf16[512,1024]{1,0:T(8,128)(2,1)} %copy-done.43, bf16[512,1536]{1,0:T(8,128)(2,1)} %bitcast.406, bf16[512,1536]{1,0:T(8,128)(2,1)} %bitcast.404, bf16[512,2048]{1,0:T(8,128)(2,1)} %pad_maximum_fusion.dgu_ref), custom_call_target="tpu_custom_call" | custom-call | flops 4831838208 | bytes 15728640 | tf_op jit(solution)/shard_map/pallas_call | solution.py:455
  370.2 9.3 %collective-permute-done.25 = bf16[2,64,1536]{2,1,0:T(8,128)(2,1)S(1)} collective-permute-done((bf16[2,64,1536]{2,1,0:T(8,128)(2,1)S(1)}, bf16[2,64,1536]{2,1,0:T(8,128)(2,1)S(1)}, u32[]{:S(2)}, u32[]{:S(2)}) %collective-permute-start.25) | collective-permute-done | bytes 393248 | tf_op jit(solution)/shard_map/ppermute | solution.py:24
  389.1 4.9 all-to-all-start.5
  395.9 6.8 shard_map.350
  404.6 12.0 %all-to-all-done.5.do_ref = bf16[8,192,128]{2,1,0:T(8,128)(2,1)} async-done(((bf16[8,192,128]{2,1,0:T(8,128)(2,1)}), bf16[8,192,128]{2,1,0:T(8,128)(2,1)}, u32[]{:S(2)}, u32[]{:S(2)}) %all-to-all-start.5) | async-done | bytes 393248 | tf_op jit(solution)/shard_map/all_to_all | solution.py:712
  416.6 23.3 %shard_map.351 = bf16[8,704,128]{2,1,0:T(8,128)(2,1)} custom-call(bf16[8,704,128]{2,1,0:T(8,128)(2,1)} %copy-done.42, bf16[8,704,128]{2,1,0:T(8,128)(2,1)} %copy-done.42, bf16[8,192,128]{2,1,0:T(8,128)(2,1)} %all-to-all-done.5.do_ref, f32[12,64,256]{2,1,0:T(8,128)} %get-tuple-element.54.ot_ref, f32[12,1,256]{2,1,0:T(1,128)} %get-tuple-element.55.lse_ref), custom_call_target="tpu_custom_call" | custom-call | flops 8053063680 | bytes 5517312 | tf_op jit(solution)/shard_map/pallas_call | solution.py:455
  440.0 4.9 all-to-all-start.6
  459.0 21.9 %collective-permute-done.30 = bf16[2,2,1,32,1536]{4,3,2,1,0:T(8,128)(2,1)S(1)} collective-permute-done((bf16[2,2,1,32,1536]{4,3,2,1,0:T(8,128)(2,1)}, bf16[2,2,1,32,1536]{4,3,2,1,0:T(8,128)(2,1)S(1)}, u32[]{:S(2)}, u32[]{:S(2)}) %collective-permute-start.30) | collective-permute-done | bytes 393248 | tf_op jit(solution)/shard_map/ppermute | solution.py:63
  481.0 8.8 %collective-permute-done.29 = bf16[2,2,1,32,1536]{4,3,2,1,0:T(8,128)(2,1)} collective-permute-done((bf16[2,2,1,32,1536]{4,3,2,1,0:T(8,128)(2,1)}, bf16[2,2,1,32,1536]{4,3,2,1,0:T(8,128)(2,1)}, u32[]{:S(2)}, u32[]{:S(2)}) %collective-permute-start.29) | collective-permute-done | bytes 393248 | tf_op jit(solution)/shard_map/ppermute | solution.py:62
  504.6 5.9 shard_map.353
  541.2 17.7 %collective-permute-done.42 = bf16[4,1024,128]{2,1,0:T(8,128)(2,1)} collective-permute-done((bf16[4,1024,128]{2,1,0:T(8,128)(2,1)}, bf16[4,1024,128]{2,1,0:T(8,128)(2,1)}, u32[]{:S(2)}, u32[]{:S(2)}) %collective-permute-start.42) | collective-permute-done | bytes 1048608 | tf_op jit(solution)/shard_map/ppermute | solution.py:88
  586.5 11.2 %collective-permute-done.35 = bf16[4,192,1152]{2,1,0:T(8,128)(2,1)} collective-permute-done((bf16[4,192,1152]{2,1,0:T(8,128)(2,1)}, bf16[4,192,1152]{2,1,0:T(8,128)(2,1)}, u32[]{:S(2)}, u32[]{:S(2)}) %collective-permute-start.35) | collective-permute-done | bytes 1769504 | tf_op jit(solution)/shard_map/ppermute | solution.py:88
  624.2 8.0 %collective-permute-start.49 = (bf16[192,384]{1,0:T(8,128)(2,1)S(1)}, bf16[192,384]{1,0:T(8,128)(2,1)S(1)}, u32[]{:S(2)}, u32[]{:S(2)}) collective-permute-start(bf16[192,384]{1,0:T(8,128)(2,1)S(1)} %bitcast.454), channel_id=1, source_target_pairs={{0,0},{1,1},{2,8},{3,9},{4,16},{5,17},{6,24},{7,25},{8,2},{9,3},{1... | collective-permute-start | bytes 442376 | tf_op jit(solution)/shard_map/ppermute | solution.py:138
  645.6 8.8 %collective-permute-done.41 = bf16[192,1152]{1,0:T(8,128)(2,1)S(1)} collective-permute-done((bf16[192,1152]{1,0:T(8,128)(2,1)S(1)}, bf16[192,1152]{1,0:T(8,128)(2,1)S(1)}, u32[]{:S(2)}, u32[]{:S(2)}) %collective-permute-start.41) | collective-permute-done | bytes 442400 | tf_op jit(solution)/shard_map/ppermute | solution.py:98
  657.0 5.8 collective-permute-start.50
  665.3 14.8 %collective-permute-done.50 = bf16[512,384]{0,1:T(8,128)(2,1)S(1)} collective-permute-done((bf16[512,384]{0,1:T(8,128)(2,1)S(1)}, bf16[512,384]{0,1:T(8,128)(2,1)S(1)}, u32[]{:S(2)}, u32[]{:S(2)}) %collective-permute-start.50) | collective-permute-done | bytes 393248 | tf_op jit(solution)/shard_map/ppermute | solution.py:138
  (598 shorter events, 280.1 us)
Async XLA Ops:
  7.2 95.9 %all-gather.4.cloned.1.call-start = ((), (), s32[]{:S(2)}) async-start(), calls=%async_computation.9 | async-start | bytes 3981312 | tf_op jit(solution)/shard_map/all_gather | solution.py:68
  22.5 19.0 %all-to-all-start = ((f32[32,4,128]{2,1,0:T(4,128)}), f32[32,4,128]{2,1,0:T(4,128)}, u32[]{:S(2)}, u32[]{:S(2)}) async-start(f32[32,4,128]{2,1,0:T(4,128)} %broadcast_in_dim.23), calls=%async_computation | async-start | bytes 131072 | tf_op jit(solution)/shard_map/all_to_all | solution.py:575
  28.9 140.1 %all-gather.6.cloned.1.call-start = ((), (), s32[]{:S(2)}) async-start(), calls=%async_computation.10 | async-start | bytes 2211840 | tf_op jit(solution)/shard_map/all_gather | solution.py:68
  28.9 19.6 %collective-permute-start = (bf16[2,64,1536]{2,1,0:T(8,128)(2,1)S(1)}, bf16[2,64,1536]{2,1,0:T(8,128)(2,1)S(1)}, u32[]{:S(2)}, u32[]{:S(2)}) collective-permute-start(bf16[2,64,1536]{2,1,0:T(8,128)(2,1)S(1)} %bitcast.360), channel_id=1, source_target_pairs={{0,16},{8,24},{16,0},{24,8},{1,17},{9,25},{17,1},{25,9},{2,18},{10... | collective-permute-start | bytes 1179656 | tf_op jit(solution)/shard_map/ppermute | solution.py:24
  29.6 22.4 %collective-permute-start.12 = (bf16[128,1536]{1,0:T(8,128)(2,1)}, bf16[128,1536]{1,0:T(8,128)(2,1)}, u32[]{:S(2)}, u32[]{:S(2)}) collective-permute-start(bf16[128,1536]{1,0:T(8,128)(2,1)} %param.32), channel_id=1, source_target_pairs={{0,1},{1,0},{2,3},{3,2},{4,5},{5,4},{6,7},{7,6},{8,9},{9,8},{10,11... | collective-permute-start | bytes 1179656 | tf_op jit(solution)/shard_map/ppermute | solution.py:108
  41.5 70.3 %all-to-all-start.4 = ((bf16[4,48,2048]{2,1,0:T(8,128)(2,1)}), bf16[4,48,2048]{2,1,0:T(8,128)(2,1)}, u32[]{:S(2)}, u32[]{:S(2)}) async-start(bf16[4,48,2048]{2,1,0:T(8,128)(2,1)} %copy.203), calls=%async_computation.4 | async-start | bytes 1572864 | tf_op jit(solution)/shard_map/all_to_all | solution.py:551
  47.4 249.7 %all-gather.8.cloned.1.call-start = ((), (), s32[]{:S(2)}) async-start(), calls=%async_computation.11 | async-start | bytes 7077888 | tf_op jit(solution)/shard_map/all_gather | solution.py:68
  54.4 57.4 %collective-permute-start.16 = (bf16[2,128,1536]{2,1,0:T(8,128)(2,1)}, bf16[2,128,1536]{2,1,0:T(8,128)(2,1)}, u32[]{:S(2)}, u32[]{:S(2)}) collective-permute-start(bf16[2,128,1536]{2,1,0:T(8,128)(2,1)} %maximum_select_fusion), channel_id=1, source_target_pairs={{2,0},{3,1},{4,2},{5,3},{6,4},{7,5},{10,8},{11,9},{12,10},{13,11},... | collective-permute-start | bytes 2359304 | tf_op jit(solution)/shard_map/ppermute | solution.py:113
  55.7 39.3 %collective-permute-start.13 = (bf16[2,128,1536]{2,1,0:T(8,128)(2,1)}, bf16[2,128,1536]{2,1,0:T(8,128)(2,1)}, u32[]{:S(2)}, u32[]{:S(2)}) collective-permute-start(bf16[2,128,1536]{2,1,0:T(8,128)(2,1)} %maximum_select_fusion), channel_id=1, source_target_pairs={{0,2},{1,3},{2,4},{3,5},{4,6},{5,7},{8,10},{9,11},{10,12},{11,13},... | collective-permute-start | bytes 2359304 | tf_op jit(solution)/shard_map/ppermute | solution.py:112
  95.0 18.1 %collective-permute-start.14 = (bf16[2,128,1536]{2,1,0:T(8,128)(2,1)}, bf16[2,128,1536]{2,1,0:T(8,128)(2,1)}, u32[]{:S(2)}, u32[]{:S(2)}) collective-permute-start(bf16[2,128,1536]{2,1,0:T(8,128)(2,1)} %collective-permute-done.13), channel_id=1, source_target_pairs={{2,4},{3,5},{4,6},{5,7},{10,12},{11,13},{12,14},{13,15},{18,20},{1... | collective-permute-start | bytes 2359304 | tf_op jit(solution)/shard_map/ppermute | solution.py:112
  111.9 49.4 %collective-permute-start.17 = (bf16[2,128,1536]{2,1,0:T(8,128)(2,1)}, bf16[2,128,1536]{2,1,0:T(8,128)(2,1)}, u32[]{:S(2)}, u32[]{:S(2)}) collective-permute-start(bf16[2,128,1536]{2,1,0:T(8,128)(2,1)} %collective-permute-done.16), channel_id=1, source_target_pairs={{2,0},{3,1},{4,2},{5,3},{10,8},{11,9},{12,10},{13,11},{18,16},{19,... | collective-permute-start | bytes 2359304 | tf_op jit(solution)/shard_map/ppermute | solution.py:113
  113.2 49.4 %collective-permute-start.15 = (bf16[2,128,1536]{2,1,0:T(8,128)(2,1)}, bf16[2,128,1536]{2,1,0:T(8,128)(2,1)}, u32[]{:S(2)}, u32[]{:S(2)}) collective-permute-start(bf16[2,128,1536]{2,1,0:T(8,128)(2,1)} %collective-permute-done.14), channel_id=1, source_target_pairs={{4,6},{5,7},{12,14},{13,15},{20,22},{21,23},{28,30},{29,31}} | collective-permute-start | bytes 2359304 | tf_op jit(solution)/shard_map/ppermute | solution.py:112
  125.1 82.1 %all-to-all-start.2 = ((bf16[8,704,128]{2,1,0:T(8,128)(2,1)}), bf16[8,704,128]{2,1,0:T(8,128)(2,1)S(1)}, u32[]{:S(2)}, u32[]{:S(2)}) async-start(bf16[8,704,128]{2,1,0:T(8,128)(2,1)} %get-tuple-element.42), calls=%async_computation.2 | async-start | bytes 2883584 | tf_op jit(solution)/shard_map/all_to_all | solution.py:624
  151.7 159.5 %collective-permute-start.5 = (bf16[2,2,1,32,1536]{4,3,2,1,0:T(8,128)(2,1)}, bf16[2,2,1,32,1536]{4,3,2,1,0:T(8,128)(2,1)}, u32[]{:S(2)}, u32[]{:S(2)}) collective-permute-start(bf16[2,2,1,32,1536]{4,3,2,1,0:T(8,128)(2,1)} %param.45), channel_id=1, source_target_pairs={{0,1},{1,2},{2,3},{3,4},{4,5},{5,6},{6,7},{8,9},{9,10},{10,11},{11... | collective-permute-start | bytes 1179656 | tf_op jit(solution)/shard_map/ppermute | solution.py:62
  155.1 156.2 %collective-permute-start.4 = (bf16[2,2,1,32,1536]{4,3,2,1,0:T(8,128)(2,1)}, bf16[2,2,1,32,1536]{4,3,2,1,0:T(8,128)(2,1)}, u32[]{:S(2)}, u32[]{:S(2)}) collective-permute-start(bf16[2,2,1,32,1536]{4,3,2,1,0:T(8,128)(2,1)} %param.45), channel_id=1, source_target_pairs={{1,0},{2,1},{3,2},{4,3},{5,4},{6,5},{7,6},{9,8},{10,9},{11,10},{12... | collective-permute-start | bytes 1179656 | tf_op jit(solution)/shard_map/ppermute | solution.py:63
  161.2 130.0 %collective-permute-start.18 = (bf16[2,128,1536]{2,1,0:T(8,128)(2,1)}, bf16[2,128,1536]{2,1,0:T(8,128)(2,1)}, u32[]{:S(2)}, u32[]{:S(2)}) collective-permute-start(bf16[2,128,1536]{2,1,0:T(8,128)(2,1)} %collective-permute-done.17), channel_id=1, source_target_pairs={{2,0},{3,1},{10,8},{11,9},{18,16},{19,17},{26,24},{27,25}} | collective-permute-start | bytes 2359304 | tf_op jit(solution)/shard_map/ppermute | solution.py:113
  172.7 66.6 %collective-permute-start.7 = (f32[1,512]{1,0:T(1,128)S(1)}, f32[1,512]{1,0:T(1,128)S(1)}, u32[]{:S(2)}, u32[]{:S(2)}) collective-permute-start(f32[1,512]{1,0:T(1,128)S(1)} %add.350), channel_id=1, source_target_pairs={{0,16},{8,24},{16,0},{24,8},{1,17},{9,25},{17,1},{25,9},{2,18},{10... | collective-permute-start | bytes 6152 | tf_op jit(solution)/shard_map/ppermute | solution.py:24
  229.4 29.3 %all-to-all-start.3 = ((bf16[8,192,128]{2,1,0:T(8,128)(2,1)}), bf16[8,192,128]{2,1,0:T(8,128)(2,1)S(1)}, u32[]{:S(2)}, u32[]{:S(2)}) async-start(bf16[8,192,128]{2,1,0:T(8,128)(2,1)} %get-tuple-element.43), calls=%async_computation.3 | async-start | bytes 786432 | tf_op jit(solution)/shard_map/all_to_all | solution.py:637
  237.2 418.3 %reduce-scatter.2.cloned.1.call-start = ((), (), s32[]{:S(2)}) async-start(), calls=%async_computation.12 | async-start | bytes 10616832 | tf_op jit(solution)/shard_map/reduce_scatter | solution.py:72
  389.1 27.6 %all-to-all-start.5 = ((bf16[8,192,128]{2,1,0:T(8,128)(2,1)}), bf16[8,192,128]{2,1,0:T(8,128)(2,1)}, u32[]{:S(2)}, u32[]{:S(2)}) async-start(bf16[8,192,128]{2,1,0:T(8,128)(2,1)} %get-tuple-element.48), calls=%async_computation.5 | async-start | bytes 786432 | tf_op jit(solution)/shard_map/all_to_all | solution.py:712
  440.0 64.7 %all-to-all-start.6 = ((bf16[8,704,128]{2,1,0:T(8,128)(2,1)}), bf16[8,704,128]{2,1,0:T(8,128)(2,1)}, u32[]{:S(2)}, u32[]{:S(2)}) async-start(bf16[8,704,128]{2,1,0:T(8,128)(2,1)} %shard_map.351), calls=%async_computation.6 | async-start | bytes 2883584 | tf_op jit(solution)/shard_map/all_to_all | solution.py:767
  447.7 33.2 %collective-permute-start.30 = (bf16[2,2,1,32,1536]{4,3,2,1,0:T(8,128)(2,1)}, bf16[2,2,1,32,1536]{4,3,2,1,0:T(8,128)(2,1)S(1)}, u32[]{:S(2)}, u32[]{:S(2)}) collective-permute-start(bf16[2,2,1,32,1536]{4,3,2,1,0:T(8,128)(2,1)} %convert_element_type.398), channel_id=1, source_target_pairs={{1,0},{2,1},{3,2},{4,3},{5,4},{6,5},{7,6},{9,8},{10,9},{11,10},{12... | collective-permute-start | bytes 1179656 | tf_op jit(solution)/shard_map/ppermute | solution.py:63
  449.8 40.0 %collective-permute-start.29 = (bf16[2,2,1,32,1536]{4,3,2,1,0:T(8,128)(2,1)}, bf16[2,2,1,32,1536]{4,3,2,1,0:T(8,128)(2,1)}, u32[]{:S(2)}, u32[]{:S(2)}) collective-permute-start(bf16[2,2,1,32,1536]{4,3,2,1,0:T(8,128)(2,1)} %convert_element_type.398), channel_id=1, source_target_pairs={{0,1},{1,2},{2,3},{3,4},{4,5},{5,6},{6,7},{8,9},{9,10},{10,11},{11... | collective-permute-start | bytes 1179656 | tf_op jit(solution)/shard_map/ppermute | solution.py:62
  459.0 36.7 %collective-permute-start.27 = (f32[1,512]{1,0:T(1,128)S(1)}, f32[1,512]{1,0:T(1,128)S(1)}, u32[]{:S(2)}, u32[]{:S(2)}) collective-permute-start(f32[1,512]{1,0:T(1,128)S(1)} %bitcast.474), channel_id=1, source_target_pairs={{0,8},{8,0},{16,24},{24,16},{1,9},{9,1},{17,25},{25,17},{2,10},{10... | collective-permute-start | bytes 6152 | tf_op jit(solution)/shard_map/ppermute | solution.py:24
  523.1 35.7 %collective-permute-start.42 = (bf16[4,1024,128]{2,1,0:T(8,128)(2,1)}, bf16[4,1024,128]{2,1,0:T(8,128)(2,1)}, u32[]{:S(2)}, u32[]{:S(2)}) collective-permute-start(bf16[4,1024,128]{2,1,0:T(8,128)(2,1)} %dynamic-slice_bitcast_fusion.1), channel_id=1, source_target_pairs={{0,1},{1,0},{2,3},{3,2},{4,5},{5,4},{6,7},{7,6},{8,9},{9,8},{10,11... | collective-permute-start | bytes 3145736 | tf_op jit(solution)/shard_map/ppermute | solution.py:88
  537.5 60.2 %collective-permute-start.35 = (bf16[4,192,1152]{2,1,0:T(8,128)(2,1)}, bf16[4,192,1152]{2,1,0:T(8,128)(2,1)}, u32[]{:S(2)}, u32[]{:S(2)}) collective-permute-start(bf16[4,192,1152]{2,1,0:T(8,128)(2,1)} %dynamic-slice_bitcast_fusion), channel_id=1, source_target_pairs={{0,1},{1,0},{2,3},{3,2},{4,5},{5,4},{6,7},{7,6},{8,9},{9,8},{10,11... | collective-permute-start | bytes 5308424 | tf_op jit(solution)/shard_map/ppermute | solution.py:88
  540.1 27.1 %collective-permute-start.34 = (bf16[2,64,1536]{2,1,0:T(8,128)(2,1)S(1)}, bf16[2,64,1536]{2,1,0:T(8,128)(2,1)S(1)}, u32[]{:S(2)}, u32[]{:S(2)}) collective-permute-start(bf16[2,64,1536]{2,1,0:T(8,128)(2,1)S(1)} %fusion.34), channel_id=1, source_target_pairs={{0,16},{8,24},{16,0},{24,8},{1,17},{9,25},{17,1},{25,9},{2,18},{10... | collective-permute-start | bytes 1179656 | tf_op jit(solution)/shard_map/ppermute | solution.py:24
  578.6 29.1 %all-to-all-start.7 = ((f32[32,7,128]{2,1,0:T(8,128)}), f32[32,7,128]{2,1,0:T(8,128)S(1)}, u32[]{:S(2)}, u32[]{:S(2)}) async-start(f32[32,7,128]{2,1,0:T(8,128)} %reshape.784), calls=%async_computation.8 | async-start | bytes 262144 | tf_op jit(solution)/shard_map/all_to_all | solution.py:813
  585.0 25.7 %collective-permute-start.47 = (bf16[1024,128]{1,0:T(8,128)(2,1)}, bf16[1024,128]{1,0:T(8,128)(2,1)}, u32[]{:S(2)}, u32[]{:S(2)}) collective-permute-start(bf16[1024,128]{1,0:T(8,128)(2,1)} %get-tuple-element.227), channel_id=1, source_target_pairs={{4,2},{5,3},{6,4},{7,5},{12,10},{13,11},{14,12},{15,13},{20,18},{2... | collective-permute-start | bytes 786440 | tf_op jit(solution)/shard_map/ppermute | solution.py:98
  610.0 22.3 %collective-permute-start.39 = (bf16[192,1152]{1,0:T(8,128)(2,1)}, bf16[192,1152]{1,0:T(8,128)(2,1)S(1)}, u32[]{:S(2)}, u32[]{:S(2)}) collective-permute-start(bf16[192,1152]{1,0:T(8,128)(2,1)} %get-tuple-element.214), channel_id=1, source_target_pairs={{6,4},{7,5},{14,12},{15,13},{22,20},{23,21},{30,28},{31,29}} | collective-permute-start | bytes 1327112 | tf_op jit(solution)/shard_map/ppermute | solution.py:98
  624.2 18.3 %collective-permute-start.49 = (bf16[192,384]{1,0:T(8,128)(2,1)S(1)}, bf16[192,384]{1,0:T(8,128)(2,1)S(1)}, u32[]{:S(2)}, u32[]{:S(2)}) collective-permute-start(bf16[192,384]{1,0:T(8,128)(2,1)S(1)} %bitcast.454), channel_id=1, source_target_pairs={{0,0},{1,1},{2,8},{3,9},{4,16},{5,17},{6,24},{7,25},{8,2},{9,3},{1... | collective-permute-start | bytes 442376 | tf_op jit(solution)/shard_map/ppermute | solution.py:138
  657.0 23.1 %collective-permute-start.50 = (bf16[512,384]{0,1:T(8,128)(2,1)S(1)}, bf16[512,384]{0,1:T(8,128)(2,1)S(1)}, u32[]{:S(2)}, u32[]{:S(2)}) collective-permute-start(bf16[512,384]{0,1:T(8,128)(2,1)S(1)} %bitcast.436), channel_id=1, source_target_pairs={{0,0},{1,1},{2,8},{3,9},{4,16},{5,17},{6,24},{7,25},{8,2},{9,3},{1... | collective-permute-start | bytes 1179656 | tf_op jit(solution)/shard_map/ppermute | solution.py:138
  (145 other events, 1919.1 us)
Sparse Core Ops, SparseCore 0:
  20.7 82.3 all-gather.3
  105.8 63.0 all-gather.5
  171.1 123.4 all-gather.7
  365.6 197.9 reduce-scatter.1

commit v3 on v2

--- a/solution.py
+++ b/solution.py
@@ -1,4 +1,5 @@
 import functools
+import itertools
 import math
 
 import jax
@@ -16,15 +17,19 @@
 F32 = jnp.float32
 BF16 = jnp.bfloat16
 RING = 8
-ROW = ("far", "row")
-ALL = ("frame", "far", "row")
+TEAM = ("y", "x")
+PLANE = ("z", "core")
+GROUP = ("far", "z", "core")
+FRAME = ("y", "core")
+ROW = ("far", "z", "x")
+ALL = ("y", "core", "far", "z", "x")
 
 
 def swap(value, bits):
-    return lax.ppermute(value, "frame", [(i, i ^ bits) for i in range(lax.axis_size("frame"))])
-
-
-def frame_sum(value):
+    return lax.ppermute(value, TEAM, [(i, i ^ bits) for i in range(4)])
+
+
+def team_sum(value):
     value = value + swap(value, 1)
     return value + swap(value, 2)
 
@@ -42,18 +47,45 @@
     return (moved, None) if work is None else lax.optimization_barrier((moved, work))
 
 
-def frame_gather(value, work=None):
-    over, work = beside(swap(value, 2), work)
-    pair = swap(jnp.stack([value, over]), 1)
-    return jnp.stack([value, pair[0], over, pair[1]]), work
-
-
-def frame_scatter(terms, work=None):
+def team_gather(value, work=None):
+    others, work = beside([swap(value, k) for k in (3, 2, 1)], work)
+    return jnp.stack([value, others[2], others[1], others[0]]), work
+
+
+def team_scatter(terms, work=None):
     low = terms.astype(BF16)
-    got = swap(jnp.stack([low[1], low[3]]), 1).astype(F32)
-    far = (terms[2] + got[1]).astype(BF16)
-    far, work = beside(swap(far, 2), work)
-    return terms[0] + got[0] + far.astype(F32), work
+    others, work = beside([swap(low[k], k) for k in (3, 2, 1)], work)
+    return terms[0] + sum(other.astype(F32) for other in others), work
+
+
+def relocate(block, target):
+    sizes = [lax.axis_size(axis) for axis in ALL]
+    pairs = []
+    for index, where in enumerate(itertools.product(*(range(size) for size in sizes))):
+        to = 0
+        for size, at in zip(sizes, target(*where)):
+            to = to * size + at
+        pairs.append((index, to))
+    return lax.ppermute(block, ALL, pairs)
+
+
+def exchange(block):
+    return relocate(block, lambda y, core, far, z, x: (y, x, far, z, core))
+
+
+def to_owner(block):
+    if lax.axis_size("far") == 1:
+        return relocate(block, lambda y, core, far, z, x: (z // 2, z % 2, 0, 2 * y + x, core))
+    return relocate(block, lambda y, core, far, z, x: (far // 2, far % 2, 2 * y + x, z, core))
+
+
+def group_gather(block):
+    return lax.all_gather(block, GROUP, axis=0, tiled=True)
+
+
+def group_scatter(terms):
+    terms = terms.reshape(-1, terms.shape[-1])
+    return lax.psum_scatter(terms, GROUP, scatter_dimension=0, tiled=True)
 
 
 def row_neighbours(block):
@@ -64,58 +96,6 @@
     return above, below
 
 
-def row_gather(block):
-    return lax.all_gather(block, ROW, axis=0, tiled=True)
-
-
-def row_scatter(terms):
-    return lax.psum_scatter(terms, ROW, scatter_dimension=0, tiled=True)
-
-
-def pick(blocks, index):
-    return lax.dynamic_index_in_dim(blocks, index, 0, keepdims=False)
-
-
-def line_scatter(terms):
-    if lax.axis_size("far") > 1:
-        return row_scatter(terms.reshape(-1, terms.shape[-1])).astype(F32)
-    place = lax.axis_index("row")
-    z, x = place // 2, place % 2
-    last = RING // 2 - 1
-    blocks = terms.reshape(last + 1, 2, -1, terms.shape[-1])
-    mine = lax.dynamic_index_in_dim(blocks, x, 1, keepdims=False)
-    other = lax.dynamic_index_in_dim(blocks, 1 - x, 1, keepdims=False)
-    got = lax.ppermute(other, "row", [(i, i ^ 1) for i in range(RING)])
-    both = (mine.astype(F32) + got.astype(F32)).astype(BF16)
-    up = down = None
-    for k in range(last, 0, -1):
-        send_up = pick(both, jnp.minimum(z + k, last))
-        send_down = pick(both, jnp.maximum(z - k, 0))
-        if up is not None:
-            send_up = (send_up.astype(F32) + up.astype(F32)).astype(BF16)
-            send_down = (send_down.astype(F32) + down.astype(F32)).astype(BF16)
-        up = lax.ppermute(send_up, "row", [(i, i + 2) for i in range(RING) if i // 2 + k <= last])
-        down = lax.ppermute(send_down, "row", [(i, i - 2) for i in range(RING) if i // 2 - k >= 0])
-    return pick(both, z).astype(F32) + up.astype(F32) + down.astype(F32)
-
-
-def line_gather(block):
-    if lax.axis_size("far") > 1:
-        return row_gather(block)
-    place = lax.axis_index("row")
-    z, x = place // 2, place % 2
-    last = RING // 2 - 1
-    other = lax.ppermute(block, "row", [(i, i ^ 1) for i in range(RING)])
-    pair = jnp.where(x == 0, jnp.stack([block, other]), jnp.stack([other, block]))
-    below, above = [pair], [pair]
-    for k in range(1, last + 1):
-        below.append(lax.ppermute(below[-1], "row", [(i, i + 2) for i in range(RING - 2) if i // 2 >= k - 1]))
-        above.append(lax.ppermute(above[-1], "row", [(i, i - 2) for i in range(2, RING) if i // 2 + k - 1 <= last]))
-    line = jnp.stack(below[:0:-1] + above)
-    line = lax.dynamic_slice_in_dim(line, last - z, last + 1, 0)
-    return line.reshape(-1, block.shape[1])
-
-
 def to_chunks(value, size):
     blocks, rows, columns = value.shape
     value = value.reshape(blocks, rows, columns // size, size).transpose(0, 2, 1, 3)
@@ -125,17 +105,6 @@
 def from_chunks(value, rows):
     blocks, _, size = value.shape
     return value.reshape(blocks, -1, rows, size).transpose(0, 2, 1, 3).reshape(blocks * rows, -1)
-
-
-def to_owner(block):
-    frames, rows = lax.axis_size("frame"), lax.axis_size(ROW)
-    part = rows // frames
-    pairs = []
-    for f in range(frames):
-        for c in range(frames):
-            for h in range(part):
-                pairs.append((f * rows + c * part + h, c * rows + f * part + h))
-    return lax.ppermute(block, ALL, pairs)
 
 
 def owners(pair):
@@ -281,26 +250,36 @@
     part = n_rows // 4
     left = turned(hidden_ref[...])
     tile = left.shape[0] // part
-    for c in range(4):
+
+    def down(c, carry):
+        block = dot_nn(left, dz_ref[:, pl.ds(pl.multiple_of(384 * c, 128), 384)]).astype(BF16)
         for j in range(3):
-            cut = 384 * c + 128 * j
-            block = dot_nn(left, dz_ref[:, cut : cut + 128]).astype(BF16)
             for h in range(part):
-                out_ref[c * part + h, tile * j : tile * j + tile, :] = block[tile * h : tile * h + tile]
+                out_ref[c * part + h, tile * j : tile * j + tile, :] = block[
+                    tile * h : tile * h + tile, 128 * j : 128 * j + 128
+                ]
+        return carry
+
+    lax.fori_loop(0, 4, down, 0)
     base = 3 * tile
-    left = turned(f_in_ref[...])
-    tile = left.shape[0] // n_rows
-    for j in range(0, dgu_ref.shape[1] // 128, 2):
-        block = dot_nn(left, dgu_ref[:, 128 * j : 128 * j + 256]).astype(BF16)
-        for r in range(n_rows):
-            for e in range(2):
-                at = base + tile * (j + e)
-                out_ref[r, at : at + tile, :] = block[tile * r : tile * r + tile, 128 * e : 128 * e + 128]
+    left_f = turned(f_in_ref[...])
+    tile_f = left_f.shape[0] // n_rows
+
+    def gate_up(j, carry):
+        block = dot_nn(left_f, dgu_ref[:, pl.ds(pl.multiple_of(256 * j, 128), 256)]).astype(BF16)
+        for e in range(2):
+            at = pl.multiple_of(base + tile_f * (2 * j + e), 16)
+            for r in range(n_rows):
+                out_ref[r, pl.ds(at, tile_f), :] = block[
+                    tile_f * r : tile_f * r + tile_f, 128 * e : 128 * e + 128
+                ]
+        return carry
+
+    lax.fori_loop(0, dgu_ref.shape[1] // 256, gate_up, 0)
 
 
 def out_kernel(attn_ref, dy_ref, dk_ref, dv_ref, dot_ref, out_ref):
     n_rows = out_ref.shape[0]
-    part = n_rows // 4
     wide = dk_ref.shape[0] // n_rows
     tall = 2 * wide + 16
     chunks = dk_ref.shape[1] // 128
@@ -317,96 +296,96 @@
             out_ref[r, tall * j : tall * j + tall, :] = block.astype(BF16)
     base = tall * chunks
     left = turned(attn_ref[...])
-    tile = left.shape[0] // part
-    for c in range(4):
-        for j in range(3):
-            cut = 384 * c + 128 * j
-            block = dot_nn(left, dy_ref[:, cut : cut + 128]).astype(BF16)
-            for h in range(part):
-                at = base + tile * j
-                out_ref[c * part + h, at : at + tile, :] = block[tile * h : tile * h + tile]
+    tile = left.shape[0] // (n_rows // 4)
+    for f in range(4):
+        block = dot_nn(left, dy_ref[:, 384 * f : 384 * f + 384]).astype(BF16)
+        for part in range(n_rows // 4):
+            member = f * (n_rows // 4) + part
+            for j in range(3):
+                out_ref[member, base + tile * j : base + tile * j + tile, :] = block[
+                    tile * part : tile * part + tile, 128 * j : 128 * j + 128
+                ]
 
 
 def dot_tt(a, b):
     return lax.dot_general(a, b, (((0,), (1,)), ((), ())), preferred_element_type=F32)
 
 
-def query_block(ref, slot, i, base):
-    if slot == 0:
-        return ref[pl.ds(i, 1), base : base + 128, :].reshape(128, 128).astype(F32)
-    return ref[pl.ds(2 * i, 2), base + 128 : base + 192, :].reshape(128, 128).astype(F32)
-
-
-def put_block(ref, slot, i, base, value):
-    if slot == 0:
-        ref[pl.ds(i, 1), base : base + 128, :] = value.reshape(1, 128, 128).astype(ref.dtype)
-    else:
-        ref[pl.ds(2 * i, 2), base + 128 : base + 192, :] = value.reshape(2, 64, 128).astype(ref.dtype)
-
-
-def self_kernel(kv_ref, q_ref, o_ref, ot_ref, lse_ref):
+def block_of(ref, i, base):
+    at = pl.multiple_of(base + 64 * (i // 4), 64)
+    return ref[pl.ds(2 * (i % 4), 2), pl.ds(at, 64), :].reshape(128, 128).astype(F32)
+
+
+def put_block(ref, i, base, value):
+    at = pl.multiple_of(base + 64 * (i // 4), 64)
+    ref[pl.ds(2 * (i % 4), 2), pl.ds(at, 64), :] = value.reshape(2, 64, 128).astype(ref.dtype)
+
+
+def slot_keys(kv_ref, slot):
+    return kv_ref[:, pl.ds(pl.multiple_of(256 * slot, 256), 256), :].reshape(-1, 128)
+
+
+def self_kernel(kv_ref, q_ref, o_ref, ot_ref, lse_ref, kvt_ref):
     lane = lanes((128, 128))
     for slot in range(2):
-        kv = kv_ref[:, 256 * slot : 256 * slot + 256, :].reshape(-1, 128)
-        kvt = kv.astype(F32).T.astype(BF16)
-
-        def step(i, carry):
-            q = query_block(q_ref, slot, i, 512) * (HDIM ** (-0.5))
-            qa = jnp.where(lane < 64, q, 0.0)
-            qb = jnp.where(lane < 64, pltpu.roll(q, 64, 1), 0.0)
-            q2 = jnp.concatenate([qa, qb], axis=0).astype(BF16)
-            s = dot_nt(kv, q2)
-            top = jnp.max(s, axis=0, keepdims=True)
-            p = jnp.exp(s - top)
-            total = jnp.sum(p, axis=0, keepdims=True)
-            ot = dot_nn(kvt, p.astype(BF16)) / total
-            o = ot.T
-            packed = jnp.where(lane < 64, pltpu.roll(o[:128], 64, 1), o[128:])
-            put_block(o_ref, slot, i, 0, packed)
-            ot_ref[pl.ds(8 * slot + i, 1)] = ot[64:].reshape(1, 64, 256)
-            lse_ref[pl.ds(8 * slot + i, 1)] = (top + jnp.log(total)).reshape(1, 1, 256)
-            return carry
-
-        lax.fori_loop(0, 8 if slot == 0 else 4, step, 0)
+        kvt_ref[slot] = turned(slot_keys(kv_ref, slot))
+
+    def step(i, carry):
+        slot = i // 8
+        q = block_of(q_ref, i, 512) * (HDIM ** (-0.5))
+        qa = jnp.where(lane < 64, q, 0.0)
+        qb = jnp.where(lane < 64, pltpu.roll(q, 64, 1), 0.0)
+        q2 = jnp.concatenate([qa, qb], axis=0).astype(BF16)
+        s = dot_nt(slot_keys(kv_ref, slot), q2)
+        top = jnp.max(s, axis=0, keepdims=True)
+        p = jnp.exp(s - top)
+        total = jnp.sum(p, axis=0, keepdims=True)
+        ot = dot_nn(kvt_ref[slot], p.astype(BF16)) / total
+        o = ot.T
+        put_block(o_ref, i, 0, jnp.where(lane < 64, pltpu.roll(o[:128], 64, 1), o[128:]))
+        ot_ref[pl.ds(i, 1)] = ot[64:].reshape(1, 64, 256)
+        lse_ref[pl.ds(i, 1)] = (top + jnp.log(total)).reshape(1, 1, 256)
+        return carry
+
+    lax.fori_loop(0, 12, step, 0)
 
 
 def self_back_kernel(merged, kv_ref, q_ref, do_ref, ot_ref, lse_ref, *rest):
     if merged:
-        dkv_ref, acc_ref = rest
+        dkv_ref, acc_ref, kvt_ref = rest
         dq_ref, base = dkv_ref, 512
     else:
-        dkv_ref, dq_ref, acc_ref = rest
+        dkv_ref, dq_ref, acc_ref, kvt_ref = rest
         base = 0
     lane = lanes((128, 128))
     for slot in range(2):
-        kv = kv_ref[:, 256 * slot : 256 * slot + 256, :].reshape(-1, 128)
-        kvt = kv.astype(F32).T.astype(BF16)
-        acc_ref[...] = jnp.zeros_like(acc_ref)
-
-        def step(i, carry):
-            q = query_block(q_ref, slot, i, 512) * (HDIM ** (-0.5))
-            d = query_block(do_ref, slot, i, 0)
-            qa = jnp.where(lane < 64, q, 0.0)
-            qb = jnp.where(lane < 64, pltpu.roll(q, 64, 1), 0.0)
-            q2 = jnp.concatenate([qa, qb], axis=0).astype(BF16)
-            da = jnp.where(lane < 64, 0.0, pltpu.roll(d, 64, 1))
-            db = jnp.where(lane < 64, 0.0, d)
-            d2 = jnp.concatenate([da, db], axis=0)
-            delta = jnp.sum(d2.T[64:] * ot_ref[pl.ds(8 * slot + i, 1)].reshape(64, 256), axis=0, keepdims=True)
-            d2 = d2.astype(BF16)
-            s = dot_nt(kv, q2)
-            p = jnp.exp(s - lse_ref[pl.ds(8 * slot + i, 1)].reshape(1, 256))
-            dp = dot_nt(kv, d2)
-            ds = (p * (dp - delta)).astype(BF16)
-            acc_ref[...] += dot_nn(ds, q2) + dot_nn(p.astype(BF16), d2)
-            dq = dot_nn(kvt, ds).T * (HDIM ** (-0.5))
-            packed = jnp.where(lane < 64, dq[:128], pltpu.roll(dq[128:], 64, 1))
-            put_block(dq_ref, slot, i, base, packed)
-            return carry
-
-        lax.fori_loop(0, 8 if slot == 0 else 4, step, 0)
+        kvt_ref[slot] = turned(slot_keys(kv_ref, slot))
+    acc_ref[...] = jnp.zeros_like(acc_ref)
+
+    def step(i, carry):
+        slot = i // 8
+        q = block_of(q_ref, i, 512) * (HDIM ** (-0.5))
+        d = block_of(do_ref, i, 0)
+        qa = jnp.where(lane < 64, q, 0.0)
+        qb = jnp.where(lane < 64, pltpu.roll(q, 64, 1), 0.0)
+        q2 = jnp.concatenate([qa, qb], axis=0).astype(BF16)
+        da = jnp.where(lane < 64, 0.0, pltpu.roll(d, 64, 1))
+        db = jnp.where(lane < 64, 0.0, d)
+        d2 = jnp.concatenate([da, db], axis=0)
+        delta = jnp.sum(d2.T[64:] * ot_ref[pl.ds(i, 1)].reshape(64, 256), axis=0, keepdims=True)
+        d2 = d2.astype(BF16)
+        kv = slot_keys(kv_ref, slot)
+        p = jnp.exp(dot_nt(kv, q2) - lse_ref[pl.ds(i, 1)].reshape(1, 256))
+        ds = (p * (dot_nt(kv, d2) - delta)).astype(BF16)
+        acc_ref[slot] += dot_nn(ds, q2) + dot_nn(p.astype(BF16), d2)
+        dq = dot_nn(kvt_ref[slot], ds).T * (HDIM ** (-0.5))
+        put_block(dq_ref, i, base, jnp.where(lane < 64, dq[:128], pltpu.roll(dq[128:], 64, 1)))
+        return carry
+
+    lax.fori_loop(0, 12, step, 0)
+    for slot in range(2):
         dkv_ref[:, 256 * slot : 256 * slot + 256, :] = (
-            acc_ref[...].reshape(-1, 256, 128).astype(dkv_ref.dtype)
+            acc_ref[slot].reshape(-1, 256, 128).astype(dkv_ref.dtype)
         )
 
 
@@ -531,12 +510,12 @@
 ):
     clips, frames, rows_here, cols, width = tokens.shape
     local = frames * rows_here * cols
-    group = lax.axis_size("frame")
+    group = lax.axis_size("y") * lax.axis_size("x")
     n_rows = lax.axis_size(ROW)
     n_far = lax.axis_size("far")
     n_all = group * n_rows
-    me = lax.axis_index("frame")
-    my_row = lax.axis_index(ROW)
+    me = lax.axis_index(TEAM)
+    my_member = lax.axis_index(GROUP)
     heads_w = width // group
     ff_w = w_gate.shape[1] // group
     count = group * clips * local
@@ -548,20 +527,18 @@
 
     def by_columns(parts):
         cut = jnp.concatenate([w.reshape(rows, group, -1) for w in parts], axis=2)
-        cut = lax.all_to_all(cut.transpose(1, 0, 2), "frame", 0, 0)
-        full = row_gather(cut.reshape(group * rows, -1))
-        full = full.reshape(n_rows, group, rows, -1).transpose(1, 0, 2, 3)
-        return full.reshape(n_rows * group * rows, -1)
+        cut = lax.all_to_all(cut.transpose(1, 0, 2), TEAM, 0, 0)
+        return cut.reshape(group * rows, -1)
+
+    def in_order(gathered):
+        full = gathered.reshape(n_far, RING // 2, 2, 2, 2, rows, -1).transpose(3, 2, 0, 1, 4, 5, 6)
+        return full.reshape(width, -1)
 
     def cap_columns(weight):
         return lax.dot_general(weight, cap2, (((0,), (1,)), ((), ())), preferred_element_type=F32).astype(BF16)
 
-    w_dn = line_gather(w_down)
-    w_qkv = by_columns([w_query, w_key, w_value])
-    side = row_gather(jnp.concatenate([cap_columns(w_cap_key), cap_columns(w_cap_value), w_out], axis=1))
-    tokens_c = clips * caps
-    k_pre_t, v_cap_t, w_o = side[:, :tokens_c], side[:, tokens_c : 2 * tokens_c], side[:, 2 * tokens_c :]
-    w_gu = by_columns([w_gate, w_up])
+    cut_qkv = by_columns([w_query, w_key, w_value])
+    cut_gu = by_columns([w_gate, w_up])
 
     half_width = width // 2
     frequencies = jnp.exp(-math.log(THETA) * jnp.arange(half_width, dtype=F32) / half_width)
@@ -569,18 +546,29 @@
     step_embed = jax.nn.silu(jnp.concatenate([jnp.cos(phases), jnp.sin(phases)], axis=1)).astype(BF16)
     mod_local = mm(step_embed, w_mod).astype(BF16).astype(F32)
     mod_cols = mod_local.shape[1]
-    note = jnp.concatenate([mod_local.reshape(-1), frame_pos.astype(F32).reshape(-1)])
+    note = jnp.concatenate([mod_local.reshape(-1), frame_pos.astype(F32).reshape(-1), row_pos.astype(F32)])
     used = note.shape[0]
     note = jnp.pad(note, (0, -used % 512)).reshape(1, -1, 128)
     note = lax.all_to_all(jnp.broadcast_to(note, (n_all,) + note.shape[1:]), ALL, 0, 0)
     note = note.reshape(n_all, -1)
+    x_own = tokens.reshape(clips, local, width)
+    x_flat = x_own.astype(F32)
+    x_group, _ = team_gather(x_own)
+    w_qkv = in_order(group_gather(cut_qkv))
+    side = jnp.concatenate([cap_columns(w_cap_key), cap_columns(w_cap_value), w_out], axis=1)
+    side = group_gather(exchange(side))
+    tokens_c = clips * caps
+    w_gu = group_gather(cut_gu)
+    w_dn = group_gather(exchange(w_down))
     mod_full = note[:, : clips * mod_cols].reshape(n_all, clips, mod_cols)
     mod_full = mod_full.transpose(1, 0, 2).reshape(clips, 4, width)
     scale_a, gate_a, scale_f, gate_f = (mod_full[:, i] for i in range(4))
-    positions = note[:, clips * mod_cols : used].reshape(group, n_rows, clips, frames)[:, 0]
+    positions = note[:, clips * mod_cols : used].reshape(2, 2, n_far, RING // 2, 2, -1)
+    here = [lax.axis_index(axis) for axis in ("core", "far", "z")]
+    positions = lax.dynamic_slice(positions, (0, *here, 0, 0), (2, 1, 1, 1, 2, positions.shape[-1]))
     order = jnp.arange(group)
-    pick = (order[None, :] == (me ^ order)[:, None]).astype(F32)
-    positions = jnp.sum(pick[:, :, None, None] * positions[None], axis=1)
+    chosen = (order[None, :] == (me ^ order)[:, None]).astype(F32)
+    positions = jnp.sum(chosen[:, :, None] * positions.reshape(1, group, -1), axis=1)
 
     above_g, below_g = row_neighbours(grad_out)
     gains = norm_gains
@@ -588,8 +576,9 @@
     own_gate = jnp.tanh(lax.dynamic_slice(mix_coefs, (0, me * heads_w), (1, heads_w)))
 
     full = (group, clips, frames, cols)
-    pos_a = jnp.broadcast_to((positions + cap_len.astype(F32)[None, :, None])[..., None], full)
-    pos_b = jnp.broadcast_to(row_pos.astype(F32)[0], full)
+    frame_at = positions[:, :-1].reshape(group, clips, frames) + cap_len.astype(F32)[None, :, None]
+    pos_a = jnp.broadcast_to(frame_at[..., None], full)
+    pos_b = jnp.broadcast_to(positions[:, -1:, None, None], full)
     pos_e = jnp.broadcast_to(col_pos.astype(F32), full)
     (fa, fb, fe), sign = rotary_lanes()
     angle = (
@@ -597,10 +586,6 @@
     )
     cosine = jnp.tile(jnp.cos(angle), (1, 2))
     sine = jnp.tile(jnp.sin(angle) * sign, (1, 2))
-
-    x_own = tokens.reshape(clips, local, width)
-    x_flat = x_own.astype(F32)
-    x_group, _ = frame_gather(x_own)
 
     def pre_piece(x_in, gain, scale_in):
         return rms_norm(x_in, gain) * (1.0 + scale_in[:, None, :])
@@ -621,7 +606,9 @@
         cosine,
         sine,
     )
-    got = lax.all_to_all(send, "row", 0, 0)
+    send, side = beside(send, side)
+    k_pre_t, v_cap_t, w_o = side[:, :tokens_c], side[:, tokens_c : 2 * tokens_c], side[:, 2 * tokens_c :]
+    got = lax.all_to_all(send, PLANE, 0, 0)
     kv_all = got
     if n_far > 1:
         kv_all = lax.all_gather(got, "far", axis=0, tiled=True)
@@ -632,15 +619,18 @@
         [shaped((RING, 192, 128), BF16), shaped((12, 64, 256)), shaped((12, 1, 256))],
         kv_all,
         got,
+        scratch=[pltpu.VMEM((2, 128, keys), BF16)],
         flops=2 * work,
     )
-    o_back = lax.all_to_all(o_pack, "row", 0, 0)
+    o_back = lax.all_to_all(o_pack, PLANE, 0, 0)
+    o_back, w_gu = beside(o_back, w_gu)
+    w_gu = in_order(w_gu)
 
     usable = (jnp.arange(caps)[None, :] < cap_len[:, None]) & (cap_mask > 0)
     bias = usable.astype(F32).reshape(clips * caps, 1)
     k_pre_t = k_pre_t.astype(F32)
     gain_cap = own_gains[2][:, None]
-    r_cap = lax.rsqrt(frame_sum(jnp.sum(k_pre_t * k_pre_t, axis=0, keepdims=True)) / width + EPS)
+    r_cap = lax.rsqrt(team_sum(jnp.sum(k_pre_t * k_pre_t, axis=0, keepdims=True)) / width + EPS)
     k_cap_t = (k_pre_t * r_cap * gain_cap).astype(BF16)
     q_cap4 = q_cap.reshape(group, clips, local, heads_w)
     (out_cross,) = cross_call(
@@ -650,14 +640,14 @@
     out_cross = out_cross.reshape(count, heads_w)
     (attn_mix,) = call(mix_kernel, [shaped((count, heads_w), BF16)], o_back, out_cross, own_gate)
 
-    y_one, _ = frame_scatter(mm(attn_mix, w_o).reshape(group, clips, local, width))
+    y_one, _ = team_scatter(mm(attn_mix, w_o).reshape(group, clips, local, width))
 
     def mid_piece(x_in, y_in, gain_two, gate_in, gain_three, scale_in):
         h_mid = x_in + jnp.tanh(gate_in)[:, None, :] * rms_norm(y_in, gain_two)
         return (h_mid, rms_norm(h_mid, gain_three) * (1.0 + scale_in[:, None, :]))
 
     (h_mid, f_in32), mid_back = jax.vjp(mid_piece, x_flat, y_one, gains[1], gate_a, gains[2], scale_f)
-    f_in, _ = frame_gather(f_in32.astype(BF16))
+    f_in, _ = team_gather(f_in32.astype(BF16))
     f_in = f_in.reshape(count, width)
     gate_up = mm(f_in, w_gu)
 
@@ -666,22 +656,18 @@
 
     hidden32, act_back = jax.vjp(act_piece, gate_up[:, :ff_w], gate_up[:, ff_w:])
     hidden = hidden32.astype(BF16)
-    z_out, _ = frame_scatter(mm(hidden, w_dn).reshape(group, clips, local, width))
+    z_out, _ = team_scatter(mm(hidden, w_dn).reshape(group, clips, local, width))
 
     def end_piece(h_in_mid, z_in, gain_four, gate_in):
         return h_in_mid + jnp.tanh(gate_in)[:, None, :] * rms_norm(z_in, gain_four)
 
     y_all, end_back = jax.vjp(end_piece, h_mid, z_out, gains[3], gate_f)
     y_grid = y_all.reshape(tokens.shape)
-    above, below = (v.astype(F32) for v in row_neighbours(y_grid.astype(BF16)))
-    output = (y_grid + mix_coefs[1] * above + mix_coefs[2] * below).astype(BF16)
-
+    above, below = row_neighbours(y_grid.astype(BF16))
     g_center = grad_out.astype(F32)
     d_y = g_center + mix_coefs[1] * below_g.astype(F32) + mix_coefs[2] * above_g.astype(F32)
-    d_above = jnp.sum(g_center * above, axis=(0, 1, 2, 3))
-    d_below = jnp.sum(g_center * below, axis=(0, 1, 2, 3))
     d_h_end, d_z, d_g_four, d_gate_f = end_back(d_y.reshape(clips, local, width))
-    d_z_all, _ = frame_gather(d_z.astype(BF16))
+    d_z_all, _ = team_gather(d_z.astype(BF16))
     d_z_all = d_z_all.reshape(count, width)
     d_hidden = lax.dot_general(d_z_all, w_dn, (((1,), (1,)), ((), ())), preferred_element_type=F32)
     d_gu = jnp.concatenate([d.astype(BF16) for d in act_back(d_hidden)], axis=1)
@@ -699,17 +685,21 @@
         d_gu,
         flops=6 * count * width * ff_w,
     )
-    d_f_in, ff_terms = frame_scatter(d_f_in.reshape(group, clips, local, width), ff_terms)
-    ff_sum = row_scatter(ff_terms.reshape(-1, 128))
+    d_f_in, ff_terms = team_scatter(d_f_in.reshape(group, clips, local, width), ff_terms)
+    ff_sum = group_scatter(ff_terms)
     d_x_mid, d_y_one, d_g_two, d_gate_a, d_g_three, d_scale_f = mid_back((d_h_end, d_f_in))
-    d_y_group, _ = frame_gather(d_y_one.astype(BF16))
+    d_y_group, (above, below) = team_gather(d_y_one.astype(BF16), (above, below))
     d_y_group = d_y_group.reshape(count, width)
     d_attn = lax.dot_general(d_y_group, w_o, (((1,), (1,)), ((), ())), preferred_element_type=F32)
 
     d_pack, d_cross = call(
         split_kernel, [shaped((RING, 192, 128), BF16), shaped((count, heads_w), BF16)], d_attn, own_gate
     )
-    d_got = lax.all_to_all(d_pack, "row", 0, 0)
+    d_got = lax.all_to_all(d_pack, PLANE, 0, 0)
+    above, below = above.astype(F32), below.astype(F32)
+    output = (y_grid + mix_coefs[1] * above + mix_coefs[2] * below).astype(BF16)
+    d_above = jnp.sum(g_center * above, axis=(0, 1, 2, 3))
+    d_below = jnp.sum(g_center * below, axis=(0, 1, 2, 3))
     d_mix_gate = jnp.sum(d_attn * out_cross, axis=0) * (1.0 - own_gate[0] * own_gate[0])
     d_q_cross, d_k_cap, d_v_cap = cross_call(
         cross_back_kernel,
@@ -721,8 +711,22 @@
         bias,
         d_cross.reshape(q_cap4.shape),
     )
-    d_got, (d_q_cross, d_k_cap, d_v_cap) = beside(d_got, (d_q_cross, d_k_cap, d_v_cap))
-    back_scratch = [pltpu.VMEM((keys, 128), F32)]
+    cap_dot = team_sum(jnp.sum(d_k_cap * gain_cap * k_pre_t, axis=0, keepdims=True))
+    wide = heads_w // n_rows
+    tile = width // n_rows
+    cut = (2 * wide + 16) * (clips * caps // 128)
+    (out_terms,) = call(
+        out_kernel,
+        [shaped((n_rows, cut + tile * (heads_w // 128), 128), BF16)],
+        attn_mix,
+        d_y_group,
+        d_k_cap,
+        d_v_cap,
+        cap_dot,
+        flops=2 * count * width * heads_w,
+    )
+    d_got, (d_q_cross, out_terms) = beside(d_got, (d_q_cross, out_terms))
+    back_scratch = [pltpu.VMEM((2, keys, 128), F32), pltpu.VMEM((2, 128, keys), BF16)]
     if n_far == 1:
         (d_send,) = call(
             functools.partial(self_back_kernel, True),
@@ -749,24 +753,11 @@
         )
         d_kv = lax.psum_scatter(d_kv, "far", scatter_dimension=0, tiled=True)
         d_send = jnp.concatenate([d_kv, d_q], axis=1)
-    cap_dot = frame_sum(jnp.sum(d_k_cap * gain_cap * k_pre_t, axis=0, keepdims=True))
-    wide = heads_w // n_rows
-    tile = width // n_rows
-    cut = (2 * wide + 16) * (clips * caps // 128)
-    (out_terms,) = call(
-        out_kernel,
-        [shaped((n_rows, cut + tile * (heads_w // 128), 128), BF16)],
-        attn_mix,
-        d_y_group,
-        d_k_cap,
-        d_v_cap,
-        cap_dot,
-        flops=2 * count * width * heads_w,
-    )
-    d_recv, (out_terms, output, d_above, d_below) = beside(
-        lax.all_to_all(d_send, "row", 0, 0), (out_terms, output, d_above, d_below)
-    )
-    out_sum = line_scatter(out_terms)
+    d_recv, (output, d_above, d_below, ff_sum) = beside(
+        lax.all_to_all(d_send, PLANE, 0, 0), (output, d_above, d_below, ff_sum)
+    )
+    out_terms, ff_sum = beside(out_terms, ff_sum)
+    out_sum = group_scatter(out_terms)
     d_qn, d_kn, d_v = call(
         back_kernel,
         [shaped((count, heads_w)), shaped((count, heads_w)), shaped((count, heads_w), BF16)],
@@ -783,9 +774,11 @@
     d_q_low = (rq * a_q - q_zero * (rq * rq * rq * dots[:, 0:1])).astype(BF16)
     d_k_low = (rk * a_k - k_zero * (rk * rk * rk * dots[:, 1:2])).astype(BF16)
     d_qkv = jnp.concatenate([d_q_low, d_k_low, d_v], axis=1)
+    d_qkv, term_qkv = beside(d_qkv, term(h_in, d_qkv))
+    term_qkv, out_sum = beside(term_qkv, out_sum)
+    qkv_sum = group_scatter(term_qkv)
     d_h_in = lax.dot_general(d_qkv, w_qkv, (((1,), (1,)), ((), ())), preferred_element_type=F32)
-    qkv_sum = line_scatter(term(h_in, d_qkv).reshape(n_rows, -1, 3 * heads_w))
-    d_h_in, _ = frame_scatter(d_h_in.reshape(group, clips, local, width))
+    d_h_in, _ = team_scatter(d_h_in.reshape(group, clips, local, width))
     d_x_pre, d_g_zero, d_scale_a = pre_back(d_h_in)
     grad_tokens = (d_x_pre + d_x_mid).reshape(tokens.shape)
 
@@ -816,28 +809,30 @@
     d_w_mod = lax.dot_general(
         step_embed, d_mod.astype(BF16), (((0,), (0,)), ((), ())), preferred_element_type=F32
     )
-    ff_sum, d_w_mod = beside(ff_sum, d_w_mod)
+    three = heads_w // 128
     mine = w_down.shape[0] * group
     sum_down = to_owner(from_chunks(ff_sum[None, : ff_rows[0]], mine)).astype(F32)
-    sum_gate, sum_up = jnp.split(ff_sum[ff_rows[0] :], 2)
-    cap_sum = from_chunks(out_sum[None, :cut], 2 * wide + 16)
-    sum_out = to_owner(from_chunks(out_sum[None, cut:].astype(BF16), tile)).astype(F32)
+    sum_gate, sum_up = jnp.split(exchange(ff_sum[ff_rows[0] :]), 2)
+    cap_sum = from_chunks(out_sum[None, :cut].astype(F32), 2 * wide + 16)
+    sum_out = to_owner(from_chunks(out_sum[None, cut:], tile)).astype(F32)
+    qkv_sum = exchange(qkv_sum).astype(F32)
 
     def result(block):
         return from_chunks(block[None], tile).astype(F32)
 
     d_k_own, d_v_own, cap_dot = cap_sum[:wide], cap_sum[wide : 2 * wide], cap_sum[2 * wide : 2 * wide + 1]
-    k_own = lax.dynamic_slice(k_pre_t, (my_row * wide, 0), (wide, clips * caps))
-    g_own = lax.dynamic_slice(gain_cap, (my_row * wide, 0), (wide, 1))
-    d_g_cap = jnp.sum(d_k_own * k_own * r_cap, axis=1)
-    d_k_zero_cap = (r_cap * g_own * d_k_own - k_own * (r_cap * r_cap * r_cap * cap_dot / width)).astype(BF16)
+    k_own = lax.dynamic_slice(k_pre_t, (my_member * wide, 0), (wide, clips * caps))
+    g_own = lax.dynamic_slice(gain_cap, (my_member * wide, 0), (wide, 1))
+    d_g_cap = exchange(jnp.sum(d_k_own * k_own * r_cap, axis=1)[None])
+    d_k_zero_cap = r_cap * g_own * d_k_own - k_own * (r_cap * r_cap * r_cap * cap_dot / width)
+    d_caps = exchange(jnp.concatenate([d_k_zero_cap, d_v_own]).astype(BF16))
 
     def cap_weight(d):
         return lax.dot_general(cap2, d, (((0,), (1,)), ((), ())), preferred_element_type=F32)
 
-    d_w_cap_key = cap_weight(d_k_zero_cap)
-    d_w_cap_value = cap_weight(d_v_own.astype(BF16))
-    d_gains = jnp.concatenate([rest[:6], d_g_cap[None]], axis=0)
+    d_w_cap_key = cap_weight(d_caps[:wide])
+    d_w_cap_value = cap_weight(d_caps[wide:])
+    d_gains = jnp.concatenate([rest[:6], d_g_cap], axis=0)
     d_mixes = rest[6:]
 
     return (
@@ -860,10 +855,10 @@
 
 def solution(mesh):
     frame, row = mesh.shape["frame"], mesh.shape["row"]
-    fine = Mesh(mesh.devices.reshape(frame, row // RING, RING), ("frame", "far", "row"))
-    grid = P(None, "frame", ROW, None, None)
+    fine = Mesh(mesh.devices.reshape(frame // 2, 2, row // RING, RING // 2, 2), ALL)
+    grid = P(None, FRAME, ROW, None, None)
     rows, columns = P(ALL, None), P(None, ALL)
-    tile = P(ROW, "frame")
+    tile = P(ROW, FRAME)
     return jax.shard_map(
         body,
         mesh=fine,
@@ -872,7 +867,7 @@
             + (rows,) * 7
             + (columns,) * 3
             + (P(),) * 6
-            + (P(None, "frame"), P(ROW), P(), grid)
+            + (P(None, FRAME), P(ROW), P(), grid)
         ),
         out_specs=(grid, grid) + (tile,) * 7 + (columns,) * 5,
         check_vma=False,

time: 700 us -> 651 us (0.930)
  the two profiles are of different devices: /device:TPU:6 before, /device:TPU:2 now
where the time goes in v3:
time: 651 us; the launch traced here: 638 us
  waiting for transfers between devices  217 us (33%)
  starting transfers between devices  120 us (18%)
  Pallas kernels  90.4 us (14%)
  local copies, waits for them, and re-layouts  68.4 us (11%)
  other arithmetic  52.9 us (8%)
  matrix products  47.6 us (7%)
  blocking collectives  25 us (4%)
  between operations  17.2 us (3%)
    pallas_call x8, Pallas kernels, call(): pl.pallas_call(kernel, out_shape=outs, in_specs=[spec] * len(args), out_s...  79.4 us
    ppermute x32, waiting for transfers between devices, swap(): return lax.ppermute(value, TEAM, [(i, i ^ bits) for i in range(4)])  76.7 us
    all_to_all x1, waiting for transfers between devices, body(): got = lax.all_to_all(send, PLANE, 0, 0)  51.5 us
    ppermute x32, starting transfers between devices, swap(): return lax.ppermute(value, TEAM, [(i, i ^ bits) for i in range(4)])  44.1 us
    all_to_all x1, waiting for transfers between devices, body(): lax.all_to_all(d_send, PLANE, 0, 0)  34.3 us
    all_to_all x2, blocking collectives, by_columns(): cut = lax.all_to_all(cut.transpose(1, 0, 2), TEAM, 0, 0)  25 us
    ppermute x8, starting transfers between devices, relocate(): return lax.ppermute(block, ALL, pairs)  19 us
    ppermute x8, waiting for transfers between devices, relocate(): return lax.ppermute(block, ALL, pairs)  18 us
  transfers between devices with their start and end apart: 57, of which 34 were waited for; matrix products, arithmetic and copies ran while one was open for 20% of the time, Pallas kernels for 14%

profile of v3, /device:TPU:2, one launch (start us, length us, event | category | flops | bytes accessed | tf_op | source)
XLA Modules:
  0.0 638.2 jit_solution(6939753055106958563)
XLA Ops:
  10.5 10.7 %all_to_all.40 = bf16[4,48,1152]{2,1,0:T(8,128)(2,1)} all-to-all(bf16[4,48,1152]{2,1,0:T(8,128)(2,1)S(1)} %copy.184), channel_id=1, replica_groups=mesh['y'=2,'core'=2,'far'=1,'z'=4,'x'=2] {'y','x'}, dimensions={0} | all-to-all | bytes 884736 | tf_op jit(solution)/shard_map/all_to_all | solution.py:530
  24.4 5.6 collective-permute-done.5
  32.4 14.3 %all_to_all.41 = bf16[4,48,2048]{2,1,0:T(8,128)(2,1)} all-to-all(bf16[4,48,2048]{2,1,0:T(8,128)(2,1)S(1)} %copy.192), channel_id=1, replica_groups=mesh['y'=2,'core'=2,'far'=1,'z'=4,'x'=2] {'y','x'}, dimensions={0} | all-to-all | bytes 1572864 | tf_op jit(solution)/shard_map/all_to_all | solution.py:530
  54.0 5.2 all-to-all-start
  61.3 6.1 all-to-all-done
  89.0 5.4 shard_map.344
  94.4 5.1 all-to-all-start.2
  111.4 7.9 %collective-permute-done.16 = bf16[128,1536]{1,0:T(8,128)(2,1)S(1)} collective-permute-done((bf16[128,1536]{1,0:T(8,128)(2,1)S(1)}, bf16[128,1536]{1,0:T(8,128)(2,1)S(1)}, u32[]{:S(2)}, u32[]{:S(2)}) %collective-permute-start.16) | collective-permute-done | bytes 393248 | tf_op jit(solution)/shard_map/ppermute | solution.py:69
  120.9 51.5 %all-to-all-done.2.kv_ref.q_ref = bf16[8,704,128]{2,1,0:T(8,128)(2,1)} async-done(((bf16[8,704,128]{2,1,0:T(8,128)(2,1)}), bf16[8,704,128]{2,1,0:T(8,128)(2,1)}, u32[]{:S(2)}, u32[]{:S(2)}) %all-to-all-start.2) | async-done | bytes 1441824 | tf_op jit(solution)/shard_map/all_to_all | solution.py:611
  172.4 21.1 %shard_map.345 = (bf16[8,192,128]{2,1,0:T(8,128)(2,1)}, f32[12,64,256]{2,1,0:T(8,128)}, f32[12,1,256]{2,1,0:T(1,128)}) custom-call(bf16[8,704,128]{2,1,0:T(8,128)(2,1)} %all-to-all-done.2.kv_ref.q_ref, bf16[8,704,128]{2,1,0:T(8,128)(2,1)} %all-to-all-done.2.kv_ref.q_ref), custom_call_target="tpu_custom_call" | custom-call | flops 3221225472 | bytes 4075520 | tf_op jit(solution)/shard_map/pallas_call | solution.py:434
  206.0 9.4 %all-to-all-done.3.o_ref = bf16[8,192,128]{2,1,0:T(8,128)(2,1)} async-done(((bf16[8,192,128]{2,1,0:T(8,128)(2,1)}), bf16[8,192,128]{2,1,0:T(8,128)(2,1)}, u32[]{:S(2)}, u32[]{:S(2)}) %all-to-all-start.3) | async-done | bytes 393248 | tf_op jit(solution)/shard_map/all_to_all | solution.py:625
  227.6 5.7 collective-permute-done.12
  242.9 8.5 %collective-permute-done.15 = bf16[2,64,1536]{2,1,0:T(8,128)(2,1)S(1)} collective-permute-done((bf16[2,64,1536]{2,1,0:T(8,128)(2,1)S(1)}, bf16[2,64,1536]{2,1,0:T(8,128)(2,1)S(1)}, u32[]{:S(2)}, u32[]{:S(2)}) %collective-permute-start.15) | collective-permute-done | bytes 393248 | tf_op jit(solution)/shard_map/ppermute | solution.py:29
  271.6 8.4 %collective-permute-done.19 = bf16[2,64,1536]{2,1,0:T(8,128)(2,1)S(1)} collective-permute-done((bf16[2,64,1536]{2,1,0:T(8,128)(2,1)S(1)}, bf16[2,64,1536]{2,1,0:T(8,128)(2,1)S(1)}, u32[]{:S(2)}, u32[]{:S(2)}) %collective-permute-start.19) | collective-permute-done | bytes 393248 | tf_op jit(solution)/shard_map/ppermute | solution.py:29
  280.0 7.1 %collective-permute-done.18 = bf16[2,64,1536]{2,1,0:T(8,128)(2,1)S(1)} collective-permute-done((bf16[2,64,1536]{2,1,0:T(8,128)(2,1)S(1)}, bf16[2,64,1536]{2,1,0:T(8,128)(2,1)S(1)}, u32[]{:S(2)}, u32[]{:S(2)}) %collective-permute-start.18) | collective-permute-done | bytes 393248 | tf_op jit(solution)/shard_map/ppermute | solution.py:29
  293.4 9.5 %collective-permute-done.22 = bf16[2,64,1536]{2,1,0:T(8,128)(2,1)S(1)} collective-permute-done((bf16[2,64,1536]{2,1,0:T(8,128)(2,1)S(1)}, bf16[2,64,1536]{2,1,0:T(8,128)(2,1)S(1)}, u32[]{:S(2)}, u32[]{:S(2)}) %collective-permute-start.22) | collective-permute-done | bytes 393248 | tf_op jit(solution)/shard_map/ppermute | solution.py:29
  302.9 5.4 collective-permute-done.21
  312.6 13.8 %fusion.68 = (bf16[512,1536]{1,0:T(8,128)(2,1)S(1)}, f32[512,1536]{1,0:T(8,128)}) fusion(bf16[1536,2048]{1,0:T(8,128)(2,1)S(1)} %bitcast.268, bf16[512,1024]{1,0:T(8,128)(2,1)S(1)} %get-tuple-element.226, bf16[512,1024]{1,0:T(8,128)(2,1)S(1)} %get-tuple-element.225), kind=kOutput, calls=%fused_computation.217 | convolution fusion | flops 3226206208 | bytes 13107200 | tf_op jit(solution)/shard_map/dot_general | solution.py:674
  331.7 15.1 %shard_map.348 = bf16[8,4608,128]{2,1,0:T(8,128)(2,1)} custom-call(bf16[512,1024]{1,0:T(8,128)(2,1)} %multiply_convert_fusion.1.hidden_ref, bf16[512,1536]{1,0:T(8,128)(2,1)} %bitcast.286, bf16[512,1536]{1,0:T(8,128)(2,1)} %bitcast.284, bf16[512,2048]{1,0:T(8,128)(2,1)} %pad_maximum_fusion.dgu_ref), custom_call_target="tpu_custom_call" | custom-call | flops 4831838208 | bytes 15728640 | tf_op jit(solution)/shard_map/pallas_call | solution.py:434
  349.9 6.5 %collective-permute-start.29 = (bf16[2,2,1,32,1536]{4,3,2,1,0:T(8,128)(2,1)S(1)}, bf16[2,2,1,32,1536]{4,3,2,1,0:T(8,128)(2,1)S(1)}, u32[]{:S(2)}, u32[]{:S(2)}) collective-permute-start(bf16[2,2,1,32,1536]{4,3,2,1,0:T(8,128)(2,1)S(1)} %convert_element_type.251), channel_id=1, source_target_pairs={{0,1},{1,2},{2,3},{3,4},{4,5},{5,6},{6,7},{8,9},{9,10},{10,11},{11... | collective-permute-start | bytes 1179656 | tf_op jit(solution)/shard_map/ppermute | solution.py:94
  371.7 7.7 %collective-permute-done.30 = bf16[2,2,1,32,1536]{4,3,2,1,0:T(8,128)(2,1)S(1)} collective-permute-done((bf16[2,2,1,32,1536]{4,3,2,1,0:T(8,128)(2,1)S(1)}, bf16[2,2,1,32,1536]{4,3,2,1,0:T(8,128)(2,1)S(1)}, u32[]{:S(2)}, u32[]{:S(2)}) %collective-permute-start.30) | collective-permute-done | bytes 393248 | tf_op jit(solution)/shard_map/ppermute | solution.py:95
  384.1 5.6 collective-permute-done.28
  394.5 6.2 all-to-all-start.5
  401.8 6.8 %shard_map.350 = (f32[4,2,64,384]{3,2,1,0:T(8,128)S(1)}, f32[384,512]{1,0:T(8,128)S(1)}, f32[384,512]{1,0:T(8,128)S(1)}) custom-call(bf16[4,2,64,384]{3,2,1,0:T(8,128)(2,1)S(1)} %bitcast.248, bf16[384,512]{1,0:T(8,128)(2,1)S(1)} %multiply_convert_fusion.3.kc_ref, bf16[384,512]{1,0:T(8,128)(2,1)S(1)} %get-tuple-element.230.vc_ref, f32[512,1]{1,0:T(8,128)S(1)} %bitcast.245, ...), custom_call_target="tpu_custom_call" | custom-call | flops 503316480 | bytes 4194304 | tf_op jit(solution)/shard_map/pallas_call | solution.py:450
  424.4 23.2 %shard_map.352 = bf16[8,704,128]{2,1,0:T(8,128)(2,1)} custom-call(bf16[8,704,128]{2,1,0:T(8,128)(2,1)} %all-to-all-done.2.kv_ref.q_ref, bf16[8,704,128]{2,1,0:T(8,128)(2,1)} %all-to-all-done.2.kv_ref.q_ref, bf16[8,192,128]{2,1,0:T(8,128)(2,1)} %all-to-all-done.5.do_ref, f32[12,64,256]{2,1,0:T(8,128)} %get-tuple-element.77.ot_ref, ...), custom_call_target="tpu_custom_call" | custom-call | flops 8053063680 | bytes 5517312 | tf_op jit(solution)/shard_map/pallas_call | solution.py:434
  447.6 5.5 all-to-all-start.6
  456.0 34.3 %all-to-all-done.6.d_ref = bf16[8,704,128]{2,1,0:T(8,128)(2,1)} async-done(((bf16[8,704,128]{2,1,0:T(8,128)(2,1)}), bf16[8,704,128]{2,1,0:T(8,128)(2,1)}, u32[]{:S(2)}, u32[]{:S(2)}) %all-to-all-start.6) | async-done | bytes 1441824 | tf_op jit(solution)/shard_map/all_to_all | solution.py:757
  490.7 5.9 shard_map.353
  499.1 6.9 %collective-permute-start.33 = (f32[2,4,128]{2,1,0:T(4,128)S(1)}, f32[2,4,128]{2,1,0:T(4,128)S(1)}, u32[]{:S(2)}, u32[]{:S(2)}) collective-permute-start(f32[2,4,128]{2,1,0:T(4,128)S(1)} %pad_maximum_fusion.11), channel_id=1, source_target_pairs={{0,1},{1,0},{16,17},{17,16},{2,3},{3,2},{18,19},{19,18},{4,5},{5,4... | collective-permute-start | bytes 12296 | tf_op jit(solution)/shard_map/ppermute | solution.py:29
  524.8 5.0 reduce-scatter.6.cloned.1.call-done
  533.5 5.9 fusion.69
  579.1 15.5 %all-to-all-start.7 = ((f32[32,7,128]{2,1,0:T(8,128)}), f32[32,7,128]{2,1,0:T(8,128)}, u32[]{:S(2)}, u32[]{:S(2)}) async-start(f32[32,7,128]{2,1,0:T(8,128)} %reshape.737), calls=%async_computation.10 | async-start | bytes 262144 | tf_op jit(solution)/shard_map/all_to_all | solution.py:806
  (538 shorter events, 270.2 us)
Async XLA Ops:
  7.2 66.6 %all-gather.5.cloned.1.call-start = ((), (), s32[]{:S(2)}) async-start(), calls=%async_computation.11 | async-start | bytes 3981312 | tf_op jit(solution)/shard_map/all_gather | solution.py:83
  21.2 73.2 %all-gather.7.cloned.1.call-start = ((), (), s32[]{:S(2)}) async-start(), calls=%async_computation.12 | async-start | bytes 2211840 | tf_op jit(solution)/shard_map/all_gather | solution.py:83
  30.7 184.6 %all-gather.9.cloned.1.call-start = ((), (), s32[]{:S(2)}) async-start(), calls=%async_computation.13 | async-start | bytes 7077888 | tf_op jit(solution)/shard_map/all_gather | solution.py:83
  46.7 24.8 %collective-permute-start.2 = (bf16[2,64,1536]{2,1,0:T(8,128)(2,1)S(1)}, bf16[2,64,1536]{2,1,0:T(8,128)(2,1)S(1)}, u32[]{:S(2)}, u32[]{:S(2)}) collective-permute-start(bf16[2,64,1536]{2,1,0:T(8,128)(2,1)S(1)} %bitcast.250), channel_id=1, source_target_pairs={{0,17},{1,16},{16,1},{17,0},{2,19},{3,18},{18,3},{19,2},{4,21},{5,... | collective-permute-start | bytes 1179656 | tf_op jit(solution)/shard_map/ppermute | solution.py:29
  48.3 23.3 %collective-permute-start.1 = (bf16[2,64,1536]{2,1,0:T(8,128)(2,1)S(1)}, bf16[2,64,1536]{2,1,0:T(8,128)(2,1)S(1)}, u32[]{:S(2)}, u32[]{:S(2)}) collective-permute-start(bf16[2,64,1536]{2,1,0:T(8,128)(2,1)S(1)} %bitcast.251), channel_id=1, source_target_pairs={{0,16},{1,17},{16,0},{17,1},{2,18},{3,19},{18,2},{19,3},{4,20},{5,... | collective-permute-start | bytes 1179656 | tf_op jit(solution)/shard_map/ppermute | solution.py:29
  49.4 22.2 %collective-permute-start = (bf16[2,64,1536]{2,1,0:T(8,128)(2,1)S(1)}, bf16[2,64,1536]{2,1,0:T(8,128)(2,1)S(1)}, u32[]{:S(2)}, u32[]{:S(2)}) collective-permute-start(bf16[2,64,1536]{2,1,0:T(8,128)(2,1)S(1)} %bitcast.252), channel_id=1, source_target_pairs={{0,1},{1,0},{16,17},{17,16},{2,3},{3,2},{18,19},{19,18},{4,5},{5,4... | collective-permute-start | bytes 1179656 | tf_op jit(solution)/shard_map/ppermute | solution.py:29
  94.4 78.0 %all-to-all-start.2 = ((bf16[8,704,128]{2,1,0:T(8,128)(2,1)}), bf16[8,704,128]{2,1,0:T(8,128)(2,1)}, u32[]{:S(2)}, u32[]{:S(2)}) async-start(bf16[8,704,128]{2,1,0:T(8,128)(2,1)} %get-tuple-element.57), calls=%async_computation.2 | async-start | bytes 2883584 | tf_op jit(solution)/shard_map/all_to_all | solution.py:611
  99.5 164.2 %all-gather.11.cloned.1.call-start = ((), (), s32[]{:S(2)}) async-start(), calls=%async_computation.14 | async-start | bytes 3538944 | tf_op jit(solution)/shard_map/all_gather | solution.py:83
  99.5 125.1 %collective-permute-start.7 = (bf16[2,2,1,32,1536]{4,3,2,1,0:T(8,128)(2,1)}, bf16[2,2,1,32,1536]{4,3,2,1,0:T(8,128)(2,1)}, u32[]{:S(2)}, u32[]{:S(2)}) collective-permute-start(bf16[2,2,1,32,1536]{4,3,2,1,0:T(8,128)(2,1)} %param.45), channel_id=1, source_target_pairs={{0,1},{1,2},{2,3},{3,4},{4,5},{5,6},{6,7},{8,9},{9,10},{10,11},{11... | collective-permute-start | bytes 1179656 | tf_op jit(solution)/shard_map/ppermute | solution.py:94
  103.6 121.0 %collective-permute-start.6 = (bf16[2,2,1,32,1536]{4,3,2,1,0:T(8,128)(2,1)}, bf16[2,2,1,32,1536]{4,3,2,1,0:T(8,128)(2,1)}, u32[]{:S(2)}, u32[]{:S(2)}) collective-permute-start(bf16[2,2,1,32,1536]{4,3,2,1,0:T(8,128)(2,1)} %param.45), channel_id=1, source_target_pairs={{1,0},{2,1},{3,2},{4,3},{5,4},{6,5},{7,6},{9,8},{10,9},{11,10},{12... | collective-permute-start | bytes 1179656 | tf_op jit(solution)/shard_map/ppermute | solution.py:95
  120.1 79.8 %collective-permute-start.9 = (f32[1,512]{1,0:T(1,128)S(1)}, f32[1,512]{1,0:T(1,128)S(1)}, u32[]{:S(2)}, u32[]{:S(2)}) collective-permute-start(f32[1,512]{1,0:T(1,128)S(1)} %add.267), channel_id=1, source_target_pairs={{0,16},{1,17},{16,0},{17,1},{2,18},{3,19},{18,2},{19,3},{4,20},{5,... | collective-permute-start | bytes 6152 | tf_op jit(solution)/shard_map/ppermute | solution.py:29
  193.5 21.9 %all-to-all-start.3 = ((bf16[8,192,128]{2,1,0:T(8,128)(2,1)}), bf16[8,192,128]{2,1,0:T(8,128)(2,1)}, u32[]{:S(2)}, u32[]{:S(2)}) async-start(bf16[8,192,128]{2,1,0:T(8,128)(2,1)} %get-tuple-element.58), calls=%async_computation.3 | async-start | bytes 786432 | tf_op jit(solution)/shard_map/all_to_all | solution.py:625
  197.7 292.5 %reduce-scatter.4.cloned.1.call-start = ((), (), s32[]{:S(2)}) async-start(), calls=%async_computation.15 | async-start | bytes 10616832 | tf_op jit(solution)/shard_map/reduce_scatter | solution.py:88
  268.6 18.5 %collective-permute-start.18 = (bf16[2,64,1536]{2,1,0:T(8,128)(2,1)S(1)}, bf16[2,64,1536]{2,1,0:T(8,128)(2,1)S(1)}, u32[]{:S(2)}, u32[]{:S(2)}) collective-permute-start(bf16[2,64,1536]{2,1,0:T(8,128)(2,1)S(1)} %bitcast.311), channel_id=1, source_target_pairs={{0,16},{1,17},{16,0},{17,1},{2,18},{3,19},{18,2},{19,3},{4,20},{5,... | collective-permute-start | bytes 1179656 | tf_op jit(solution)/shard_map/ppermute | solution.py:29
  269.9 17.2 %collective-permute-start.17 = (bf16[2,64,1536]{2,1,0:T(8,128)(2,1)S(1)}, bf16[2,64,1536]{2,1,0:T(8,128)(2,1)S(1)}, u32[]{:S(2)}, u32[]{:S(2)}) collective-permute-start(bf16[2,64,1536]{2,1,0:T(8,128)(2,1)S(1)} %bitcast.308), channel_id=1, source_target_pairs={{0,17},{1,16},{16,1},{17,0},{2,19},{3,18},{18,3},{19,2},{4,21},{5,... | collective-permute-start | bytes 1179656 | tf_op jit(solution)/shard_map/ppermute | solution.py:29
  328.1 18.6 %collective-permute-start.23 = (bf16[2,64,1536]{2,1,0:T(8,128)(2,1)S(1)}, bf16[2,64,1536]{2,1,0:T(8,128)(2,1)}, u32[]{:S(2)}, u32[]{:S(2)}) collective-permute-start(bf16[2,64,1536]{2,1,0:T(8,128)(2,1)S(1)} %bitcast.313), channel_id=1, source_target_pairs={{0,17},{1,16},{16,1},{17,0},{2,19},{3,18},{18,3},{19,2},{4,21},{5,... | collective-permute-start | bytes 1179656 | tf_op jit(solution)/shard_map/ppermute | solution.py:29
  329.7 18.0 %collective-permute-start.24 = (bf16[2,64,1536]{2,1,0:T(8,128)(2,1)S(1)}, bf16[2,64,1536]{2,1,0:T(8,128)(2,1)}, u32[]{:S(2)}, u32[]{:S(2)}) collective-permute-start(bf16[2,64,1536]{2,1,0:T(8,128)(2,1)S(1)} %bitcast.310), channel_id=1, source_target_pairs={{0,16},{1,17},{16,0},{17,1},{2,18},{3,19},{18,2},{19,3},{4,20},{5,... | collective-permute-start | bytes 1179656 | tf_op jit(solution)/shard_map/ppermute | solution.py:29
  331.1 17.6 %collective-permute-start.25 = (bf16[2,64,1536]{2,1,0:T(8,128)(2,1)S(1)}, bf16[2,64,1536]{2,1,0:T(8,128)(2,1)}, u32[]{:S(2)}, u32[]{:S(2)}) collective-permute-start(bf16[2,64,1536]{2,1,0:T(8,128)(2,1)S(1)} %bitcast.307), channel_id=1, source_target_pairs={{0,1},{1,0},{16,17},{17,16},{2,3},{3,2},{18,19},{19,18},{4,5},{5,4... | collective-permute-start | bytes 1179656 | tf_op jit(solution)/shard_map/ppermute | solution.py:29
  349.9 21.7 %collective-permute-start.29 = (bf16[2,2,1,32,1536]{4,3,2,1,0:T(8,128)(2,1)S(1)}, bf16[2,2,1,32,1536]{4,3,2,1,0:T(8,128)(2,1)S(1)}, u32[]{:S(2)}, u32[]{:S(2)}) collective-permute-start(bf16[2,2,1,32,1536]{4,3,2,1,0:T(8,128)(2,1)S(1)} %convert_element_type.251), channel_id=1, source_target_pairs={{0,1},{1,2},{2,3},{3,4},{4,5},{5,6},{6,7},{8,9},{9,10},{10,11},{11... | collective-permute-start | bytes 1179656 | tf_op jit(solution)/shard_map/ppermute | solution.py:94
  356.4 22.9 %collective-permute-start.30 = (bf16[2,2,1,32,1536]{4,3,2,1,0:T(8,128)(2,1)S(1)}, bf16[2,2,1,32,1536]{4,3,2,1,0:T(8,128)(2,1)S(1)}, u32[]{:S(2)}, u32[]{:S(2)}) collective-permute-start(bf16[2,2,1,32,1536]{4,3,2,1,0:T(8,128)(2,1)S(1)} %convert_element_type.251), channel_id=1, source_target_pairs={{1,0},{2,1},{3,2},{4,3},{5,4},{6,5},{7,6},{9,8},{10,9},{11,10},{12... | collective-permute-start | bytes 1179656 | tf_op jit(solution)/shard_map/ppermute | solution.py:95
  364.9 19.2 %collective-permute-start.27 = (bf16[2,64,1536]{2,1,0:T(8,128)(2,1)S(1)}, bf16[2,64,1536]{2,1,0:T(8,128)(2,1)S(1)}, u32[]{:S(2)}, u32[]{:S(2)}) collective-permute-start(bf16[2,64,1536]{2,1,0:T(8,128)(2,1)S(1)} %fusion.23), channel_id=1, source_target_pairs={{0,16},{1,17},{16,0},{17,1},{2,18},{3,19},{18,2},{19,3},{4,20},{5,... | collective-permute-start | bytes 1179656 | tf_op jit(solution)/shard_map/ppermute | solution.py:29
  365.7 24.0 %collective-permute-start.28 = (bf16[2,64,1536]{2,1,0:T(8,128)(2,1)S(1)}, bf16[2,64,1536]{2,1,0:T(8,128)(2,1)S(1)}, u32[]{:S(2)}, u32[]{:S(2)}) collective-permute-start(bf16[2,64,1536]{2,1,0:T(8,128)(2,1)S(1)} %fusion.23), channel_id=1, source_target_pairs={{0,1},{1,0},{16,17},{17,16},{2,3},{3,2},{18,19},{19,18},{4,5},{5,4... | collective-permute-start | bytes 1179656 | tf_op jit(solution)/shard_map/ppermute | solution.py:29
  394.5 29.9 %all-to-all-start.5 = ((bf16[8,192,128]{2,1,0:T(8,128)(2,1)}), bf16[8,192,128]{2,1,0:T(8,128)(2,1)}, u32[]{:S(2)}, u32[]{:S(2)}) async-start(bf16[8,192,128]{2,1,0:T(8,128)(2,1)} %get-tuple-element.71), calls=%async_computation.5 | async-start | bytes 786432 | tf_op jit(solution)/shard_map/all_to_all | solution.py:698
  447.6 42.6 %all-to-all-start.6 = ((bf16[8,704,128]{2,1,0:T(8,128)(2,1)}), bf16[8,704,128]{2,1,0:T(8,128)(2,1)}, u32[]{:S(2)}, u32[]{:S(2)}) async-start(bf16[8,704,128]{2,1,0:T(8,128)(2,1)} %shard_map.352), calls=%async_computation.6 | async-start | bytes 2883584 | tf_op jit(solution)/shard_map/all_to_all | solution.py:757
  453.2 76.7 %reduce-scatter.6.cloned.1.call-start = ((), (), s32[]{:S(2)}) async-start(), calls=%async_computation.16 | async-start | bytes 2359296 | tf_op jit(solution)/shard_map/reduce_scatter | solution.py:88
  490.3 129.9 %reduce-scatter.8.cloned.1.call-start = ((), (), s32[]{:S(2)}) async-start(), calls=%async_computation.17 | async-start | bytes 3981312 | tf_op jit(solution)/shard_map/reduce_scatter | solution.py:88
  531.6 28.5 %collective-permute-start.41 = (bf16[512,384]{0,1:T(8,128)(2,1)}, bf16[512,384]{0,1:T(8,128)(2,1)}, u32[]{:S(2)}, u32[]{:S(2)}) collective-permute-start(bf16[512,384]{0,1:T(8,128)(2,1)} %bitcast.322), channel_id=1, source_target_pairs={{0,0},{1,2},{2,8},{3,10},{4,16},{5,18},{6,24},{7,26},{8,1},{9,3},{... | collective-permute-start | bytes 1179656 | tf_op jit(solution)/shard_map/ppermute | solution.py:69
  540.5 21.6 %collective-permute-start.37 = (bf16[2,64,1536]{2,1,0:T(8,128)(2,1)}, bf16[2,64,1536]{2,1,0:T(8,128)(2,1)}, u32[]{:S(2)}, u32[]{:S(2)}) collective-permute-start(bf16[2,64,1536]{2,1,0:T(8,128)(2,1)} %bitcast.83), channel_id=1, source_target_pairs={{0,1},{1,0},{16,17},{17,16},{2,3},{3,2},{18,19},{19,18},{4,5},{5,4... | collective-permute-start | bytes 1179656 | tf_op jit(solution)/shard_map/ppermute | solution.py:29
  544.0 18.2 %collective-permute-start.36 = (bf16[2,64,1536]{2,1,0:T(8,128)(2,1)}, bf16[2,64,1536]{2,1,0:T(8,128)(2,1)}, u32[]{:S(2)}, u32[]{:S(2)}) collective-permute-start(bf16[2,64,1536]{2,1,0:T(8,128)(2,1)} %bitcast.82), channel_id=1, source_target_pairs={{0,16},{1,17},{16,0},{17,1},{2,18},{3,19},{18,2},{19,3},{4,20},{5,... | collective-permute-start | bytes 1179656 | tf_op jit(solution)/shard_map/ppermute | solution.py:29
  544.0 18.3 %collective-permute-start.35 = (bf16[2,64,1536]{2,1,0:T(8,128)(2,1)}, bf16[2,64,1536]{2,1,0:T(8,128)(2,1)}, u32[]{:S(2)}, u32[]{:S(2)}) collective-permute-start(bf16[2,64,1536]{2,1,0:T(8,128)(2,1)} %bitcast.81), channel_id=1, source_target_pairs={{0,17},{1,16},{16,1},{17,0},{2,19},{3,18},{18,3},{19,2},{4,21},{5,... | collective-permute-start | bytes 1179656 | tf_op jit(solution)/shard_map/ppermute | solution.py:29
  554.1 51.5 %collective-permute-start.40 = (bf16[3072,128]{1,0:T(8,128)(2,1)}, bf16[3072,128]{1,0:T(8,128)(2,1)}, u32[]{:S(2)}, u32[]{:S(2)}) collective-permute-start(bf16[3072,128]{1,0:T(8,128)(2,1)} %slice.285), channel_id=1, source_target_pairs={{0,0},{1,8},{2,2},{3,10},{4,4},{5,12},{6,6},{7,14},{8,1},{9,9},{10... | collective-permute-start | bytes 2359304 | tf_op jit(solution)/shard_map/ppermute | solution.py:69
  579.1 22.6 %all-to-all-start.7 = ((f32[32,7,128]{2,1,0:T(8,128)}), f32[32,7,128]{2,1,0:T(8,128)}, u32[]{:S(2)}, u32[]{:S(2)}) async-start(f32[32,7,128]{2,1,0:T(8,128)} %reshape.737), calls=%async_computation.10 | async-start | bytes 262144 | tf_op jit(solution)/shard_map/all_to_all | solution.py:806
  (132 other events, 2048.8 us)
Sparse Core Ops, SparseCore 0:
  21.3 41.7 all-gather.4
  65.4 27.0 all-gather.6
  94.1 92.5 all-gather.8
  188.2 49.0 all-gather.10
  348.8 117.8 reduce-scatter.3
  490.4 39.4 reduce-scatter.5
  532.2 51.6 reduce-scatter.7

commit v4 on v3

--- a/solution.py
+++ b/solution.py
@@ -30,17 +30,16 @@
 
 
 def team_sum(value):
-    value = value + swap(value, 1)
-    return value + swap(value, 2)
+    one, two, three = (swap(value, k) for k in (1, 2, 3))
+    return (value + one) + (two + three)
 
 
 def token_sum(value):
     blocks = value.reshape(value.shape[0], 4, -1)
-    got = swap(blocks, 1).reshape(value.shape[0], 2, 2, -1)
-    blocks = blocks + got[:, :, ::-1].reshape(blocks.shape)
-    got = swap(blocks, 2)
-    blocks = blocks + jnp.concatenate([got[:, 2:], got[:, :2]], axis=1)
-    return blocks.reshape(value.shape)
+    one, two, three = (swap(blocks, k) for k in (1, 2, 3))
+    pairs = one.reshape(value.shape[0], 2, 2, -1)[:, :, ::-1].reshape(blocks.shape)
+    halves = jnp.concatenate([two[:, 2:], two[:, :2]], axis=1)
+    return ((blocks + pairs) + (halves + three[:, ::-1])).reshape(value.shape)
 
 
 def beside(moved, work):
@@ -428,7 +427,7 @@
     dv_ref[...] = dv
 
 
-def call(kernel, outs, *args, scratch=(), flops=0):
+def call(kernel, outs, *args, scratch=(), flops=0, grant=16):
     size = sum(math.prod(a.shape) * a.dtype.itemsize for a in (*args, *outs))
     spec = pl.BlockSpec(memory_space=pltpu.VMEM)
     return pl.pallas_call(
@@ -437,7 +436,7 @@
         in_specs=[spec] * len(args),
         out_specs=[spec] * len(outs),
         scratch_shapes=list(scratch),
-        compiler_params=pltpu.CompilerParams(vmem_limit_bytes=56 << 20),
+        compiler_params=pltpu.CompilerParams(vmem_limit_bytes=grant << 20),
         cost_estimate=pl.CostEstimate(flops=flops, bytes_accessed=size, transcendentals=flops // 256),
     )(*args)
 
@@ -453,11 +452,38 @@
         out_shape=outs,
         in_specs=[kinds[c] for c in specs[0]],
         out_specs=[kinds[c] for c in specs[1]],
-        compiler_params=pltpu.CompilerParams(vmem_limit_bytes=40 << 20),
+        compiler_params=pltpu.CompilerParams(vmem_limit_bytes=16 << 20),
         cost_estimate=pl.CostEstimate(
             flops=12 * len(args) * 256 * 256 * 128, bytes_accessed=4 << 20, transcendentals=12 << 16
         ),
     )(*args)
+
+
+def product_kernel(left_ref, right_ref, out_ref):
+    term = dot_nt(left_ref[...], right_ref[...])
+
+    @pl.when(pl.program_id(0) == 0)
+    def _():
+        out_ref[...] = term
+
+    @pl.when(pl.program_id(0) > 0)
+    def _():
+        out_ref[...] += term
+
+
+def product(left, right):
+    (rows, deep), (columns, _) = left.shape, right.shape
+    return pl.pallas_call(
+        product_kernel,
+        grid=(deep // 512,),
+        out_shape=shaped((rows, columns)),
+        in_specs=[pl.BlockSpec((rows, 512), lambda k: (0, k)), pl.BlockSpec((columns, 512), lambda k: (0, k))],
+        out_specs=pl.BlockSpec((rows, columns), lambda k: (0, 0)),
+        compiler_params=pltpu.CompilerParams(vmem_limit_bytes=20 << 20),
+        cost_estimate=pl.CostEstimate(
+            flops=2 * rows * columns * deep, bytes_accessed=2 * deep * (rows + columns), transcendentals=0
+        ),
+    )(left, right)
 
 
 def shaped(shape, dtype=F32):
@@ -538,7 +564,6 @@
         return lax.dot_general(weight, cap2, (((0,), (1,)), ((), ())), preferred_element_type=F32).astype(BF16)
 
     cut_qkv = by_columns([w_query, w_key, w_value])
-    cut_gu = by_columns([w_gate, w_up])
 
     half_width = width // 2
     frequencies = jnp.exp(-math.log(THETA) * jnp.arange(half_width, dtype=F32) / half_width)
@@ -550,16 +575,18 @@
     used = note.shape[0]
     note = jnp.pad(note, (0, -used % 512)).reshape(1, -1, 128)
     note = lax.all_to_all(jnp.broadcast_to(note, (n_all,) + note.shape[1:]), ALL, 0, 0)
+    note, (w_gate, w_up) = beside(note, (w_gate, w_up))
+    cut_gu = by_columns([w_gate, w_up])
     note = note.reshape(n_all, -1)
     x_own = tokens.reshape(clips, local, width)
     x_flat = x_own.astype(F32)
     x_group, _ = team_gather(x_own)
     w_qkv = in_order(group_gather(cut_qkv))
-    side = jnp.concatenate([cap_columns(w_cap_key), cap_columns(w_cap_value), w_out], axis=1)
-    side = group_gather(exchange(side))
     tokens_c = clips * caps
-    w_gu = group_gather(cut_gu)
-    w_dn = group_gather(exchange(w_down))
+    blank = jnp.zeros((rows, width - 2 * tokens_c), BF16)
+    cap_rows = jnp.concatenate([cap_columns(w_cap_key), cap_columns(w_cap_value), blank], axis=1)
+    side = group_gather(exchange(jnp.concatenate([w_out, cap_rows])))
+    down_rows = exchange(w_down)
     mod_full = note[:, : clips * mod_cols].reshape(n_all, clips, mod_cols)
     mod_full = mod_full.transpose(1, 0, 2).reshape(clips, 4, width)
     scale_a, gate_a, scale_f, gate_f = (mod_full[:, i] for i in range(4))
@@ -570,7 +597,6 @@
     chosen = (order[None, :] == (me ^ order)[:, None]).astype(F32)
     positions = jnp.sum(chosen[:, :, None] * positions.reshape(1, group, -1), axis=1)
 
-    above_g, below_g = row_neighbours(grad_out)
     gains = norm_gains
     own_gains = lax.dynamic_slice(gains, (4, me * heads_w), (3, heads_w))
     own_gate = jnp.tanh(lax.dynamic_slice(mix_coefs, (0, me * heads_w), (1, heads_w)))
@@ -606,9 +632,10 @@
         cosine,
         sine,
     )
-    send, side = beside(send, side)
-    k_pre_t, v_cap_t, w_o = side[:, :tokens_c], side[:, tokens_c : 2 * tokens_c], side[:, 2 * tokens_c :]
-    got = lax.all_to_all(send, PLANE, 0, 0)
+    got, (side, cut_gu, down_rows, (above_g, below_g)) = beside(
+        lax.all_to_all(send, PLANE, 0, 0), (side, cut_gu, down_rows, row_neighbours(grad_out))
+    )
+    w_gu = group_gather(cut_gu)
     kv_all = got
     if n_far > 1:
         kv_all = lax.all_gather(got, "far", axis=0, tiled=True)
@@ -621,10 +648,14 @@
         got,
         scratch=[pltpu.VMEM((2, 128, keys), BF16)],
         flops=2 * work,
-    )
+        grant=24 if n_far == 1 else 56,
+    )
+    o_pack, side = beside(o_pack, side)
     o_back = lax.all_to_all(o_pack, PLANE, 0, 0)
-    o_back, w_gu = beside(o_back, w_gu)
-    w_gu = in_order(w_gu)
+    side = side.reshape(n_rows, -1, width)
+    w_o = side[:, :rows].reshape(-1, width)
+    k_pre_t = side[:, rows:, :tokens_c].reshape(-1, tokens_c)
+    v_cap_t = side[:, rows:, tokens_c : 2 * tokens_c].reshape(-1, tokens_c)
 
     usable = (jnp.arange(caps)[None, :] < cap_len[:, None]) & (cap_mask > 0)
     bias = usable.astype(F32).reshape(clips * caps, 1)
@@ -640,14 +671,17 @@
     out_cross = out_cross.reshape(count, heads_w)
     (attn_mix,) = call(mix_kernel, [shaped((count, heads_w), BF16)], o_back, out_cross, own_gate)
 
-    y_one, _ = team_scatter(mm(attn_mix, w_o).reshape(group, clips, local, width))
+    y_one, (w_gu, down_rows) = team_scatter(
+        mm(attn_mix, w_o).reshape(group, clips, local, width), (w_gu, down_rows)
+    )
+    w_dn = group_gather(down_rows)
 
     def mid_piece(x_in, y_in, gain_two, gate_in, gain_three, scale_in):
         h_mid = x_in + jnp.tanh(gate_in)[:, None, :] * rms_norm(y_in, gain_two)
         return (h_mid, rms_norm(h_mid, gain_three) * (1.0 + scale_in[:, None, :]))
 
     (h_mid, f_in32), mid_back = jax.vjp(mid_piece, x_flat, y_one, gains[1], gate_a, gains[2], scale_f)
-    f_in, _ = team_gather(f_in32.astype(BF16))
+    f_in, w_gu = team_gather(f_in32.astype(BF16), in_order(w_gu))
     f_in = f_in.reshape(count, width)
     gate_up = mm(f_in, w_gu)
 
@@ -671,7 +705,7 @@
     d_z_all = d_z_all.reshape(count, width)
     d_hidden = lax.dot_general(d_z_all, w_dn, (((1,), (1,)), ((), ())), preferred_element_type=F32)
     d_gu = jnp.concatenate([d.astype(BF16) for d in act_back(d_hidden)], axis=1)
-    d_f_in = lax.dot_general(d_gu, w_gu, (((1,), (1,)), ((), ())), preferred_element_type=F32)
+    d_f_in = product(d_gu, w_gu)
     def term(left, right):
         return lax.dot_general(left, right, (((0,), (0,)), ((), ())), preferred_element_type=F32).astype(BF16)
 
@@ -684,11 +718,12 @@
         f_in,
         d_gu,
         flops=6 * count * width * ff_w,
+        grant=32,
     )
     d_f_in, ff_terms = team_scatter(d_f_in.reshape(group, clips, local, width), ff_terms)
     ff_sum = group_scatter(ff_terms)
     d_x_mid, d_y_one, d_g_two, d_gate_a, d_g_three, d_scale_f = mid_back((d_h_end, d_f_in))
-    d_y_group, (above, below) = team_gather(d_y_one.astype(BF16), (above, below))
+    d_y_group, _ = team_gather(d_y_one.astype(BF16))
     d_y_group = d_y_group.reshape(count, width)
     d_attn = lax.dot_general(d_y_group, w_o, (((1,), (1,)), ((), ())), preferred_element_type=F32)
 
@@ -696,10 +731,6 @@
         split_kernel, [shaped((RING, 192, 128), BF16), shaped((count, heads_w), BF16)], d_attn, own_gate
     )
     d_got = lax.all_to_all(d_pack, PLANE, 0, 0)
-    above, below = above.astype(F32), below.astype(F32)
-    output = (y_grid + mix_coefs[1] * above + mix_coefs[2] * below).astype(BF16)
-    d_above = jnp.sum(g_center * above, axis=(0, 1, 2, 3))
-    d_below = jnp.sum(g_center * below, axis=(0, 1, 2, 3))
     d_mix_gate = jnp.sum(d_attn * out_cross, axis=0) * (1.0 - own_gate[0] * own_gate[0])
     d_q_cross, d_k_cap, d_v_cap = cross_call(
         cross_back_kernel,
@@ -711,6 +742,41 @@
         bias,
         d_cross.reshape(q_cap4.shape),
     )
+    d_got, (d_q_cross, d_k_cap, d_v_cap) = beside(d_got, (d_q_cross, d_k_cap, d_v_cap))
+    back_scratch = [pltpu.VMEM((2, keys, 128), F32), pltpu.VMEM((2, 128, keys), BF16)]
+    if n_far == 1:
+        (d_send,) = call(
+            functools.partial(self_back_kernel, True),
+            [shaped((RING, 704, 128), BF16)],
+            kv_all,
+            got,
+            d_got,
+            o_t,
+            lse,
+            scratch=back_scratch,
+            flops=5 * work,
+            grant=32 if n_far == 1 else 60,
+        )
+    else:
+        d_kv, d_q = call(
+            functools.partial(self_back_kernel, False),
+            [shaped((kv_all.shape[0], 512, 128), BF16), shaped((RING, 192, 128), BF16)],
+            kv_all,
+            got,
+            d_got,
+            o_t,
+            lse,
+            scratch=back_scratch,
+            flops=5 * work,
+            grant=32 if n_far == 1 else 60,
+        )
+        d_kv = lax.psum_scatter(d_kv, "far", scatter_dimension=0, tiled=True)
+        d_send = jnp.concatenate([d_kv, d_q], axis=1)
+    d_send, (above, below) = beside(d_send, (above, below))
+    above, below = above.astype(F32), below.astype(F32)
+    output = (y_grid + mix_coefs[1] * above + mix_coefs[2] * below).astype(BF16)
+    d_above = jnp.sum(g_center * above, axis=(0, 1, 2, 3))
+    d_below = jnp.sum(g_center * below, axis=(0, 1, 2, 3))
     cap_dot = team_sum(jnp.sum(d_k_cap * gain_cap * k_pre_t, axis=0, keepdims=True))
     wide = heads_w // n_rows
     tile = width // n_rows
@@ -725,38 +791,24 @@
         cap_dot,
         flops=2 * count * width * heads_w,
     )
-    d_got, (d_q_cross, out_terms) = beside(d_got, (d_q_cross, out_terms))
-    back_scratch = [pltpu.VMEM((2, keys, 128), F32), pltpu.VMEM((2, 128, keys), BF16)]
-    if n_far == 1:
-        (d_send,) = call(
-            functools.partial(self_back_kernel, True),
-            [shaped((RING, 704, 128), BF16)],
-            kv_all,
-            got,
-            d_got,
-            o_t,
-            lse,
-            scratch=back_scratch,
-            flops=5 * work,
-        )
-    else:
-        d_kv, d_q = call(
-            functools.partial(self_back_kernel, False),
-            [shaped((kv_all.shape[0], 512, 128), BF16), shaped((RING, 192, 128), BF16)],
-            kv_all,
-            got,
-            d_got,
-            o_t,
-            lse,
-            scratch=back_scratch,
-            flops=5 * work,
-        )
-        d_kv = lax.psum_scatter(d_kv, "far", scatter_dimension=0, tiled=True)
-        d_send = jnp.concatenate([d_kv, d_q], axis=1)
-    d_recv, (output, d_above, d_below, ff_sum) = beside(
-        lax.all_to_all(d_send, PLANE, 0, 0), (output, d_above, d_below, ff_sum)
-    )
-    out_terms, ff_sum = beside(out_terms, ff_sum)
+
+    def spread(block):
+        return lax.dynamic_update_slice(jnp.zeros((width,), F32), block, (me * heads_w,))
+
+    def owners_sum(mods, rows_in):
+        first = mods.reshape(clips, -1, mod_cols).transpose(1, 0, 2).reshape(-1, clips * mod_cols)
+        first = jnp.pad(first, ((0, n_all - first.shape[0]), (0, 0)))
+        other = lax.optimization_barrier(jnp.stack(rows_in))
+        other = other.reshape(len(rows_in), n_all, share).transpose(1, 0, 2).reshape(n_all, -1)
+        both = jnp.concatenate([first, other], axis=1)
+        both = jnp.pad(both, ((0, 0), (0, -both.shape[1] % 128))).reshape(n_all, -1, 128)
+        both = jnp.sum(lax.all_to_all(both, ALL, 0, 0), axis=0).reshape(-1)
+        cut = clips * mod_cols
+        return both[:cut].reshape(clips, mod_cols), both[cut : cut + len(rows_in) * share].reshape(-1, share)
+
+    d_recv, (output, out_terms, ff_sum) = beside(
+        lax.all_to_all(d_send, PLANE, 0, 0), (output, out_terms, ff_sum)
+    )
     out_sum = group_scatter(out_terms)
     d_qn, d_kn, d_v = call(
         back_kernel,
@@ -774,20 +826,17 @@
     d_q_low = (rq * a_q - q_zero * (rq * rq * rq * dots[:, 0:1])).astype(BF16)
     d_k_low = (rk * a_k - k_zero * (rk * rk * rk * dots[:, 1:2])).astype(BF16)
     d_qkv = jnp.concatenate([d_q_low, d_k_low, d_v], axis=1)
-    d_qkv, term_qkv = beside(d_qkv, term(h_in, d_qkv))
-    term_qkv, out_sum = beside(term_qkv, out_sum)
+    d_h_in = lax.dot_general(d_qkv, w_qkv, (((1,), (1,)), ((), ())), preferred_element_type=F32)
+    sum_down = to_owner(from_chunks(ff_sum[None, : ff_rows[0]], w_down.shape[0] * group))
+    d_h_in, (term_qkv, out_sum, sum_down) = team_scatter(
+        d_h_in.reshape(group, clips, local, width), (term(h_in, d_qkv), out_sum, sum_down)
+    )
     qkv_sum = group_scatter(term_qkv)
-    d_h_in = lax.dot_general(d_qkv, w_qkv, (((1,), (1,)), ((), ())), preferred_element_type=F32)
-    d_h_in, _ = team_scatter(d_h_in.reshape(group, clips, local, width))
     d_x_pre, d_g_zero, d_scale_a = pre_back(d_h_in)
     grad_tokens = (d_x_pre + d_x_mid).reshape(tokens.shape)
 
-    def spread(block):
-        return lax.dynamic_update_slice(jnp.zeros((width,), F32), block, (me * heads_w,))
-
-    d_mod = jnp.concatenate([d_scale_a, d_gate_a, d_scale_f, d_gate_f], axis=1)
-    d_mod = d_mod.reshape(clips, n_all, mod_cols).transpose(1, 0, 2).reshape(n_all, -1)
-    rest = jnp.stack(
+    d_mod, sums = owners_sum(
+        jnp.concatenate([d_scale_a, d_gate_a, d_scale_f, d_gate_f], axis=1),
         [
             d_g_zero,
             d_g_two,
@@ -798,42 +847,37 @@
             spread(d_mix_gate),
             d_above,
             d_below,
-        ]
-    )
-    rest = rest.reshape(9, n_all, share).transpose(1, 0, 2).reshape(n_all, -1)
-    small = jnp.concatenate([d_mod, rest], axis=1)
-    small = jnp.pad(small, ((0, 0), (0, -small.shape[1] % 128))).reshape(n_all, -1, 128)
-    small = jnp.sum(lax.all_to_all(small, ALL, 0, 0), axis=0).reshape(-1)
-    d_mod = small[: clips * mod_cols].reshape(clips, mod_cols)
-    rest = small[clips * mod_cols : clips * mod_cols + 9 * share].reshape(9, share)
+        ],
+    )
     d_w_mod = lax.dot_general(
         step_embed, d_mod.astype(BF16), (((0,), (0,)), ((), ())), preferred_element_type=F32
     )
-    three = heads_w // 128
-    mine = w_down.shape[0] * group
-    sum_down = to_owner(from_chunks(ff_sum[None, : ff_rows[0]], mine)).astype(F32)
-    sum_gate, sum_up = jnp.split(exchange(ff_sum[ff_rows[0] :]), 2)
     cap_sum = from_chunks(out_sum[None, :cut].astype(F32), 2 * wide + 16)
-    sum_out = to_owner(from_chunks(out_sum[None, cut:], tile)).astype(F32)
-    qkv_sum = exchange(qkv_sum).astype(F32)
-
-    def result(block):
-        return from_chunks(block[None], tile).astype(F32)
-
     d_k_own, d_v_own, cap_dot = cap_sum[:wide], cap_sum[wide : 2 * wide], cap_sum[2 * wide : 2 * wide + 1]
     k_own = lax.dynamic_slice(k_pre_t, (my_member * wide, 0), (wide, clips * caps))
     g_own = lax.dynamic_slice(gain_cap, (my_member * wide, 0), (wide, 1))
     d_g_cap = exchange(jnp.sum(d_k_own * k_own * r_cap, axis=1)[None])
     d_k_zero_cap = r_cap * g_own * d_k_own - k_own * (r_cap * r_cap * r_cap * cap_dot / width)
     d_caps = exchange(jnp.concatenate([d_k_zero_cap, d_v_own]).astype(BF16))
+    sum_gu = exchange(ff_sum[ff_rows[0] :])
+    sum_out = to_owner(from_chunks(out_sum[None, cut:], tile))
+    d_w_mod, qkv_sum = beside(d_w_mod, exchange(qkv_sum))
+    qkv_sum, sum_gu, sum_out, d_caps, d_g_cap = lax.optimization_barrier(
+        (qkv_sum, sum_gu, sum_out, d_caps, d_g_cap)
+    )
+    qkv_sum = qkv_sum.astype(F32)
+    sum_gate, sum_up = jnp.split(sum_gu, 2)
+
+    def result(block):
+        return from_chunks(block[None], tile).astype(F32)
 
     def cap_weight(d):
         return lax.dot_general(cap2, d, (((0,), (1,)), ((), ())), preferred_element_type=F32)
 
     d_w_cap_key = cap_weight(d_caps[:wide])
     d_w_cap_value = cap_weight(d_caps[wide:])
-    d_gains = jnp.concatenate([rest[:6], d_g_cap], axis=0)
-    d_mixes = rest[6:]
+    d_gains = jnp.concatenate([sums[:6], d_g_cap], axis=0)
+    d_mixes = sums[6:]
 
     return (
         output,
@@ -841,10 +885,10 @@
         qkv_sum[:, :heads_w],
         qkv_sum[:, heads_w : 2 * heads_w],
         qkv_sum[:, 2 * heads_w :],
-        sum_out,
+        sum_out.astype(F32),
         result(sum_gate),
         result(sum_up),
-        sum_down,
+        sum_down.astype(F32),
         d_w_cap_key,
         d_w_cap_value,
         d_w_mod,

time: 651 us -> 632 us (0.971)
  the two profiles are of different devices: /device:TPU:2 before, /device:TPU:5 now
where the time goes in v4:
time: 632 us; the launch traced here: 620 us
  waiting for transfers between devices  211 us (33%)
  starting transfers between devices  138 us (22%)
  local copies, waits for them, and re-layouts  84.5 us (13%)
  Pallas kernels  81.3 us (13%)
  other arithmetic  48.4 us (8%)
  matrix products  30.3 us (5%)
  between operations  17.2 us (3%)
  blocking collectives  9.6 us (2%)
    ppermute x36, waiting for transfers between devices, swap(): return lax.ppermute(value, TEAM, [(i, i ^ bits) for i in range(4)])  110 us
    pallas_call x8, Pallas kernels, call(): pl.pallas_call(kernel, out_shape=outs, in_specs=[spec] * len(args), out_s...  55.9 us
    unnamed x249, local copies, waits for them, and re-layouts  45.7 us
    ppermute x8, starting transfers between devices, relocate(): return lax.ppermute(block, ALL, pairs)  43.5 us
    all_to_all x1, waiting for transfers between devices, body(): lax.all_to_all(d_send, PLANE, 0, 0)  43.4 us
    ppermute x36, starting transfers between devices, swap(): return lax.ppermute(value, TEAM, [(i, i ^ bits) for i in range(4)])  32.3 us
    all_to_all x1, waiting for transfers between devices, body(): lax.all_to_all(send, PLANE, 0, 0)  17.6 us
    pallas_call x1, Pallas kernels, product(): pl.pallas_call(product_kernel, grid=(deep // 512,), out_shape=shaped((row...  14.5 us
  transfers between devices with their start and end apart: 62, of which 24 were waited for; matrix products, arithmetic and copies ran while one was open for 16% of the time, Pallas kernels for 11%

profile of v4, /device:TPU:5, one launch (start us, length us, event | category | flops | bytes accessed | tf_op | source)
XLA Modules:
  0.0 620.0 jit_solution(10529005727253582751)
XLA Ops:
  10.5 9.6 %all_to_all.40 = bf16[4,48,1152]{2,1,0:T(8,128)(2,1)} all-to-all(bf16[4,48,1152]{2,1,0:T(8,128)(2,1)S(1)} %copy.131), channel_id=1, replica_groups=mesh['y'=2,'core'=2,'far'=1,'z'=4,'x'=2] {'y','x'}, dimensions={0} | all-to-all | bytes 884736 | tf_op jit(solution)/shard_map/all_to_all | solution.py:556
  24.9 7.5 %all-to-all-start = ((f32[32,4,128]{2,1,0:T(4,128)}), f32[32,4,128]{2,1,0:T(4,128)S(1)}, u32[]{:S(2)}, u32[]{:S(2)}) async-start(f32[32,4,128]{2,1,0:T(4,128)} %broadcast_in_dim.29), calls=%async_computation | async-start | bytes 131072 | tf_op jit(solution)/shard_map/all_to_all | solution.py:577
  91.2 5.2 collective-permute-start.8
  98.7 6.0 collective-permute-done.8
  108.9 17.6 %all-to-all-done.2.kv_ref.q_ref = bf16[8,704,128]{2,1,0:T(8,128)(2,1)S(1)} async-done(((bf16[8,704,128]{2,1,0:T(8,128)(2,1)}), bf16[8,704,128]{2,1,0:T(8,128)(2,1)S(1)}, u32[]{:S(2)}, u32[]{:S(2)}) %all-to-all-start.2) | async-done | bytes 1441824 | tf_op jit(solution)/shard_map/all_to_all | solution.py:636
  129.0 18.3 %shard_map.345 = (bf16[8,192,128]{2,1,0:T(8,128)(2,1)S(1)}, f32[12,64,256]{2,1,0:T(8,128)S(1)}, f32[12,1,256]{2,1,0:T(1,128)S(1)}) custom-call(bf16[8,704,128]{2,1,0:T(8,128)(2,1)S(1)} %all-to-all-done.2.kv_ref.q_ref, bf16[8,704,128]{2,1,0:T(8,128)(2,1)S(1)} %all-to-all-done.2.kv_ref.q_ref), custom_call_target="tpu_custom_call" | custom-call | flops 3221225472 | bytes 4075520 | tf_op jit(solution)/shard_map/pallas_call | solution.py:433
  152.2 12.5 %all-to-all-start.4 = ((bf16[8,192,128]{2,1,0:T(8,128)(2,1)}), bf16[8,192,128]{2,1,0:T(8,128)(2,1)S(1)}, u32[]{:S(2)}, u32[]{:S(2)}) async-start(bf16[8,192,128]{2,1,0:T(8,128)(2,1)} %copy-done.33), calls=%async_computation.4 | async-start | bytes 786432 | tf_op jit(solution)/shard_map/all_to_all | solution.py:654
  173.9 12.8 %all-to-all-done.4.o_ref = bf16[8,192,128]{2,1,0:T(8,128)(2,1)S(1)} async-done(((bf16[8,192,128]{2,1,0:T(8,128)(2,1)}), bf16[8,192,128]{2,1,0:T(8,128)(2,1)S(1)}, u32[]{:S(2)}, u32[]{:S(2)}) %all-to-all-start.4) | async-done | bytes 393248 | tf_op jit(solution)/shard_map/all_to_all | solution.py:654
  193.8 8.8 %collective-permute-done.13 = bf16[2,64,1536]{2,1,0:T(8,128)(2,1)S(1)} collective-permute-done((bf16[2,64,1536]{2,1,0:T(8,128)(2,1)S(1)}, bf16[2,64,1536]{2,1,0:T(8,128)(2,1)S(1)}, u32[]{:S(2)}, u32[]{:S(2)}) %collective-permute-start.13) | collective-permute-done | bytes 393248 | tf_op jit(solution)/shard_map/ppermute | solution.py:29
  202.5 8.9 %collective-permute-done.14 = bf16[2,64,1536]{2,1,0:T(8,128)(2,1)S(1)} collective-permute-done((bf16[2,64,1536]{2,1,0:T(8,128)(2,1)S(1)}, bf16[2,64,1536]{2,1,0:T(8,128)(2,1)S(1)}, u32[]{:S(2)}, u32[]{:S(2)}) %collective-permute-start.14) | collective-permute-done | bytes 393248 | tf_op jit(solution)/shard_map/ppermute | solution.py:29
  220.7 7.3 %collective-permute-done.16 = bf16[2,64,1536]{2,1,0:T(8,128)(2,1)S(1)} collective-permute-done((bf16[2,64,1536]{2,1,0:T(8,128)(2,1)S(1)}, bf16[2,64,1536]{2,1,0:T(8,128)(2,1)S(1)}, u32[]{:S(2)}, u32[]{:S(2)}) %collective-permute-start.16) | collective-permute-done | bytes 393248 | tf_op jit(solution)/shard_map/ppermute | solution.py:29
  227.9 9.2 %collective-permute-done.17 = bf16[2,64,1536]{2,1,0:T(8,128)(2,1)S(1)} collective-permute-done((bf16[2,64,1536]{2,1,0:T(8,128)(2,1)S(1)}, bf16[2,64,1536]{2,1,0:T(8,128)(2,1)S(1)}, u32[]{:S(2)}, u32[]{:S(2)}) %collective-permute-start.17) | collective-permute-done | bytes 393248 | tf_op jit(solution)/shard_map/ppermute | solution.py:29
  254.7 7.6 %collective-permute-done.21 = bf16[2,64,1536]{2,1,0:T(8,128)(2,1)S(1)} collective-permute-done((bf16[2,64,1536]{2,1,0:T(8,128)(2,1)S(1)}, bf16[2,64,1536]{2,1,0:T(8,128)(2,1)S(1)}, u32[]{:S(2)}, u32[]{:S(2)}) %collective-permute-start.21) | collective-permute-done | bytes 393248 | tf_op jit(solution)/shard_map/ppermute | solution.py:29
  262.3 9.3 %collective-permute-done.20 = bf16[2,64,1536]{2,1,0:T(8,128)(2,1)S(1)} collective-permute-done((bf16[2,64,1536]{2,1,0:T(8,128)(2,1)S(1)}, bf16[2,64,1536]{2,1,0:T(8,128)(2,1)S(1)}, u32[]{:S(2)}, u32[]{:S(2)}) %collective-permute-start.20) | collective-permute-done | bytes 393248 | tf_op jit(solution)/shard_map/ppermute | solution.py:29
  276.5 7.5 %collective-permute-done.24 = bf16[2,64,1536]{2,1,0:T(8,128)(2,1)S(1)} collective-permute-done((bf16[2,64,1536]{2,1,0:T(8,128)(2,1)S(1)}, bf16[2,64,1536]{2,1,0:T(8,128)(2,1)S(1)}, u32[]{:S(2)}, u32[]{:S(2)}) %collective-permute-start.24) | collective-permute-done | bytes 393248 | tf_op jit(solution)/shard_map/ppermute | solution.py:29
  284.0 10.2 %collective-permute-done.23 = bf16[2,64,1536]{2,1,0:T(8,128)(2,1)S(1)} collective-permute-done((bf16[2,64,1536]{2,1,0:T(8,128)(2,1)S(1)}, bf16[2,64,1536]{2,1,0:T(8,128)(2,1)S(1)}, u32[]{:S(2)}, u32[]{:S(2)}) %collective-permute-start.23) | collective-permute-done | bytes 393248 | tf_op jit(solution)/shard_map/ppermute | solution.py:29
  297.2 14.5 %shard_map.348 = f32[512,1536]{1,0:T(8,128)S(1)} custom-call(bf16[512,2048]{1,0:T(8,128)(2,1)S(1)} %pad_maximum_fusion.left_ref.dgu_ref, bf16[1536,2048]{1,0:T(8,128)(2,1)S(1)} %bitcast.244), custom_call_target="tpu_custom_call" | custom-call | flops 3221225472 | bytes 8388608 | tf_op jit(solution)/shard_map/pallas_call | solution.py:476
  316.2 8.6 %shard_map.349 = bf16[8,4608,128]{2,1,0:T(8,128)(2,1)S(1)} custom-call(bf16[512,1024]{1,0:T(8,128)(2,1)S(1)} %copy-done.26, bf16[512,1536]{1,0:T(8,128)(2,1)S(1)} %bitcast.249, bf16[512,1536]{1,0:T(8,128)(2,1)S(1)} %bitcast.247, bf16[512,2048]{1,0:T(8,128)(2,1)S(1)} %pad_maximum_fusion.left_ref.dgu_ref), custom_call_target="tpu_custom_call" | custom-call | flops 4831838208 | bytes 15728640 | tf_op jit(solution)/shard_map/pallas_call | solution.py:433
  328.5 5.5 collective-permute-done.26
  342.0 8.5 %collective-permute-done.30 = bf16[2,64,1536]{2,1,0:T(8,128)(2,1)S(1)} collective-permute-done((bf16[2,64,1536]{2,1,0:T(8,128)(2,1)S(1)}, bf16[2,64,1536]{2,1,0:T(8,128)(2,1)S(1)}, u32[]{:S(2)}, u32[]{:S(2)}) %collective-permute-start.30) | collective-permute-done | bytes 393248 | tf_op jit(solution)/shard_map/ppermute | solution.py:29
  350.5 9.3 %collective-permute-done.29 = bf16[2,64,1536]{2,1,0:T(8,128)(2,1)S(1)} collective-permute-done((bf16[2,64,1536]{2,1,0:T(8,128)(2,1)S(1)}, bf16[2,64,1536]{2,1,0:T(8,128)(2,1)S(1)}, u32[]{:S(2)}, u32[]{:S(2)}) %collective-permute-start.29) | collective-permute-done | bytes 393248 | tf_op jit(solution)/shard_map/ppermute | solution.py:29
  379.6 6.8 %shard_map.351 = (f32[4,2,64,384]{3,2,1,0:T(8,128)S(1)}, f32[384,512]{1,0:T(8,128)S(1)}, f32[384,512]{1,0:T(8,128)S(1)}) custom-call(bf16[4,2,64,384]{3,2,1,0:T(8,128)(2,1)S(1)} %bitcast.256, bf16[384,512]{1,0:T(8,128)(2,1)S(1)} %copy-done.19, bf16[384,512]{1,0:T(8,128)(2,1)S(1)} %bitcast.251, f32[512,1]{1,0:T(8,128)S(1)} %bitcast.253, ...), custom_call_target="tpu_custom_call" | custom-call | flops 503316480 | bytes 4194304 | tf_op jit(solution)/shard_map/pallas_call | solution.py:449
  391.6 20.9 %shard_map.352 = bf16[8,704,128]{2,1,0:T(8,128)(2,1)S(1)} custom-call(bf16[8,704,128]{2,1,0:T(8,128)(2,1)S(1)} %copy-done.23, bf16[8,704,128]{2,1,0:T(8,128)(2,1)S(1)} %copy-done.23, bf16[8,192,128]{2,1,0:T(8,128)(2,1)} %all-to-all-done.5.do_ref, f32[12,64,256]{2,1,0:T(8,128)S(1)} %copy-done.43, f32[12,1,256]{2,1,0:T(1,128)S(1)} %get-tuple-element.112.lse_ref), custom_call_target="tpu_custom_call" | custom-call | flops 8053063680 | bytes 5517312 | tf_op jit(solution)/shard_map/pallas_call | solution.py:433
  413.7 7.6 %all-to-all-start.6 = ((bf16[8,704,128]{2,1,0:T(8,128)(2,1)}), bf16[8,704,128]{2,1,0:T(8,128)(2,1)}, u32[]{:S(2)}, u32[]{:S(2)}) async-start(bf16[8,704,128]{2,1,0:T(8,128)(2,1)} %copy-done.24), calls=%async_computation.6 | async-start | bytes 2883584 | tf_op jit(solution)/shard_map/all_to_all | solution.py:810
  430.4 43.4 %all-to-all-done.6.d_ref = bf16[8,704,128]{2,1,0:T(8,128)(2,1)} async-done(((bf16[8,704,128]{2,1,0:T(8,128)(2,1)}), bf16[8,704,128]{2,1,0:T(8,128)(2,1)}, u32[]{:S(2)}, u32[]{:S(2)}) %all-to-all-start.6) | async-done | bytes 1441824 | tf_op jit(solution)/shard_map/all_to_all | solution.py:810
  488.9 9.3 %collective-permute-start.42 = (bf16[512,384]{0,1:T(8,128)(2,1)}, bf16[512,384]{0,1:T(8,128)(2,1)}, u32[]{:S(2)}, u32[]{:S(2)}) collective-permute-start(bf16[512,384]{0,1:T(8,128)(2,1)} %bitcast.317), channel_id=1, source_target_pairs={{0,0},{1,2},{2,8},{3,10},{4,16},{5,18},{6,24},{7,26},{8,1},{9,3},{... | collective-permute-start | bytes 1179656 | tf_op jit(solution)/shard_map/ppermute | solution.py:68
  514.8 8.4 %collective-permute-done.39 = bf16[2,64,1536]{2,1,0:T(8,128)(2,1)} collective-permute-done((bf16[2,64,1536]{2,1,0:T(8,128)(2,1)}, bf16[2,64,1536]{2,1,0:T(8,128)(2,1)}, u32[]{:S(2)}, u32[]{:S(2)}) %collective-permute-start.39) | collective-permute-done | bytes 393248 | tf_op jit(solution)/shard_map/ppermute | solution.py:29
  523.2 8.0 %collective-permute-done.40 = bf16[2,64,1536]{2,1,0:T(8,128)(2,1)} collective-permute-done((bf16[2,64,1536]{2,1,0:T(8,128)(2,1)}, bf16[2,64,1536]{2,1,0:T(8,128)(2,1)}, u32[]{:S(2)}, u32[]{:S(2)}) %collective-permute-start.40) | collective-permute-done | bytes 393248 | tf_op jit(solution)/shard_map/ppermute | solution.py:29
  538.5 7.4 %collective-permute-start.44 = (bf16[3072,128]{1,0:T(8,128)(2,1)}, bf16[3072,128]{1,0:T(8,128)(2,1)}, u32[]{:S(2)}, u32[]{:S(2)}) collective-permute-start(bf16[3072,128]{1,0:T(8,128)(2,1)} %slice.283), channel_id=1, source_target_pairs={{0,0},{1,8},{2,2},{3,10},{4,4},{5,12},{6,6},{7,14},{8,1},{9,9},{10... | collective-permute-start | bytes 2359304 | tf_op jit(solution)/shard_map/ppermute | solution.py:68
  553.1 8.9 %all-to-all-start.7 = ((f32[32,7,128]{2,1,0:T(8,128)}), f32[32,7,128]{2,1,0:T(8,128)}, u32[]{:S(2)}, u32[]{:S(2)}) async-start(f32[32,7,128]{2,1,0:T(8,128)} %reshape.727), calls=%async_computation.9 | async-start | bytes 262144 | tf_op jit(solution)/shard_map/all_to_all | solution.py:805
  576.9 7.3 %reduce-scatter.8.cloned.1.call-done = bf16[192,1152]{1,0:T(8,128)(2,1)} async-done(((bf16[1536,1152]{1,0:T(8,128)(2,1)}), bf16[192,1152]{1,0:T(8,128)(2,1)}) %reduce-scatter.8.cloned.1.call-update) | async-done | bytes 442384 | tf_op jit(solution)/shard_map/reduce_scatter | solution.py:87
  584.2 10.6 %collective-permute-start.43 = (bf16[192,1152]{1,0:T(8,128)(2,1)}, bf16[192,1152]{1,0:T(8,128)(2,1)S(1)}, u32[]{:S(2)}, u32[]{:S(2)}) collective-permute-start(bf16[192,1152]{1,0:T(8,128)(2,1)} %reduce-scatter.8.cloned.1.call-done), channel_id=1, source_target_pairs={{0,0},{1,8},{2,2},{3,10},{4,4},{5,12},{6,6},{7,14},{8,1},{9,9},{10... | collective-permute-start | bytes 1327112 | tf_op jit(solution)/shard_map/ppermute | solution.py:68
  (563 shorter events, 259.4 us)
Async XLA Ops:
  7.2 58.0 %all-gather.5.cloned.1.call-start = ((), (), s32[]{:S(2)}) async-start(), calls=%async_computation.11 | async-start | bytes 3981312 | tf_op jit(solution)/shard_map/all_gather | solution.py:82
  20.2 32.3 %collective-permute-start.2 = (bf16[2,64,1536]{2,1,0:T(8,128)(2,1)S(1)}, bf16[2,64,1536]{2,1,0:T(8,128)(2,1)S(1)}, u32[]{:S(2)}, u32[]{:S(2)}) collective-permute-start(bf16[2,64,1536]{2,1,0:T(8,128)(2,1)S(1)} %bitcast.258), channel_id=1, source_target_pairs={{0,17},{1,16},{16,1},{17,0},{2,19},{3,18},{18,3},{19,2},{4,21},{5,... | collective-permute-start | bytes 1179656 | tf_op jit(solution)/shard_map/ppermute | solution.py:29
  21.1 31.3 %collective-permute-start.1 = (bf16[2,64,1536]{2,1,0:T(8,128)(2,1)S(1)}, bf16[2,64,1536]{2,1,0:T(8,128)(2,1)}, u32[]{:S(2)}, u32[]{:S(2)}) collective-permute-start(bf16[2,64,1536]{2,1,0:T(8,128)(2,1)S(1)} %bitcast.259), channel_id=1, source_target_pairs={{0,16},{1,17},{16,0},{17,1},{2,18},{3,19},{18,2},{19,3},{4,20},{5,... | collective-permute-start | bytes 1179656 | tf_op jit(solution)/shard_map/ppermute | solution.py:29
  21.7 30.8 %collective-permute-start = (bf16[2,64,1536]{2,1,0:T(8,128)(2,1)S(1)}, bf16[2,64,1536]{2,1,0:T(8,128)(2,1)}, u32[]{:S(2)}, u32[]{:S(2)}) collective-permute-start(bf16[2,64,1536]{2,1,0:T(8,128)(2,1)S(1)} %bitcast.260), channel_id=1, source_target_pairs={{0,1},{1,0},{16,17},{17,16},{2,3},{3,2},{18,19},{19,18},{4,5},{5,4... | collective-permute-start | bytes 1179656 | tf_op jit(solution)/shard_map/ppermute | solution.py:29
  47.3 35.7 %all-to-all-start.3 = ((bf16[4,48,2048]{2,1,0:T(8,128)(2,1)}), bf16[4,48,2048]{2,1,0:T(8,128)(2,1)S(1)}, u32[]{:S(2)}, u32[]{:S(2)}) async-start(bf16[4,48,2048]{2,1,0:T(8,128)(2,1)} %copy.138), calls=%async_computation.3 | async-start | bytes 1572864 | tf_op jit(solution)/shard_map/all_to_all | solution.py:556
  51.7 57.2 %all-gather.7.cloned.1.call-start = ((), (), s32[]{:S(2)}) async-start(), calls=%async_computation.12 | async-start | bytes 2654208 | tf_op jit(solution)/shard_map/all_gather | solution.py:82
  83.9 42.6 %all-to-all-start.2 = ((bf16[8,704,128]{2,1,0:T(8,128)(2,1)}), bf16[8,704,128]{2,1,0:T(8,128)(2,1)S(1)}, u32[]{:S(2)}, u32[]{:S(2)}) async-start(bf16[8,704,128]{2,1,0:T(8,128)(2,1)} %copy-done.25), calls=%async_computation.2 | async-start | bytes 2883584 | tf_op jit(solution)/shard_map/all_to_all | solution.py:636
  89.0 122.5 %all-gather.9.cloned.1.call-start = ((), (), s32[]{:S(2)}) async-start(), calls=%async_computation.13 | async-start | bytes 7077888 | tf_op jit(solution)/shard_map/all_gather | solution.py:82
  149.5 19.3 %collective-permute-start.11 = (f32[1,512]{1,0:T(1,128)S(1)}, f32[1,512]{1,0:T(1,128)S(1)}, u32[]{:S(2)}, u32[]{:S(2)}) collective-permute-start(f32[1,512]{1,0:T(1,128)S(1)} %bitcast.347), channel_id=1, source_target_pairs={{0,16},{1,17},{16,0},{17,1},{2,18},{3,19},{18,2},{19,3},{4,20},{5,... | collective-permute-start | bytes 6152 | tf_op jit(solution)/shard_map/ppermute | solution.py:29
  152.2 34.5 %all-to-all-start.4 = ((bf16[8,192,128]{2,1,0:T(8,128)(2,1)}), bf16[8,192,128]{2,1,0:T(8,128)(2,1)S(1)}, u32[]{:S(2)}, u32[]{:S(2)}) async-start(bf16[8,192,128]{2,1,0:T(8,128)(2,1)} %copy-done.33), calls=%async_computation.4 | async-start | bytes 786432 | tf_op jit(solution)/shard_map/all_to_all | solution.py:654
  164.7 83.0 %all-gather.11.cloned.1.call-start = ((), (), s32[]{:S(2)}) async-start(), calls=%async_computation.14 | async-start | bytes 3538944 | tf_op jit(solution)/shard_map/all_gather | solution.py:82
  192.3 19.2 %collective-permute-start.14 = (bf16[2,64,1536]{2,1,0:T(8,128)(2,1)S(1)}, bf16[2,64,1536]{2,1,0:T(8,128)(2,1)S(1)}, u32[]{:S(2)}, u32[]{:S(2)}) collective-permute-start(bf16[2,64,1536]{2,1,0:T(8,128)(2,1)S(1)} %bitcast.307), channel_id=1, source_target_pairs={{0,16},{1,17},{16,0},{17,1},{2,18},{3,19},{18,2},{19,3},{4,20},{5,... | collective-permute-start | bytes 1179656 | tf_op jit(solution)/shard_map/ppermute | solution.py:29
  211.5 262.3 %reduce-scatter.4.cloned.1.call-start = ((), (), s32[]{:S(2)}) async-start(), calls=%async_computation.15 | async-start | bytes 10616832 | tf_op jit(solution)/shard_map/reduce_scatter | solution.py:87
  217.9 19.3 %collective-permute-start.17 = (bf16[2,64,1536]{2,1,0:T(8,128)(2,1)S(1)}, bf16[2,64,1536]{2,1,0:T(8,128)(2,1)S(1)}, u32[]{:S(2)}, u32[]{:S(2)}) collective-permute-start(bf16[2,64,1536]{2,1,0:T(8,128)(2,1)S(1)} %multiply_convert_fusion.2), channel_id=1, source_target_pairs={{0,16},{1,17},{16,0},{17,1},{2,18},{3,19},{18,2},{19,3},{4,20},{5,... | collective-permute-start | bytes 1179656 | tf_op jit(solution)/shard_map/ppermute | solution.py:29
  217.9 19.3 %collective-permute-start.18 = (bf16[2,64,1536]{2,1,0:T(8,128)(2,1)S(1)}, bf16[2,64,1536]{2,1,0:T(8,128)(2,1)S(1)}, u32[]{:S(2)}, u32[]{:S(2)}) collective-permute-start(bf16[2,64,1536]{2,1,0:T(8,128)(2,1)S(1)} %multiply_convert_fusion.2), channel_id=1, source_target_pairs={{0,1},{1,0},{16,17},{17,16},{2,3},{3,2},{18,19},{19,18},{4,5},{5,4... | collective-permute-start | bytes 1179656 | tf_op jit(solution)/shard_map/ppermute | solution.py:29
  275.1 19.1 %collective-permute-start.23 = (bf16[2,64,1536]{2,1,0:T(8,128)(2,1)S(1)}, bf16[2,64,1536]{2,1,0:T(8,128)(2,1)S(1)}, u32[]{:S(2)}, u32[]{:S(2)}) collective-permute-start(bf16[2,64,1536]{2,1,0:T(8,128)(2,1)S(1)} %fusion.18), channel_id=1, source_target_pairs={{0,16},{1,17},{16,0},{17,1},{2,18},{3,19},{18,2},{19,3},{4,20},{5,... | collective-permute-start | bytes 1179656 | tf_op jit(solution)/shard_map/ppermute | solution.py:29
  314.8 19.3 %collective-permute-start.26 = (bf16[2,64,1536]{2,1,0:T(8,128)(2,1)S(1)}, bf16[2,64,1536]{2,1,0:T(8,128)(2,1)}, u32[]{:S(2)}, u32[]{:S(2)}) collective-permute-start(bf16[2,64,1536]{2,1,0:T(8,128)(2,1)S(1)} %bitcast.301), channel_id=1, source_target_pairs={{0,16},{1,17},{16,0},{17,1},{2,18},{3,19},{18,2},{19,3},{4,20},{5,... | collective-permute-start | bytes 1179656 | tf_op jit(solution)/shard_map/ppermute | solution.py:29
  340.6 19.3 %collective-permute-start.29 = (bf16[2,64,1536]{2,1,0:T(8,128)(2,1)S(1)}, bf16[2,64,1536]{2,1,0:T(8,128)(2,1)S(1)}, u32[]{:S(2)}, u32[]{:S(2)}) collective-permute-start(bf16[2,64,1536]{2,1,0:T(8,128)(2,1)S(1)} %fusion.19), channel_id=1, source_target_pairs={{0,16},{1,17},{16,0},{17,1},{2,18},{3,19},{18,2},{19,3},{4,20},{5,... | collective-permute-start | bytes 1179656 | tf_op jit(solution)/shard_map/ppermute | solution.py:29
  364.1 25.0 %all-to-all-start.5 = ((bf16[8,192,128]{2,1,0:T(8,128)(2,1)}), bf16[8,192,128]{2,1,0:T(8,128)(2,1)}, u32[]{:S(2)}, u32[]{:S(2)}) async-start(bf16[8,192,128]{2,1,0:T(8,128)(2,1)} %copy-done.34), calls=%async_computation.5 | async-start | bytes 786432 | tf_op jit(solution)/shard_map/all_to_all | solution.py:733
  370.3 43.4 %collective-permute-start.31 = (bf16[2,2,1,32,1536]{4,3,2,1,0:T(8,128)(2,1)}, bf16[2,2,1,32,1536]{4,3,2,1,0:T(8,128)(2,1)}, u32[]{:S(2)}, u32[]{:S(2)}) collective-permute-start(bf16[2,2,1,32,1536]{4,3,2,1,0:T(8,128)(2,1)} %convert_element_type.259), channel_id=1, source_target_pairs={{0,1},{1,2},{2,3},{3,4},{4,5},{5,6},{6,7},{8,9},{9,10},{10,11},{11... | collective-permute-start | bytes 1179656 | tf_op jit(solution)/shard_map/ppermute | solution.py:93
  373.3 40.3 %collective-permute-start.32 = (bf16[2,2,1,32,1536]{4,3,2,1,0:T(8,128)(2,1)}, bf16[2,2,1,32,1536]{4,3,2,1,0:T(8,128)(2,1)}, u32[]{:S(2)}, u32[]{:S(2)}) collective-permute-start(bf16[2,2,1,32,1536]{4,3,2,1,0:T(8,128)(2,1)} %convert_element_type.259), channel_id=1, source_target_pairs={{1,0},{2,1},{3,2},{4,3},{5,4},{6,5},{7,6},{9,8},{10,9},{11,10},{12... | collective-permute-start | bytes 1179656 | tf_op jit(solution)/shard_map/ppermute | solution.py:94
  413.7 60.1 %all-to-all-start.6 = ((bf16[8,704,128]{2,1,0:T(8,128)(2,1)}), bf16[8,704,128]{2,1,0:T(8,128)(2,1)}, u32[]{:S(2)}, u32[]{:S(2)}) async-start(bf16[8,704,128]{2,1,0:T(8,128)(2,1)} %copy-done.24), calls=%async_computation.6 | async-start | bytes 2883584 | tf_op jit(solution)/shard_map/all_to_all | solution.py:810
  421.3 109.9 %reduce-scatter.6.cloned.1.call-start = ((), (), s32[]{:S(2)}) async-start(), calls=%async_computation.16 | async-start | bytes 2359296 | tf_op jit(solution)/shard_map/reduce_scatter | solution.py:87
  473.8 110.4 %reduce-scatter.8.cloned.1.call-start = ((), (), s32[]{:S(2)}) async-start(), calls=%async_computation.17 | async-start | bytes 3981312 | tf_op jit(solution)/shard_map/reduce_scatter | solution.py:87
  488.9 25.9 %collective-permute-start.42 = (bf16[512,384]{0,1:T(8,128)(2,1)}, bf16[512,384]{0,1:T(8,128)(2,1)}, u32[]{:S(2)}, u32[]{:S(2)}) collective-permute-start(bf16[512,384]{0,1:T(8,128)(2,1)} %bitcast.317), channel_id=1, source_target_pairs={{0,0},{1,2},{2,8},{3,10},{4,16},{5,18},{6,24},{7,26},{8,1},{9,3},{... | collective-permute-start | bytes 1179656 | tf_op jit(solution)/shard_map/ppermute | solution.py:68
  508.1 23.1 %collective-permute-start.40 = (bf16[2,64,1536]{2,1,0:T(8,128)(2,1)}, bf16[2,64,1536]{2,1,0:T(8,128)(2,1)}, u32[]{:S(2)}, u32[]{:S(2)}) collective-permute-start(bf16[2,64,1536]{2,1,0:T(8,128)(2,1)} %bitcast.83), channel_id=1, source_target_pairs={{0,16},{1,17},{16,0},{17,1},{2,18},{3,19},{18,2},{19,3},{4,20},{5,... | collective-permute-start | bytes 1179656 | tf_op jit(solution)/shard_map/ppermute | solution.py:29
  508.1 23.1 %collective-permute-start.41 = (bf16[2,64,1536]{2,1,0:T(8,128)(2,1)}, bf16[2,64,1536]{2,1,0:T(8,128)(2,1)}, u32[]{:S(2)}, u32[]{:S(2)}) collective-permute-start(bf16[2,64,1536]{2,1,0:T(8,128)(2,1)} %bitcast.84), channel_id=1, source_target_pairs={{0,1},{1,0},{16,17},{17,16},{2,3},{3,2},{18,19},{19,18},{4,5},{5,4... | collective-permute-start | bytes 1179656 | tf_op jit(solution)/shard_map/ppermute | solution.py:29
  538.5 63.9 %collective-permute-start.44 = (bf16[3072,128]{1,0:T(8,128)(2,1)}, bf16[3072,128]{1,0:T(8,128)(2,1)}, u32[]{:S(2)}, u32[]{:S(2)}) collective-permute-start(bf16[3072,128]{1,0:T(8,128)(2,1)} %slice.283), channel_id=1, source_target_pairs={{0,0},{1,8},{2,2},{3,10},{4,4},{5,12},{6,6},{7,14},{8,1},{9,9},{10... | collective-permute-start | bytes 2359304 | tf_op jit(solution)/shard_map/ppermute | solution.py:68
  553.1 46.1 %all-to-all-start.7 = ((f32[32,7,128]{2,1,0:T(8,128)}), f32[32,7,128]{2,1,0:T(8,128)}, u32[]{:S(2)}, u32[]{:S(2)}) async-start(f32[32,7,128]{2,1,0:T(8,128)} %reshape.727), calls=%async_computation.9 | async-start | bytes 262144 | tf_op jit(solution)/shard_map/all_to_all | solution.py:805
  562.8 39.6 %collective-permute-start.45 = (bf16[192,384]{1,0:T(8,128)(2,1)}, bf16[192,384]{1,0:T(8,128)(2,1)S(1)}, u32[]{:S(2)}, u32[]{:S(2)}) collective-permute-start(bf16[192,384]{1,0:T(8,128)(2,1)} %bitcast.222), channel_id=1, source_target_pairs={{0,0},{1,2},{2,8},{3,10},{4,16},{5,18},{6,24},{7,26},{8,1},{9,3},{... | collective-permute-start | bytes 442376 | tf_op jit(solution)/shard_map/ppermute | solution.py:68
  570.6 31.8 %collective-permute-start.46 = (bf16[96,512]{1,0:T(8,128)(2,1)S(1)}, bf16[96,512]{1,0:T(8,128)(2,1)}, u32[]{:S(2)}, u32[]{:S(2)}) collective-permute-start(bf16[96,512]{1,0:T(8,128)(2,1)S(1)} %pad_maximum_fusion.7), channel_id=1, source_target_pairs={{0,0},{1,8},{2,2},{3,10},{4,4},{5,12},{6,6},{7,14},{8,1},{9,9},{10... | collective-permute-start | bytes 294920 | tf_op jit(solution)/shard_map/ppermute | solution.py:68
  574.0 28.4 %collective-permute-start.47 = (f32[1,48]{1,0:T(1,128)S(1)}, f32[1,48]{1,0:T(1,128)S(1)}, u32[]{:S(2)}, u32[]{:S(2)}) collective-permute-start(f32[1,48]{1,0:T(1,128)S(1)} %bitcast.362), channel_id=1, source_target_pairs={{0,0},{1,8},{2,2},{3,10},{4,4},{5,12},{6,6},{7,14},{8,1},{9,9},{10... | collective-permute-start | bytes 584 | tf_op jit(solution)/shard_map/ppermute | solution.py:68
  (152 other events, 1276.6 us)
Sparse Core Ops, SparseCore 0:
  20.3 44.8 all-gather.4
  66.8 33.3 all-gather.6
  126.7 79.9 all-gather.8
  211.6 36.0 all-gather.10
  334.2 129.1 reduce-scatter.3
  474.0 50.7 reduce-scatter.5
  531.3 52.8 reduce-scatter.7

commit v5 on v4

--- a/solution.py
+++ b/solution.py
@@ -64,17 +64,32 @@
         to = 0
         for size, at in zip(sizes, target(*where)):
             to = to * size + at
-        pairs.append((index, to))
-    return lax.ppermute(block, ALL, pairs)
+        if to != index:
+            pairs.append((index, to))
+    here = [lax.axis_index(axis) for axis in ALL]
+    stays = functools.reduce(lambda a, b: a & b, [a == b for a, b in zip(here, target(*here))])
+    return stays, block, lax.ppermute(block, ALL, pairs)
+
+
+def settled(moved):
+    stays, block, received = moved
+    return jnp.where(stays, block, received)
 
 
 def exchange(block):
     return relocate(block, lambda y, core, far, z, x: (y, x, far, z, core))
 
 
+def piece_member(f, part, parts):
+    if parts > 2:
+        return f * parts + part
+    core = f // 2
+    return (f % 2 * 2 + (part ^ core)) * 2 + core
+
+
 def to_owner(block):
     if lax.axis_size("far") == 1:
-        return relocate(block, lambda y, core, far, z, x: (z // 2, z % 2, 0, 2 * y + x, core))
+        return relocate(block, lambda y, core, far, z, x: (core, z // 2, 0, 2 * y + x, z % 2 ^ core))
     return relocate(block, lambda y, core, far, z, x: (far // 2, far % 2, 2 * y + x, z, core))
 
 
@@ -250,16 +265,13 @@
     left = turned(hidden_ref[...])
     tile = left.shape[0] // part
 
-    def down(c, carry):
-        block = dot_nn(left, dz_ref[:, pl.ds(pl.multiple_of(384 * c, 128), 384)]).astype(BF16)
+    for c in range(4):
+        block = dot_nn(left, dz_ref[:, 384 * c : 384 * c + 384]).astype(BF16)
         for j in range(3):
             for h in range(part):
-                out_ref[c * part + h, tile * j : tile * j + tile, :] = block[
+                out_ref[piece_member(c, h, part), tile * j : tile * j + tile, :] = block[
                     tile * h : tile * h + tile, 128 * j : 128 * j + 128
                 ]
-        return carry
-
-    lax.fori_loop(0, 4, down, 0)
     base = 3 * tile
     left_f = turned(f_in_ref[...])
     tile_f = left_f.shape[0] // n_rows
@@ -299,7 +311,7 @@
     for f in range(4):
         block = dot_nn(left, dy_ref[:, 384 * f : 384 * f + 384]).astype(BF16)
         for part in range(n_rows // 4):
-            member = f * (n_rows // 4) + part
+            member = piece_member(f, part, n_rows // 4)
             for j in range(3):
                 out_ref[member, base + tile * j : base + tile * j + tile, :] = block[
                     tile * part : tile * part + tile, 128 * j : 128 * j + 128
@@ -459,31 +471,44 @@
     )(*args)
 
 
-def product_kernel(left_ref, right_ref, out_ref):
-    term = dot_nt(left_ref[...], right_ref[...])
-
-    @pl.when(pl.program_id(0) == 0)
-    def _():
-        out_ref[...] = term
-
-    @pl.when(pl.program_id(0) > 0)
-    def _():
-        out_ref[...] += term
-
-
-def product(left, right):
-    (rows, deep), (columns, _) = left.shape, right.shape
-    return pl.pallas_call(
-        product_kernel,
-        grid=(deep // 512,),
-        out_shape=shaped((rows, columns)),
-        in_specs=[pl.BlockSpec((rows, 512), lambda k: (0, k)), pl.BlockSpec((columns, 512), lambda k: (0, k))],
-        out_specs=pl.BlockSpec((rows, columns), lambda k: (0, 0)),
-        compiler_params=pltpu.CompilerParams(vmem_limit_bytes=20 << 20),
-        cost_estimate=pl.CostEstimate(
-            flops=2 * rows * columns * deep, bytes_accessed=2 * deep * (rows + columns), transcendentals=0
-        ),
-    )(left, right)
+def feed_kernel(f_in_ref, w_gu_ref, w_dn_ref, gu_ref, hidden_ref, z_ref):
+    half_w = hidden_ref.shape[1]
+    z_ref[...] = jnp.zeros_like(z_ref)
+
+    def step(j, carry):
+        at = pl.multiple_of(256 * j, 256)
+        up_at = pl.multiple_of(half_w + 256 * j, 256)
+        gate = dot_nn(f_in_ref[...], w_gu_ref[:, pl.ds(at, 256)])
+        up = dot_nn(f_in_ref[...], w_gu_ref[:, pl.ds(up_at, 256)])
+        gu_ref[:, pl.ds(at, 256)] = gate
+        gu_ref[:, pl.ds(up_at, 256)] = up
+        hidden = (gate * jax.nn.sigmoid(gate) * up).astype(BF16)
+        hidden_ref[:, pl.ds(at, 256)] = hidden
+        z_ref[...] += dot_nn(hidden, w_dn_ref[pl.ds(at, 256), :])
+        return carry
+
+    lax.fori_loop(0, half_w // 256, step, 0)
+
+
+def feed_back_kernel(dz_ref, w_dn_ref, gu_ref, w_gu_ref, dgu_ref, df_ref):
+    half_w = w_dn_ref.shape[0]
+    df_ref[...] = jnp.zeros_like(df_ref)
+
+    def step(j, carry):
+        at = pl.multiple_of(256 * j, 256)
+        up_at = pl.multiple_of(half_w + 256 * j, 256)
+        d_hidden = dot_nt(dz_ref[...], w_dn_ref[pl.ds(at, 256), :])
+        gate, up = gu_ref[:, pl.ds(at, 256)], gu_ref[:, pl.ds(up_at, 256)]
+        sigma = jax.nn.sigmoid(gate)
+        d_gate = (d_hidden * up * (sigma * (1.0 + gate * (1.0 - sigma)))).astype(BF16)
+        d_up = (d_hidden * (gate * sigma)).astype(BF16)
+        dgu_ref[:, pl.ds(at, 256)] = d_gate
+        dgu_ref[:, pl.ds(up_at, 256)] = d_up
+        df_ref[...] += dot_nt(d_gate, w_gu_ref[:, pl.ds(at, 256)])
+        df_ref[...] += dot_nt(d_up, w_gu_ref[:, pl.ds(up_at, 256)])
+        return carry
+
+    lax.fori_loop(0, half_w // 256, step, 0)
 
 
 def shaped(shape, dtype=F32):
@@ -585,8 +610,8 @@
     tokens_c = clips * caps
     blank = jnp.zeros((rows, width - 2 * tokens_c), BF16)
     cap_rows = jnp.concatenate([cap_columns(w_cap_key), cap_columns(w_cap_value), blank], axis=1)
-    side = group_gather(exchange(jnp.concatenate([w_out, cap_rows])))
-    down_rows = exchange(w_down)
+    side = group_gather(settled(exchange(jnp.concatenate([w_out, cap_rows]))))
+    down_rows = settled(exchange(w_down))
     mod_full = note[:, : clips * mod_cols].reshape(n_all, clips, mod_cols)
     mod_full = mod_full.transpose(1, 0, 2).reshape(clips, 4, width)
     scale_a, gate_a, scale_f, gate_f = (mod_full[:, i] for i in range(4))
@@ -632,8 +657,20 @@
         cosine,
         sine,
     )
-    got, (side, cut_gu, down_rows, (above_g, below_g)) = beside(
-        lax.all_to_all(send, PLANE, 0, 0), (side, cut_gu, down_rows, row_neighbours(grad_out))
+    side = side.reshape(n_rows, -1, width)
+    w_o = side[:, :rows].reshape(-1, width)
+    k_pre_t = side[:, rows:, :tokens_c].reshape(-1, tokens_c)
+    v_cap_t = side[:, rows:, tokens_c : 2 * tokens_c].reshape(-1, tokens_c)
+
+    usable = (jnp.arange(caps)[None, :] < cap_len[:, None]) & (cap_mask > 0)
+    bias = usable.astype(F32).reshape(clips * caps, 1)
+    k_pre_t = k_pre_t.astype(F32)
+    gain_cap = own_gains[2][:, None]
+    r_cap = lax.rsqrt(team_sum(jnp.sum(k_pre_t * k_pre_t, axis=0, keepdims=True)) / width + EPS)
+    k_cap_t = (k_pre_t * r_cap * gain_cap).astype(BF16)
+    got, (k_pre_t, r_cap, k_cap_t, v_cap_t, w_o, cut_gu, down_rows, (above_g, below_g)) = beside(
+        lax.all_to_all(send, PLANE, 0, 0),
+        (k_pre_t, r_cap, k_cap_t, v_cap_t, w_o, cut_gu, down_rows, row_neighbours(grad_out)),
     )
     w_gu = group_gather(cut_gu)
     kv_all = got
@@ -650,19 +687,8 @@
         flops=2 * work,
         grant=24 if n_far == 1 else 56,
     )
-    o_pack, side = beside(o_pack, side)
     o_back = lax.all_to_all(o_pack, PLANE, 0, 0)
-    side = side.reshape(n_rows, -1, width)
-    w_o = side[:, :rows].reshape(-1, width)
-    k_pre_t = side[:, rows:, :tokens_c].reshape(-1, tokens_c)
-    v_cap_t = side[:, rows:, tokens_c : 2 * tokens_c].reshape(-1, tokens_c)
-
-    usable = (jnp.arange(caps)[None, :] < cap_len[:, None]) & (cap_mask > 0)
-    bias = usable.astype(F32).reshape(clips * caps, 1)
-    k_pre_t = k_pre_t.astype(F32)
-    gain_cap = own_gains[2][:, None]
-    r_cap = lax.rsqrt(team_sum(jnp.sum(k_pre_t * k_pre_t, axis=0, keepdims=True)) / width + EPS)
-    k_cap_t = (k_pre_t * r_cap * gain_cap).astype(BF16)
+
     q_cap4 = q_cap.reshape(group, clips, local, heads_w)
     (out_cross,) = cross_call(
         cross_kernel, [shaped(q_cap4.shape)], ("toob", "t"), q_cap4, k_cap_t, v_cap_t, bias
@@ -683,14 +709,16 @@
     (h_mid, f_in32), mid_back = jax.vjp(mid_piece, x_flat, y_one, gains[1], gate_a, gains[2], scale_f)
     f_in, w_gu = team_gather(f_in32.astype(BF16), in_order(w_gu))
     f_in = f_in.reshape(count, width)
-    gate_up = mm(f_in, w_gu)
-
-    def act_piece(gate_in, up_in):
-        return jax.nn.silu(gate_in) * up_in
-
-    hidden32, act_back = jax.vjp(act_piece, gate_up[:, :ff_w], gate_up[:, ff_w:])
-    hidden = hidden32.astype(BF16)
-    z_out, _ = team_scatter(mm(hidden, w_dn).reshape(group, clips, local, width))
+    gate_up, hidden, z_terms = call(
+        feed_kernel,
+        [shaped((count, 2 * ff_w)), shaped((count, ff_w), BF16), shaped((count, width))],
+        f_in,
+        w_gu,
+        w_dn,
+        flops=6 * count * width * ff_w,
+        grant=32,
+    )
+    z_out, _ = team_scatter(z_terms.reshape(group, clips, local, width))
 
     def end_piece(h_in_mid, z_in, gain_four, gate_in):
         return h_in_mid + jnp.tanh(gate_in)[:, None, :] * rms_norm(z_in, gain_four)
@@ -703,9 +731,17 @@
     d_h_end, d_z, d_g_four, d_gate_f = end_back(d_y.reshape(clips, local, width))
     d_z_all, _ = team_gather(d_z.astype(BF16))
     d_z_all = d_z_all.reshape(count, width)
-    d_hidden = lax.dot_general(d_z_all, w_dn, (((1,), (1,)), ((), ())), preferred_element_type=F32)
-    d_gu = jnp.concatenate([d.astype(BF16) for d in act_back(d_hidden)], axis=1)
-    d_f_in = product(d_gu, w_gu)
+    d_gu, d_f_in = call(
+        feed_back_kernel,
+        [shaped((count, 2 * ff_w), BF16), shaped((count, width))],
+        d_z_all,
+        w_dn,
+        gate_up,
+        w_gu,
+        flops=6 * count * width * ff_w,
+        grant=32,
+    )
+
     def term(left, right):
         return lax.dot_general(left, right, (((0,), (0,)), ((), ())), preferred_element_type=F32).astype(BF16)
 
@@ -732,17 +768,6 @@
     )
     d_got = lax.all_to_all(d_pack, PLANE, 0, 0)
     d_mix_gate = jnp.sum(d_attn * out_cross, axis=0) * (1.0 - own_gate[0] * own_gate[0])
-    d_q_cross, d_k_cap, d_v_cap = cross_call(
-        cross_back_kernel,
-        [shaped(q_cap4.shape), shaped((heads_w, clips * caps)), shaped((heads_w, clips * caps))],
-        ("toobt", "too"),
-        q_cap4,
-        k_cap_t,
-        v_cap_t,
-        bias,
-        d_cross.reshape(q_cap4.shape),
-    )
-    d_got, (d_q_cross, d_k_cap, d_v_cap) = beside(d_got, (d_q_cross, d_k_cap, d_v_cap))
     back_scratch = [pltpu.VMEM((2, keys, 128), F32), pltpu.VMEM((2, 128, keys), BF16)]
     if n_far == 1:
         (d_send,) = call(
@@ -772,7 +797,17 @@
         )
         d_kv = lax.psum_scatter(d_kv, "far", scatter_dimension=0, tiled=True)
         d_send = jnp.concatenate([d_kv, d_q], axis=1)
-    d_send, (above, below) = beside(d_send, (above, below))
+    d_send, (above, below, d_cross) = beside(d_send, (above, below, d_cross))
+    d_q_cross, d_k_cap, d_v_cap = cross_call(
+        cross_back_kernel,
+        [shaped(q_cap4.shape), shaped((heads_w, clips * caps)), shaped((heads_w, clips * caps))],
+        ("toobt", "too"),
+        q_cap4,
+        k_cap_t,
+        v_cap_t,
+        bias,
+        d_cross.reshape(q_cap4.shape),
+    )
     above, below = above.astype(F32), below.astype(F32)
     output = (y_grid + mix_coefs[1] * above + mix_coefs[2] * below).astype(BF16)
     d_above = jnp.sum(g_center * above, axis=(0, 1, 2, 3))
@@ -806,8 +841,8 @@
         cut = clips * mod_cols
         return both[:cut].reshape(clips, mod_cols), both[cut : cut + len(rows_in) * share].reshape(-1, share)
 
-    d_recv, (output, out_terms, ff_sum) = beside(
-        lax.all_to_all(d_send, PLANE, 0, 0), (output, out_terms, ff_sum)
+    d_recv, (output, out_terms, ff_sum, d_q_cross) = beside(
+        lax.all_to_all(d_send, PLANE, 0, 0), (output, out_terms, ff_sum, d_q_cross)
     )
     out_sum = group_scatter(out_terms)
     d_qn, d_kn, d_v = call(
@@ -827,13 +862,13 @@
     d_k_low = (rk * a_k - k_zero * (rk * rk * rk * dots[:, 1:2])).astype(BF16)
     d_qkv = jnp.concatenate([d_q_low, d_k_low, d_v], axis=1)
     d_h_in = lax.dot_general(d_qkv, w_qkv, (((1,), (1,)), ((), ())), preferred_element_type=F32)
-    sum_down = to_owner(from_chunks(ff_sum[None, : ff_rows[0]], w_down.shape[0] * group))
-    d_h_in, (term_qkv, out_sum, sum_down) = team_scatter(
-        d_h_in.reshape(group, clips, local, width), (term(h_in, d_qkv), out_sum, sum_down)
+    d_h_in, (term_qkv, out_sum) = team_scatter(
+        d_h_in.reshape(group, clips, local, width), (term(h_in, d_qkv), out_sum)
     )
     qkv_sum = group_scatter(term_qkv)
     d_x_pre, d_g_zero, d_scale_a = pre_back(d_h_in)
     grad_tokens = (d_x_pre + d_x_mid).reshape(tokens.shape)
+    d_g_zero, (ff_sum, out_sum) = beside(d_g_zero, (ff_sum, out_sum))
 
     d_mod, sums = owners_sum(
         jnp.concatenate([d_scale_a, d_gate_a, d_scale_f, d_gate_f], axis=1),
@@ -849,23 +884,22 @@
             d_below,
         ],
     )
-    d_w_mod = lax.dot_general(
-        step_embed, d_mod.astype(BF16), (((0,), (0,)), ((), ())), preferred_element_type=F32
-    )
     cap_sum = from_chunks(out_sum[None, :cut].astype(F32), 2 * wide + 16)
     d_k_own, d_v_own, cap_dot = cap_sum[:wide], cap_sum[wide : 2 * wide], cap_sum[2 * wide : 2 * wide + 1]
     k_own = lax.dynamic_slice(k_pre_t, (my_member * wide, 0), (wide, clips * caps))
     g_own = lax.dynamic_slice(gain_cap, (my_member * wide, 0), (wide, 1))
-    d_g_cap = exchange(jnp.sum(d_k_own * k_own * r_cap, axis=1)[None])
+    caps_gain = exchange(jnp.sum(d_k_own * k_own * r_cap, axis=1)[None])
     d_k_zero_cap = r_cap * g_own * d_k_own - k_own * (r_cap * r_cap * r_cap * cap_dot / width)
-    d_caps = exchange(jnp.concatenate([d_k_zero_cap, d_v_own]).astype(BF16))
-    sum_gu = exchange(ff_sum[ff_rows[0] :])
-    sum_out = to_owner(from_chunks(out_sum[None, cut:], tile))
-    d_w_mod, qkv_sum = beside(d_w_mod, exchange(qkv_sum))
-    qkv_sum, sum_gu, sum_out, d_caps, d_g_cap = lax.optimization_barrier(
-        (qkv_sum, sum_gu, sum_out, d_caps, d_g_cap)
-    )
-    qkv_sum = qkv_sum.astype(F32)
+    moved = [
+        caps_gain,
+        exchange(jnp.concatenate([d_k_zero_cap, d_v_own]).astype(BF16)),
+        exchange(ff_sum[ff_rows[0] :]),
+    ]
+    d_mod, received = beside(d_mod, [m[2] for m in moved])
+    d_g_cap, d_caps, sum_gu = (settled((*m[:2], r)) for m, r in zip(moved, received))
+    d_w_mod = lax.dot_general(
+        step_embed, d_mod.astype(BF16), (((0,), (0,)), ((), ())), preferred_element_type=F32
+    )
     sum_gate, sum_up = jnp.split(sum_gu, 2)
 
     def result(block):
@@ -877,23 +911,35 @@
     d_w_cap_key = cap_weight(d_caps[:wide])
     d_w_cap_value = cap_weight(d_caps[wide:])
     d_gains = jnp.concatenate([sums[:6], d_g_cap], axis=0)
-    d_mixes = sums[6:]
-
+    mine = w_down.shape[0] * group
+    owned = jnp.concatenate(
+        [from_chunks(ff_sum[None, : ff_rows[0]], mine), from_chunks(out_sum[None, cut:], tile)]
+    )
+    ready = (
+        result(sum_gate),
+        result(sum_up),
+        d_w_cap_key,
+        d_w_cap_value,
+        d_w_mod,
+        d_gains,
+        sums[6:],
+    )
+    owned, qkv_sum = beside(owned, qkv_sum)
+    moved = to_owner(owned), exchange(qkv_sum)
+    received, ready = beside([m[2] for m in moved], ready)
+    owned, qkv_sum = (settled((*m[:2], r)).astype(F32) for m, r in zip(moved, received))
+    gate_grad, up_grad, *ready = ready
     return (
         output,
         grad_tokens,
         qkv_sum[:, :heads_w],
         qkv_sum[:, heads_w : 2 * heads_w],
         qkv_sum[:, 2 * heads_w :],
-        sum_out.astype(F32),
-        result(sum_gate),
-        result(sum_up),
-        sum_down.astype(F32),
-        d_w_cap_key,
-        d_w_cap_value,
-        d_w_mod,
-        d_gains,
-        d_mixes,
+        owned[mine:],
+        gate_grad,
+        up_grad,
+        owned[:mine],
+        *ready,
     )
 
 

time: 632 us -> 627 us (level)
  the two profiles are of different devices: /device:TPU:5 before, /device:TPU:2 now
where the time goes in v5:
time: 627 us; the launch traced here: 616 us
  waiting for transfers between devices  220 us (35%)
  starting transfers between devices  118 us (19%)
  local copies, waits for them, and re-layouts  96.9 us (15%)
  Pallas kernels  85.4 us (14%)
  other arithmetic  48 us (8%)
  matrix products  20.3 us (3%)
  between operations  17.1 us (3%)
  blocking collectives  10.8 us (2%)
    ppermute x36, waiting for transfers between devices, swap(): return lax.ppermute(value, TEAM, [(i, i ^ bits) for i in range(4)])  102 us
    pallas_call x10, Pallas kernels, call(): pl.pallas_call(kernel, out_shape=outs, in_specs=[spec] * len(args), out_s...  74.5 us
    ppermute x36, starting transfers between devices, swap(): return lax.ppermute(value, TEAM, [(i, i ^ bits) for i in range(4)])  44.7 us
    unnamed x265, local copies, waits for them, and re-layouts  43.2 us
    all_to_all x1, waiting for transfers between devices, body(): lax.all_to_all(d_send, PLANE, 0, 0)  29.9 us
    ppermute x7, waiting for transfers between devices, relocate(): return (stays, block, lax.ppermute(block, ALL, pairs))  28.5 us
    ppermute x7, starting transfers between devices, relocate(): return (stays, block, lax.ppermute(block, ALL, pairs))  19.7 us
    all_to_all x1, waiting for transfers between devices, body(): o_back = lax.all_to_all(o_pack, PLANE, 0, 0)  15.2 us
  transfers between devices with their start and end apart: 61, of which 31 were waited for; matrix products, arithmetic and copies ran while one was open for 19% of the time, Pallas kernels for 11%

profile of v5, /device:TPU:2, one launch (start us, length us, event | category | flops | bytes accessed | tf_op | source)
XLA Modules:
  0.0 616.2 jit_solution(7460006595669719066)
XLA Ops:
  10.5 10.8 %all_to_all.40 = bf16[4,48,1152]{2,1,0:T(8,128)(2,1)} all-to-all(bf16[4,48,1152]{2,1,0:T(8,128)(2,1)S(1)} %copy.143), channel_id=1, replica_groups=mesh['y'=2,'core'=2,'far'=1,'z'=4,'x'=2] {'y','x'}, dimensions={0} | all-to-all | bytes 884736 | tf_op jit(solution)/shard_map/all_to_all | solution.py:581
  27.0 5.2 all-to-all-start
  84.0 4.8 all-to-all-start.2
  94.4 4.8 collective-permute-start.12
  109.7 15.0 %collective-permute-done.11 = bf16[2,2,1,32,1536]{4,3,2,1,0:T(8,128)(2,1)} collective-permute-done((bf16[2,2,1,32,1536]{4,3,2,1,0:T(8,128)(2,1)}, bf16[2,2,1,32,1536]{4,3,2,1,0:T(8,128)(2,1)}, u32[]{:S(2)}, u32[]{:S(2)}) %collective-permute-start.11) | collective-permute-done | bytes 393248 | tf_op jit(solution)/shard_map/ppermute | solution.py:108
  127.1 21.0 %shard_map.345 = (bf16[8,192,128]{2,1,0:T(8,128)(2,1)}, f32[12,64,256]{2,1,0:T(8,128)S(1)}, f32[12,1,256]{2,1,0:T(1,128)S(1)}) custom-call(bf16[8,704,128]{2,1,0:T(8,128)(2,1)} %all-to-all-done.2.kv_ref.q_ref, bf16[8,704,128]{2,1,0:T(8,128)(2,1)} %all-to-all-done.2.kv_ref.q_ref), custom_call_target="tpu_custom_call" | custom-call | flops 3221225472 | bytes 4075520 | tf_op jit(solution)/shard_map/pallas_call | solution.py:445
  149.1 10.3 %all-to-all-start.4 = ((bf16[8,192,128]{2,1,0:T(8,128)(2,1)}), bf16[8,192,128]{2,1,0:T(8,128)(2,1)S(1)}, u32[]{:S(2)}, u32[]{:S(2)}) async-start(bf16[8,192,128]{2,1,0:T(8,128)(2,1)} %get-tuple-element.99), calls=%async_computation.4 | async-start | bytes 786432 | tf_op jit(solution)/shard_map/all_to_all | solution.py:690
  167.4 15.2 %all-to-all-done.4.o_ref = bf16[8,192,128]{2,1,0:T(8,128)(2,1)S(1)} async-done(((bf16[8,192,128]{2,1,0:T(8,128)(2,1)}), bf16[8,192,128]{2,1,0:T(8,128)(2,1)S(1)}, u32[]{:S(2)}, u32[]{:S(2)}) %all-to-all-start.4) | async-done | bytes 393248 | tf_op jit(solution)/shard_map/all_to_all | solution.py:690
  190.3 9.5 %collective-permute-done.13 = bf16[2,64,1536]{2,1,0:T(8,128)(2,1)S(1)} collective-permute-done((bf16[2,64,1536]{2,1,0:T(8,128)(2,1)S(1)}, bf16[2,64,1536]{2,1,0:T(8,128)(2,1)S(1)}, u32[]{:S(2)}, u32[]{:S(2)}) %collective-permute-start.13) | collective-permute-done | bytes 393248 | tf_op jit(solution)/shard_map/ppermute | solution.py:29
  199.8 7.2 %collective-permute-done.14 = bf16[2,64,1536]{2,1,0:T(8,128)(2,1)S(1)} collective-permute-done((bf16[2,64,1536]{2,1,0:T(8,128)(2,1)S(1)}, bf16[2,64,1536]{2,1,0:T(8,128)(2,1)S(1)}, u32[]{:S(2)}, u32[]{:S(2)}) %collective-permute-start.14) | collective-permute-done | bytes 393248 | tf_op jit(solution)/shard_map/ppermute | solution.py:29
  219.3 6.1 collective-permute-done.16
  225.4 7.5 %collective-permute-done.17 = bf16[2,64,1536]{2,1,0:T(8,128)(2,1)S(1)} collective-permute-done((bf16[2,64,1536]{2,1,0:T(8,128)(2,1)S(1)}, bf16[2,64,1536]{2,1,0:T(8,128)(2,1)S(1)}, u32[]{:S(2)}, u32[]{:S(2)}) %collective-permute-start.17) | collective-permute-done | bytes 393248 | tf_op jit(solution)/shard_map/ppermute | solution.py:29
  233.1 12.7 %all-gather.11.cloned.1.call-done.w_dn_ref = bf16[1024,1536]{1,0:T(8,128)(2,1)} async-done(((bf16[128,1536]{1,0:T(8,128)(2,1)}), bf16[1024,1536]{1,0:T(8,128)(2,1)}) %all-gather.11.cloned.1.call-update) | async-done | bytes 3145744 | tf_op jit(solution)/shard_map/all_gather | solution.py:97
  250.5 6.6 %shard_map.348 = (f32[512,2048]{1,0:T(8,128)S(1)}, bf16[512,1024]{1,0:T(8,128)(2,1)S(1)}, f32[512,1536]{1,0:T(8,128)S(1)}) custom-call(bf16[512,1536]{1,0:T(8,128)(2,1)S(1)} %bitcast.234, bf16[1536,2048]{1,0:T(8,128)(2,1)S(1)} %bitcast.232, bf16[1024,1536]{1,0:T(8,128)(2,1)S(1)} %copy-done.30), custom_call_target="tpu_custom_call" | custom-call | flops 4831838208 | bytes 19398656 | tf_op jit(solution)/shard_map/pallas_call | solution.py:445
  261.1 9.2 %collective-permute-done.19 = bf16[2,64,1536]{2,1,0:T(8,128)(2,1)S(1)} collective-permute-done((bf16[2,64,1536]{2,1,0:T(8,128)(2,1)S(1)}, bf16[2,64,1536]{2,1,0:T(8,128)(2,1)S(1)}, u32[]{:S(2)}, u32[]{:S(2)}) %collective-permute-start.19) | collective-permute-done | bytes 393248 | tf_op jit(solution)/shard_map/ppermute | solution.py:29
  270.3 7.7 %collective-permute-done.20 = bf16[2,64,1536]{2,1,0:T(8,128)(2,1)S(1)} collective-permute-done((bf16[2,64,1536]{2,1,0:T(8,128)(2,1)S(1)}, bf16[2,64,1536]{2,1,0:T(8,128)(2,1)S(1)}, u32[]{:S(2)}, u32[]{:S(2)}) %collective-permute-start.20) | collective-permute-done | bytes 393248 | tf_op jit(solution)/shard_map/ppermute | solution.py:29
  284.3 8.5 %collective-permute-done.22 = bf16[2,64,1536]{2,1,0:T(8,128)(2,1)S(1)} collective-permute-done((bf16[2,64,1536]{2,1,0:T(8,128)(2,1)S(1)}, bf16[2,64,1536]{2,1,0:T(8,128)(2,1)S(1)}, u32[]{:S(2)}, u32[]{:S(2)}) %collective-permute-start.22) | collective-permute-done | bytes 393248 | tf_op jit(solution)/shard_map/ppermute | solution.py:29
  292.8 7.7 %collective-permute-done.23 = bf16[2,64,1536]{2,1,0:T(8,128)(2,1)S(1)} collective-permute-done((bf16[2,64,1536]{2,1,0:T(8,128)(2,1)S(1)}, bf16[2,64,1536]{2,1,0:T(8,128)(2,1)S(1)}, u32[]{:S(2)}, u32[]{:S(2)}) %collective-permute-start.23) | collective-permute-done | bytes 393248 | tf_op jit(solution)/shard_map/ppermute | solution.py:29
  300.7 9.6 %shard_map.349 = (bf16[512,2048]{1,0:T(8,128)(2,1)S(1)}, f32[512,1536]{1,0:T(8,128)S(1)}) custom-call(bf16[512,1536]{1,0:T(8,128)(2,1)S(1)} %bitcast.236, bf16[1024,1536]{1,0:T(8,128)(2,1)S(1)} %copy-done.30, f32[512,2048]{1,0:T(8,128)S(1)} %get-tuple-element.118.gu_ref, bf16[1536,2048]{1,0:T(8,128)(2,1)S(1)} %bitcast.233), custom_call_target="tpu_custom_call" | custom-call | flops 4831838208 | bytes 20447232 | tf_op jit(solution)/shard_map/pallas_call | solution.py:445
  315.6 7.3 %shard_map.350 = bf16[8,4608,128]{2,1,0:T(8,128)(2,1)S(1)} custom-call(bf16[512,1024]{1,0:T(8,128)(2,1)S(1)} %get-tuple-element.120.hidden_ref, bf16[512,1536]{1,0:T(8,128)(2,1)S(1)} %bitcast.237, bf16[512,1536]{1,0:T(8,128)(2,1)S(1)} %bitcast.235, bf16[512,2048]{1,0:T(8,128)(2,1)S(1)} %get-tuple-element.121.dgu_ref), custom_call_target="tpu_custom_call" | custom-call | flops 4831838208 | bytes 15728640 | tf_op jit(solution)/shard_map/pallas_call | solution.py:445
  341.4 8.5 %collective-permute-done.28 = bf16[2,64,1536]{2,1,0:T(8,128)(2,1)S(1)} collective-permute-done((bf16[2,64,1536]{2,1,0:T(8,128)(2,1)S(1)}, bf16[2,64,1536]{2,1,0:T(8,128)(2,1)S(1)}, u32[]{:S(2)}, u32[]{:S(2)}) %collective-permute-start.28) | collective-permute-done | bytes 393248 | tf_op jit(solution)/shard_map/ppermute | solution.py:29
  349.9 8.8 %collective-permute-done.29 = bf16[2,64,1536]{2,1,0:T(8,128)(2,1)S(1)} collective-permute-done((bf16[2,64,1536]{2,1,0:T(8,128)(2,1)S(1)}, bf16[2,64,1536]{2,1,0:T(8,128)(2,1)S(1)}, u32[]{:S(2)}, u32[]{:S(2)}) %collective-permute-start.29) | collective-permute-done | bytes 393248 | tf_op jit(solution)/shard_map/ppermute | solution.py:29
  376.3 10.5 %all-to-all-done.5.do_ref = bf16[8,192,128]{2,1,0:T(8,128)(2,1)} async-done(((bf16[8,192,128]{2,1,0:T(8,128)(2,1)}), bf16[8,192,128]{2,1,0:T(8,128)(2,1)}, u32[]{:S(2)}, u32[]{:S(2)}) %all-to-all-start.5) | async-done | bytes 393248 | tf_op jit(solution)/shard_map/all_to_all | solution.py:769
  388.0 21.9 %shard_map.352 = bf16[8,704,128]{2,1,0:T(8,128)(2,1)S(1)} custom-call(bf16[8,704,128]{2,1,0:T(8,128)(2,1)} %all-to-all-done.2.kv_ref.q_ref, bf16[8,704,128]{2,1,0:T(8,128)(2,1)} %all-to-all-done.2.kv_ref.q_ref, bf16[8,192,128]{2,1,0:T(8,128)(2,1)} %all-to-all-done.5.do_ref, f32[12,64,256]{2,1,0:T(8,128)S(1)} %copy-done.36, ...), custom_call_target="tpu_custom_call" | custom-call | flops 8053063680 | bytes 5517312 | tf_op jit(solution)/shard_map/pallas_call | solution.py:445
  420.3 6.8 %shard_map.353 = (f32[4,2,64,384]{3,2,1,0:T(8,128)S(1)}, f32[384,512]{1,0:T(8,128)S(1)}, f32[384,512]{1,0:T(8,128)S(1)}) custom-call(bf16[4,2,64,384]{3,2,1,0:T(8,128)(2,1)S(1)} %bitcast.244, bf16[384,512]{1,0:T(8,128)(2,1)S(1)} %copy-done.17, bf16[384,512]{1,0:T(8,128)(2,1)S(1)} %bitcast.239, f32[512,1]{1,0:T(8,128)S(1)} %bitcast.241, ...), custom_call_target="tpu_custom_call" | custom-call | flops 503316480 | bytes 4194304 | tf_op jit(solution)/shard_map/pallas_call | solution.py:461
  436.4 29.9 %all-to-all-done.6.d_ref = bf16[8,704,128]{2,1,0:T(8,128)(2,1)} async-done(((bf16[8,704,128]{2,1,0:T(8,128)(2,1)}), bf16[8,704,128]{2,1,0:T(8,128)(2,1)}, u32[]{:S(2)}, u32[]{:S(2)}) %all-to-all-start.6) | async-done | bytes 1441824 | tf_op jit(solution)/shard_map/all_to_all | solution.py:845
  501.4 5.6 collective-permute-done.39
  507.0 5.9 collective-permute-done.40
  538.1 7.3 %all-to-all-start.7 = ((f32[32,7,128]{2,1,0:T(8,128)}), f32[32,7,128]{2,1,0:T(8,128)S(1)}, u32[]{:S(2)}, u32[]{:S(2)}) async-start(f32[32,7,128]{2,1,0:T(8,128)} %reshape.728), calls=%async_computation.10 | async-start | bytes 262144 | tf_op jit(solution)/shard_map/all_to_all | solution.py:840
  556.0 5.4 collective-permute-done.46
  581.6 9.5 %collective-permute-done.43 = bf16[192,1152]{1,0:T(8,128)(2,1)S(1)} collective-permute-done((bf16[192,1152]{1,0:T(8,128)(2,1)}, bf16[192,1152]{1,0:T(8,128)(2,1)S(1)}, u32[]{:S(2)}, u32[]{:S(2)}) %collective-permute-start.43) | collective-permute-done | bytes 442400 | tf_op jit(solution)/shard_map/ppermute | solution.py:71
  591.1 13.5 %collective-permute-done.42 = bf16[704,384]{1,0:T(8,128)(2,1)S(1)} collective-permute-done((bf16[704,384]{1,0:T(8,128)(2,1)}, bf16[704,384]{1,0:T(8,128)(2,1)S(1)}, u32[]{:S(2)}, u32[]{:S(2)}) %collective-permute-start.42) | collective-permute-done | bytes 540704 | tf_op jit(solution)/shard_map/ppermute | solution.py:71
  (583 shorter events, 278.7 us)
Async XLA Ops:
  7.2 57.6 %all-gather.5.cloned.1.call-start = ((), (), s32[]{:S(2)}) async-start(), calls=%async_computation.11 | async-start | bytes 3981312 | tf_op jit(solution)/shard_map/all_gather | solution.py:97
  21.4 37.0 %collective-permute-start = (bf16[2,64,1536]{2,1,0:T(8,128)(2,1)S(1)}, bf16[2,64,1536]{2,1,0:T(8,128)(2,1)S(1)}, u32[]{:S(2)}, u32[]{:S(2)}) collective-permute-start(bf16[2,64,1536]{2,1,0:T(8,128)(2,1)S(1)} %bitcast.246), channel_id=1, source_target_pairs={{0,1},{1,0},{16,17},{17,16},{2,3},{3,2},{18,19},{19,18},{4,5},{5,4... | collective-permute-start | bytes 1179656 | tf_op jit(solution)/shard_map/ppermute | solution.py:29
  22.8 35.6 %collective-permute-start.1 = (bf16[2,64,1536]{2,1,0:T(8,128)(2,1)S(1)}, bf16[2,64,1536]{2,1,0:T(8,128)(2,1)S(1)}, u32[]{:S(2)}, u32[]{:S(2)}) collective-permute-start(bf16[2,64,1536]{2,1,0:T(8,128)(2,1)S(1)} %bitcast.247), channel_id=1, source_target_pairs={{0,16},{1,17},{16,0},{17,1},{2,18},{3,19},{18,2},{19,3},{4,20},{5,... | collective-permute-start | bytes 1179656 | tf_op jit(solution)/shard_map/ppermute | solution.py:29
  23.5 34.9 %collective-permute-start.2 = (bf16[2,64,1536]{2,1,0:T(8,128)(2,1)S(1)}, bf16[2,64,1536]{2,1,0:T(8,128)(2,1)}, u32[]{:S(2)}, u32[]{:S(2)}) collective-permute-start(bf16[2,64,1536]{2,1,0:T(8,128)(2,1)S(1)} %bitcast.248), channel_id=1, source_target_pairs={{0,17},{1,16},{16,1},{17,0},{2,19},{3,18},{18,3},{19,2},{4,21},{5,... | collective-permute-start | bytes 1179656 | tf_op jit(solution)/shard_map/ppermute | solution.py:29
  32.2 69.4 %all-gather.7.cloned.1.call-start = ((), (), s32[]{:S(2)}) async-start(), calls=%async_computation.12 | async-start | bytes 2654208 | tf_op jit(solution)/shard_map/all_gather | solution.py:97
  54.8 29.2 %all-to-all-start.3 = ((bf16[4,48,2048]{2,1,0:T(8,128)(2,1)}), bf16[4,48,2048]{2,1,0:T(8,128)(2,1)S(1)}, u32[]{:S(2)}, u32[]{:S(2)}) async-start(bf16[4,48,2048]{2,1,0:T(8,128)(2,1)} %copy.150), calls=%async_computation.3 | async-start | bytes 1572864 | tf_op jit(solution)/shard_map/all_to_all | solution.py:581
  84.0 43.1 %all-to-all-start.2 = ((bf16[8,704,128]{2,1,0:T(8,128)(2,1)}), bf16[8,704,128]{2,1,0:T(8,128)(2,1)}, u32[]{:S(2)}, u32[]{:S(2)}) async-start(bf16[8,704,128]{2,1,0:T(8,128)(2,1)} %copy-done.20), calls=%async_computation.2 | async-start | bytes 2883584 | tf_op jit(solution)/shard_map/all_to_all | solution.py:672
  88.8 118.2 %all-gather.9.cloned.1.call-start = ((), (), s32[]{:S(2)}) async-start(), calls=%async_computation.13 | async-start | bytes 7077888 | tf_op jit(solution)/shard_map/all_gather | solution.py:97
  92.3 32.4 %collective-permute-start.11 = (bf16[2,2,1,32,1536]{4,3,2,1,0:T(8,128)(2,1)}, bf16[2,2,1,32,1536]{4,3,2,1,0:T(8,128)(2,1)}, u32[]{:S(2)}, u32[]{:S(2)}) collective-permute-start(bf16[2,2,1,32,1536]{4,3,2,1,0:T(8,128)(2,1)} %param.45), channel_id=1, source_target_pairs={{0,1},{1,2},{2,3},{3,4},{4,5},{5,6},{6,7},{8,9},{9,10},{10,11},{11... | collective-permute-start | bytes 1179656 | tf_op jit(solution)/shard_map/ppermute | solution.py:108
  94.4 30.4 %collective-permute-start.12 = (bf16[2,2,1,32,1536]{4,3,2,1,0:T(8,128)(2,1)}, bf16[2,2,1,32,1536]{4,3,2,1,0:T(8,128)(2,1)}, u32[]{:S(2)}, u32[]{:S(2)}) collective-permute-start(bf16[2,2,1,32,1536]{4,3,2,1,0:T(8,128)(2,1)} %param.45), channel_id=1, source_target_pairs={{1,0},{2,1},{3,2},{4,3},{5,4},{6,5},{7,6},{9,8},{10,9},{11,10},{12... | collective-permute-start | bytes 1179656 | tf_op jit(solution)/shard_map/ppermute | solution.py:109
  149.1 33.5 %all-to-all-start.4 = ((bf16[8,192,128]{2,1,0:T(8,128)(2,1)}), bf16[8,192,128]{2,1,0:T(8,128)(2,1)S(1)}, u32[]{:S(2)}, u32[]{:S(2)}) async-start(bf16[8,192,128]{2,1,0:T(8,128)(2,1)} %get-tuple-element.99), calls=%async_computation.4 | async-start | bytes 786432 | tf_op jit(solution)/shard_map/all_to_all | solution.py:690
  159.3 86.5 %all-gather.11.cloned.1.call-start = ((), (), s32[]{:S(2)}) async-start(), calls=%async_computation.14 | async-start | bytes 3538944 | tf_op jit(solution)/shard_map/all_gather | solution.py:97
  188.4 18.6 %collective-permute-start.14 = (bf16[2,64,1536]{2,1,0:T(8,128)(2,1)S(1)}, bf16[2,64,1536]{2,1,0:T(8,128)(2,1)S(1)}, u32[]{:S(2)}, u32[]{:S(2)}) collective-permute-start(bf16[2,64,1536]{2,1,0:T(8,128)(2,1)S(1)} %bitcast.302), channel_id=1, source_target_pairs={{0,16},{1,17},{16,0},{17,1},{2,18},{3,19},{18,2},{19,3},{4,20},{5,... | collective-permute-start | bytes 1179656 | tf_op jit(solution)/shard_map/ppermute | solution.py:29
  189.0 18.1 %collective-permute-start.15 = (bf16[2,64,1536]{2,1,0:T(8,128)(2,1)S(1)}, bf16[2,64,1536]{2,1,0:T(8,128)(2,1)S(1)}, u32[]{:S(2)}, u32[]{:S(2)}) collective-permute-start(bf16[2,64,1536]{2,1,0:T(8,128)(2,1)S(1)} %bitcast.299), channel_id=1, source_target_pairs={{0,1},{1,0},{16,17},{17,16},{2,3},{3,2},{18,19},{19,18},{4,5},{5,4... | collective-permute-start | bytes 1179656 | tf_op jit(solution)/shard_map/ppermute | solution.py:29
  207.1 259.3 %reduce-scatter.4.cloned.1.call-start = ((), (), s32[]{:S(2)}) async-start(), calls=%async_computation.15 | async-start | bytes 10616832 | tf_op jit(solution)/shard_map/reduce_scatter | solution.py:102
  214.2 18.6 %collective-permute-start.17 = (bf16[2,64,1536]{2,1,0:T(8,128)(2,1)S(1)}, bf16[2,64,1536]{2,1,0:T(8,128)(2,1)S(1)}, u32[]{:S(2)}, u32[]{:S(2)}) collective-permute-start(bf16[2,64,1536]{2,1,0:T(8,128)(2,1)S(1)} %multiply_convert_fusion), channel_id=1, source_target_pairs={{0,16},{1,17},{16,0},{17,1},{2,18},{3,19},{18,2},{19,3},{4,20},{5,... | collective-permute-start | bytes 1179656 | tf_op jit(solution)/shard_map/ppermute | solution.py:29
  215.0 17.9 %collective-permute-start.18 = (bf16[2,64,1536]{2,1,0:T(8,128)(2,1)S(1)}, bf16[2,64,1536]{2,1,0:T(8,128)(2,1)S(1)}, u32[]{:S(2)}, u32[]{:S(2)}) collective-permute-start(bf16[2,64,1536]{2,1,0:T(8,128)(2,1)S(1)} %multiply_convert_fusion), channel_id=1, source_target_pairs={{0,1},{1,0},{16,17},{17,16},{2,3},{3,2},{18,19},{19,18},{4,5},{5,4... | collective-permute-start | bytes 1179656 | tf_op jit(solution)/shard_map/ppermute | solution.py:29
  258.9 19.1 %collective-permute-start.20 = (bf16[2,64,1536]{2,1,0:T(8,128)(2,1)S(1)}, bf16[2,64,1536]{2,1,0:T(8,128)(2,1)S(1)}, u32[]{:S(2)}, u32[]{:S(2)}) collective-permute-start(bf16[2,64,1536]{2,1,0:T(8,128)(2,1)S(1)} %bitcast.301), channel_id=1, source_target_pairs={{0,16},{1,17},{16,0},{17,1},{2,18},{3,19},{18,2},{19,3},{4,20},{5,... | collective-permute-start | bytes 1179656 | tf_op jit(solution)/shard_map/ppermute | solution.py:29
  259.4 18.6 %collective-permute-start.21 = (bf16[2,64,1536]{2,1,0:T(8,128)(2,1)S(1)}, bf16[2,64,1536]{2,1,0:T(8,128)(2,1)S(1)}, u32[]{:S(2)}, u32[]{:S(2)}) collective-permute-start(bf16[2,64,1536]{2,1,0:T(8,128)(2,1)S(1)} %bitcast.297), channel_id=1, source_target_pairs={{0,1},{1,0},{16,17},{17,16},{2,3},{3,2},{18,19},{19,18},{4,5},{5,4... | collective-permute-start | bytes 1179656 | tf_op jit(solution)/shard_map/ppermute | solution.py:29
  281.4 19.1 %collective-permute-start.23 = (bf16[2,64,1536]{2,1,0:T(8,128)(2,1)S(1)}, bf16[2,64,1536]{2,1,0:T(8,128)(2,1)S(1)}, u32[]{:S(2)}, u32[]{:S(2)}) collective-permute-start(bf16[2,64,1536]{2,1,0:T(8,128)(2,1)S(1)} %fusion.14), channel_id=1, source_target_pairs={{0,16},{1,17},{16,0},{17,1},{2,18},{3,19},{18,2},{19,3},{4,20},{5,... | collective-permute-start | bytes 1179656 | tf_op jit(solution)/shard_map/ppermute | solution.py:29
  339.6 19.2 %collective-permute-start.29 = (bf16[2,64,1536]{2,1,0:T(8,128)(2,1)S(1)}, bf16[2,64,1536]{2,1,0:T(8,128)(2,1)S(1)}, u32[]{:S(2)}, u32[]{:S(2)}) collective-permute-start(bf16[2,64,1536]{2,1,0:T(8,128)(2,1)S(1)} %fusion.15), channel_id=1, source_target_pairs={{0,16},{1,17},{16,0},{17,1},{2,18},{3,19},{18,2},{19,3},{4,20},{5,... | collective-permute-start | bytes 1179656 | tf_op jit(solution)/shard_map/ppermute | solution.py:29
  340.0 18.7 %collective-permute-start.30 = (bf16[2,64,1536]{2,1,0:T(8,128)(2,1)S(1)}, bf16[2,64,1536]{2,1,0:T(8,128)(2,1)S(1)}, u32[]{:S(2)}, u32[]{:S(2)}) collective-permute-start(bf16[2,64,1536]{2,1,0:T(8,128)(2,1)S(1)} %fusion.15), channel_id=1, source_target_pairs={{0,17},{1,16},{16,1},{17,0},{2,19},{3,18},{18,3},{19,2},{4,21},{5,... | collective-permute-start | bytes 1179656 | tf_op jit(solution)/shard_map/ppermute | solution.py:29
  363.5 23.3 %all-to-all-start.5 = ((bf16[8,192,128]{2,1,0:T(8,128)(2,1)}), bf16[8,192,128]{2,1,0:T(8,128)(2,1)}, u32[]{:S(2)}, u32[]{:S(2)}) async-start(bf16[8,192,128]{2,1,0:T(8,128)(2,1)} %copy-done.26), calls=%async_computation.5 | async-start | bytes 786432 | tf_op jit(solution)/shard_map/all_to_all | solution.py:769
  369.5 41.5 %collective-permute-start.31 = (bf16[2,2,1,32,1536]{4,3,2,1,0:T(8,128)(2,1)}, bf16[2,2,1,32,1536]{4,3,2,1,0:T(8,128)(2,1)}, u32[]{:S(2)}, u32[]{:S(2)}) collective-permute-start(bf16[2,2,1,32,1536]{4,3,2,1,0:T(8,128)(2,1)} %convert_element_type.243), channel_id=1, source_target_pairs={{0,1},{1,2},{2,3},{3,4},{4,5},{5,6},{6,7},{8,9},{9,10},{10,11},{11... | collective-permute-start | bytes 1179656 | tf_op jit(solution)/shard_map/ppermute | solution.py:108
  373.2 37.8 %collective-permute-start.32 = (bf16[2,2,1,32,1536]{4,3,2,1,0:T(8,128)(2,1)}, bf16[2,2,1,32,1536]{4,3,2,1,0:T(8,128)(2,1)}, u32[]{:S(2)}, u32[]{:S(2)}) collective-permute-start(bf16[2,2,1,32,1536]{4,3,2,1,0:T(8,128)(2,1)} %convert_element_type.243), channel_id=1, source_target_pairs={{1,0},{2,1},{3,2},{4,3},{5,4},{6,5},{7,6},{9,8},{10,9},{11,10},{12... | collective-permute-start | bytes 1179656 | tf_op jit(solution)/shard_map/ppermute | solution.py:109
  411.0 55.3 %all-to-all-start.6 = ((bf16[8,704,128]{2,1,0:T(8,128)(2,1)}), bf16[8,704,128]{2,1,0:T(8,128)(2,1)}, u32[]{:S(2)}, u32[]{:S(2)}) async-start(bf16[8,704,128]{2,1,0:T(8,128)(2,1)} %copy-done.21), calls=%async_computation.6 | async-start | bytes 2883584 | tf_op jit(solution)/shard_map/all_to_all | solution.py:845
  415.3 97.8 %reduce-scatter.6.cloned.1.call-start = ((), (), s32[]{:S(2)}) async-start(), calls=%async_computation.16 | async-start | bytes 2359296 | tf_op jit(solution)/shard_map/reduce_scatter | solution.py:102
  466.3 101.1 %reduce-scatter.8.cloned.1.call-start = ((), (), s32[]{:S(2)}) async-start(), calls=%async_computation.17 | async-start | bytes 3981312 | tf_op jit(solution)/shard_map/reduce_scatter | solution.py:102
  531.0 25.0 %collective-permute-start.45 = (bf16[96,512]{1,0:T(8,128)(2,1)S(1)}, bf16[96,512]{1,0:T(8,128)(2,1)}, u32[]{:S(2)}, u32[]{:S(2)}) collective-permute-start(bf16[96,512]{1,0:T(8,128)(2,1)S(1)} %pad_maximum_fusion.7), channel_id=1, source_target_pairs={{1,8},{3,10},{5,12},{7,14},{8,1},{10,3},{12,5},{14,7},{17,24},{19,... | collective-permute-start | bytes 294920 | tf_op jit(solution)/shard_map/ppermute | solution.py:71
  534.1 21.9 %collective-permute-start.44 = (f32[1,48]{1,0:T(1,128)}, f32[1,48]{1,0:T(1,128)}, u32[]{:S(2)}, u32[]{:S(2)}) collective-permute-start(f32[1,48]{1,0:T(1,128)} %bitcast.98), channel_id=1, source_target_pairs={{1,8},{3,10},{5,12},{7,14},{8,1},{10,3},{12,5},{14,7},{17,24},{19,... | collective-permute-start | bytes 584 | tf_op jit(solution)/shard_map/ppermute | solution.py:71
  568.5 36.1 %collective-permute-start.42 = (bf16[704,384]{1,0:T(8,128)(2,1)}, bf16[704,384]{1,0:T(8,128)(2,1)S(1)}, u32[]{:S(2)}, u32[]{:S(2)}) collective-permute-start(bf16[704,384]{1,0:T(8,128)(2,1)} %copy.160), channel_id=1, source_target_pairs={{1,2},{2,1},{4,8},{5,10},{6,9},{7,11},{8,17},{9,19},{10,16},{11,18... | collective-permute-start | bytes 1622024 | tf_op jit(solution)/shard_map/ppermute | solution.py:71
  570.6 20.5 %collective-permute-start.43 = (bf16[192,1152]{1,0:T(8,128)(2,1)}, bf16[192,1152]{1,0:T(8,128)(2,1)S(1)}, u32[]{:S(2)}, u32[]{:S(2)}) collective-permute-start(bf16[192,1152]{1,0:T(8,128)(2,1)} %reduce-scatter.8.cloned.1.call-done), channel_id=1, source_target_pairs={{1,8},{3,10},{5,12},{7,14},{8,1},{10,3},{12,5},{14,7},{17,24},{19,... | collective-permute-start | bytes 1327112 | tf_op jit(solution)/shard_map/ppermute | solution.py:71
  (159 other events, 1221.4 us)
Sparse Core Ops, SparseCore 0:
  21.5 43.2 all-gather.4
  67.0 33.4 all-gather.6
  127.2 79.6 all-gather.8
  208.9 36.8 all-gather.10
  331.6 132.7 reduce-scatter.3
  466.6 46.5 reduce-scatter.5
  515.4 46.1 reduce-scatter.7

commit v6 on v5

--- a/solution.py
+++ b/solution.py
@@ -716,7 +716,7 @@
         w_gu,
         w_dn,
         flops=6 * count * width * ff_w,
-        grant=32,
+        grant=24,
     )
     z_out, _ = team_scatter(z_terms.reshape(group, clips, local, width))
 
@@ -739,7 +739,7 @@
         gate_up,
         w_gu,
         flops=6 * count * width * ff_w,
-        grant=32,
+        grant=24,
     )
 
     def term(left, right):
@@ -754,7 +754,7 @@
         f_in,
         d_gu,
         flops=6 * count * width * ff_w,
-        grant=32,
+        grant=24,
     )
     d_f_in, ff_terms = team_scatter(d_f_in.reshape(group, clips, local, width), ff_terms)
     ff_sum = group_scatter(ff_terms)
@@ -780,7 +780,7 @@
             lse,
             scratch=back_scratch,
             flops=5 * work,
-            grant=32 if n_far == 1 else 60,
+            grant=26 if n_far == 1 else 60,
         )
     else:
         d_kv, d_q = call(
@@ -793,7 +793,7 @@
             lse,
             scratch=back_scratch,
             flops=5 * work,
-            grant=32 if n_far == 1 else 60,
+            grant=26 if n_far == 1 else 60,
         )
         d_kv = lax.psum_scatter(d_kv, "far", scatter_dimension=0, tiled=True)
         d_send = jnp.concatenate([d_kv, d_q], axis=1)

time: 627 us -> 627 us (level)
  no operation moved by 1% of the time
where the time goes in v6:
time: 627 us; the launch traced here: 616 us
  waiting for transfers between devices  220 us (35%)
  starting transfers between devices  118 us (19%)
  local copies, waits for them, and re-layouts  96.9 us (15%)
  Pallas kernels  85.4 us (14%)
  other arithmetic  48.1 us (8%)
  matrix products  20.3 us (3%)
  between operations  17.1 us (3%)
  blocking collectives  10.8 us (2%)
    ppermute x36, waiting for transfers between devices, swap(): return lax.ppermute(value, TEAM, [(i, i ^ bits) for i in range(4)])  102 us
    pallas_call x10, Pallas kernels, call(): pl.pallas_call(kernel, out_shape=outs, in_specs=[spec] * len(args), out_s...  74.5 us
    ppermute x36, starting transfers between devices, swap(): return lax.ppermute(value, TEAM, [(i, i ^ bits) for i in range(4)])  44.7 us
    unnamed x265, local copies, waits for them, and re-layouts  43.2 us
    all_to_all x1, waiting for transfers between devices, body(): lax.all_to_all(d_send, PLANE, 0, 0)  29.9 us
    ppermute x7, waiting for transfers between devices, relocate(): return (stays, block, lax.ppermute(block, ALL, pairs))  28.4 us
    ppermute x7, starting transfers between devices, relocate(): return (stays, block, lax.ppermute(block, ALL, pairs))  19.7 us
    all_to_all x1, waiting for transfers between devices, body(): o_back = lax.all_to_all(o_pack, PLANE, 0, 0)  15.2 us
  transfers between devices with their start and end apart: 61, of which 31 were waited for; matrix products, arithmetic and copies ran while one was open for 19% of the time, Pallas kernels for 11%

profile of v6, /device:TPU:2, one launch (start us, length us, event | category | flops | bytes accessed | tf_op | source)
XLA Modules:
  0.0 616.2 jit_solution(1756093778172086843)
XLA Ops:
  10.5 10.8 %all_to_all.40 = bf16[4,48,1152]{2,1,0:T(8,128)(2,1)} all-to-all(bf16[4,48,1152]{2,1,0:T(8,128)(2,1)S(1)} %copy.143), channel_id=1, replica_groups=mesh['y'=2,'core'=2,'far'=1,'z'=4,'x'=2] {'y','x'}, dimensions={0} | all-to-all | bytes 884736 | tf_op jit(solution)/shard_map/all_to_all | solution.py:581
  27.0 5.2 all-to-all-start
  84.0 4.8 all-to-all-start.2
  94.4 4.8 collective-permute-start.12
  109.7 15.0 %collective-permute-done.11 = bf16[2,2,1,32,1536]{4,3,2,1,0:T(8,128)(2,1)} collective-permute-done((bf16[2,2,1,32,1536]{4,3,2,1,0:T(8,128)(2,1)}, bf16[2,2,1,32,1536]{4,3,2,1,0:T(8,128)(2,1)}, u32[]{:S(2)}, u32[]{:S(2)}) %collective-permute-start.11) | collective-permute-done | bytes 393248 | tf_op jit(solution)/shard_map/ppermute | solution.py:108
  127.1 21.0 %shard_map.345 = (bf16[8,192,128]{2,1,0:T(8,128)(2,1)}, f32[12,64,256]{2,1,0:T(8,128)S(1)}, f32[12,1,256]{2,1,0:T(1,128)S(1)}) custom-call(bf16[8,704,128]{2,1,0:T(8,128)(2,1)} %all-to-all-done.2.kv_ref.q_ref, bf16[8,704,128]{2,1,0:T(8,128)(2,1)} %all-to-all-done.2.kv_ref.q_ref), custom_call_target="tpu_custom_call" | custom-call | flops 3221225472 | bytes 4075520 | tf_op jit(solution)/shard_map/pallas_call | solution.py:445
  149.1 10.3 %all-to-all-start.4 = ((bf16[8,192,128]{2,1,0:T(8,128)(2,1)}), bf16[8,192,128]{2,1,0:T(8,128)(2,1)S(1)}, u32[]{:S(2)}, u32[]{:S(2)}) async-start(bf16[8,192,128]{2,1,0:T(8,128)(2,1)} %get-tuple-element.99), calls=%async_computation.4 | async-start | bytes 786432 | tf_op jit(solution)/shard_map/all_to_all | solution.py:690
  167.4 15.2 %all-to-all-done.4.o_ref = bf16[8,192,128]{2,1,0:T(8,128)(2,1)S(1)} async-done(((bf16[8,192,128]{2,1,0:T(8,128)(2,1)}), bf16[8,192,128]{2,1,0:T(8,128)(2,1)S(1)}, u32[]{:S(2)}, u32[]{:S(2)}) %all-to-all-start.4) | async-done | bytes 393248 | tf_op jit(solution)/shard_map/all_to_all | solution.py:690
  190.3 9.5 %collective-permute-done.13 = bf16[2,64,1536]{2,1,0:T(8,128)(2,1)S(1)} collective-permute-done((bf16[2,64,1536]{2,1,0:T(8,128)(2,1)S(1)}, bf16[2,64,1536]{2,1,0:T(8,128)(2,1)S(1)}, u32[]{:S(2)}, u32[]{:S(2)}) %collective-permute-start.13) | collective-permute-done | bytes 393248 | tf_op jit(solution)/shard_map/ppermute | solution.py:29
  199.8 7.2 %collective-permute-done.14 = bf16[2,64,1536]{2,1,0:T(8,128)(2,1)S(1)} collective-permute-done((bf16[2,64,1536]{2,1,0:T(8,128)(2,1)S(1)}, bf16[2,64,1536]{2,1,0:T(8,128)(2,1)S(1)}, u32[]{:S(2)}, u32[]{:S(2)}) %collective-permute-start.14) | collective-permute-done | bytes 393248 | tf_op jit(solution)/shard_map/ppermute | solution.py:29
  219.3 6.1 collective-permute-done.16
  225.4 7.5 %collective-permute-done.17 = bf16[2,64,1536]{2,1,0:T(8,128)(2,1)S(1)} collective-permute-done((bf16[2,64,1536]{2,1,0:T(8,128)(2,1)S(1)}, bf16[2,64,1536]{2,1,0:T(8,128)(2,1)S(1)}, u32[]{:S(2)}, u32[]{:S(2)}) %collective-permute-start.17) | collective-permute-done | bytes 393248 | tf_op jit(solution)/shard_map/ppermute | solution.py:29
  233.1 12.7 %all-gather.11.cloned.1.call-done.w_dn_ref = bf16[1024,1536]{1,0:T(8,128)(2,1)} async-done(((bf16[128,1536]{1,0:T(8,128)(2,1)}), bf16[1024,1536]{1,0:T(8,128)(2,1)}) %all-gather.11.cloned.1.call-update) | async-done | bytes 3145744 | tf_op jit(solution)/shard_map/all_gather | solution.py:97
  250.5 6.6 %shard_map.348 = (f32[512,2048]{1,0:T(8,128)S(1)}, bf16[512,1024]{1,0:T(8,128)(2,1)S(1)}, f32[512,1536]{1,0:T(8,128)S(1)}) custom-call(bf16[512,1536]{1,0:T(8,128)(2,1)S(1)} %bitcast.234, bf16[1536,2048]{1,0:T(8,128)(2,1)S(1)} %bitcast.232, bf16[1024,1536]{1,0:T(8,128)(2,1)S(1)} %copy-done.30), custom_call_target="tpu_custom_call" | custom-call | flops 4831838208 | bytes 19398656 | tf_op jit(solution)/shard_map/pallas_call | solution.py:445
  261.1 9.2 %collective-permute-done.19 = bf16[2,64,1536]{2,1,0:T(8,128)(2,1)S(1)} collective-permute-done((bf16[2,64,1536]{2,1,0:T(8,128)(2,1)S(1)}, bf16[2,64,1536]{2,1,0:T(8,128)(2,1)S(1)}, u32[]{:S(2)}, u32[]{:S(2)}) %collective-permute-start.19) | collective-permute-done | bytes 393248 | tf_op jit(solution)/shard_map/ppermute | solution.py:29
  270.3 7.7 %collective-permute-done.20 = bf16[2,64,1536]{2,1,0:T(8,128)(2,1)S(1)} collective-permute-done((bf16[2,64,1536]{2,1,0:T(8,128)(2,1)S(1)}, bf16[2,64,1536]{2,1,0:T(8,128)(2,1)S(1)}, u32[]{:S(2)}, u32[]{:S(2)}) %collective-permute-start.20) | collective-permute-done | bytes 393248 | tf_op jit(solution)/shard_map/ppermute | solution.py:29
  284.3 8.5 %collective-permute-done.22 = bf16[2,64,1536]{2,1,0:T(8,128)(2,1)S(1)} collective-permute-done((bf16[2,64,1536]{2,1,0:T(8,128)(2,1)S(1)}, bf16[2,64,1536]{2,1,0:T(8,128)(2,1)S(1)}, u32[]{:S(2)}, u32[]{:S(2)}) %collective-permute-start.22) | collective-permute-done | bytes 393248 | tf_op jit(solution)/shard_map/ppermute | solution.py:29
  292.8 7.7 %collective-permute-done.23 = bf16[2,64,1536]{2,1,0:T(8,128)(2,1)S(1)} collective-permute-done((bf16[2,64,1536]{2,1,0:T(8,128)(2,1)S(1)}, bf16[2,64,1536]{2,1,0:T(8,128)(2,1)S(1)}, u32[]{:S(2)}, u32[]{:S(2)}) %collective-permute-start.23) | collective-permute-done | bytes 393248 | tf_op jit(solution)/shard_map/ppermute | solution.py:29
  300.7 9.6 %shard_map.349 = (bf16[512,2048]{1,0:T(8,128)(2,1)S(1)}, f32[512,1536]{1,0:T(8,128)S(1)}) custom-call(bf16[512,1536]{1,0:T(8,128)(2,1)S(1)} %bitcast.236, bf16[1024,1536]{1,0:T(8,128)(2,1)S(1)} %copy-done.30, f32[512,2048]{1,0:T(8,128)S(1)} %get-tuple-element.118.gu_ref, bf16[1536,2048]{1,0:T(8,128)(2,1)S(1)} %bitcast.233), custom_call_target="tpu_custom_call" | custom-call | flops 4831838208 | bytes 20447232 | tf_op jit(solution)/shard_map/pallas_call | solution.py:445
  315.6 7.3 %shard_map.350 = bf16[8,4608,128]{2,1,0:T(8,128)(2,1)S(1)} custom-call(bf16[512,1024]{1,0:T(8,128)(2,1)S(1)} %get-tuple-element.120.hidden_ref, bf16[512,1536]{1,0:T(8,128)(2,1)S(1)} %bitcast.237, bf16[512,1536]{1,0:T(8,128)(2,1)S(1)} %bitcast.235, bf16[512,2048]{1,0:T(8,128)(2,1)S(1)} %get-tuple-element.121.dgu_ref), custom_call_target="tpu_custom_call" | custom-call | flops 4831838208 | bytes 15728640 | tf_op jit(solution)/shard_map/pallas_call | solution.py:445
  341.5 8.5 %collective-permute-done.28 = bf16[2,64,1536]{2,1,0:T(8,128)(2,1)S(1)} collective-permute-done((bf16[2,64,1536]{2,1,0:T(8,128)(2,1)S(1)}, bf16[2,64,1536]{2,1,0:T(8,128)(2,1)S(1)}, u32[]{:S(2)}, u32[]{:S(2)}) %collective-permute-start.28) | collective-permute-done | bytes 393248 | tf_op jit(solution)/shard_map/ppermute | solution.py:29
  350.0 8.8 %collective-permute-done.29 = bf16[2,64,1536]{2,1,0:T(8,128)(2,1)S(1)} collective-permute-done((bf16[2,64,1536]{2,1,0:T(8,128)(2,1)S(1)}, bf16[2,64,1536]{2,1,0:T(8,128)(2,1)S(1)}, u32[]{:S(2)}, u32[]{:S(2)}) %collective-permute-start.29) | collective-permute-done | bytes 393248 | tf_op jit(solution)/shard_map/ppermute | solution.py:29
  376.4 10.5 %all-to-all-done.5.do_ref = bf16[8,192,128]{2,1,0:T(8,128)(2,1)} async-done(((bf16[8,192,128]{2,1,0:T(8,128)(2,1)}), bf16[8,192,128]{2,1,0:T(8,128)(2,1)}, u32[]{:S(2)}, u32[]{:S(2)}) %all-to-all-start.5) | async-done | bytes 393248 | tf_op jit(solution)/shard_map/all_to_all | solution.py:769
  388.0 21.9 %shard_map.352 = bf16[8,704,128]{2,1,0:T(8,128)(2,1)S(1)} custom-call(bf16[8,704,128]{2,1,0:T(8,128)(2,1)} %all-to-all-done.2.kv_ref.q_ref, bf16[8,704,128]{2,1,0:T(8,128)(2,1)} %all-to-all-done.2.kv_ref.q_ref, bf16[8,192,128]{2,1,0:T(8,128)(2,1)} %all-to-all-done.5.do_ref, f32[12,64,256]{2,1,0:T(8,128)S(1)} %copy-done.36, ...), custom_call_target="tpu_custom_call" | custom-call | flops 8053063680 | bytes 5517312 | tf_op jit(solution)/shard_map/pallas_call | solution.py:445
  420.4 6.8 %shard_map.353 = (f32[4,2,64,384]{3,2,1,0:T(8,128)S(1)}, f32[384,512]{1,0:T(8,128)S(1)}, f32[384,512]{1,0:T(8,128)S(1)}) custom-call(bf16[4,2,64,384]{3,2,1,0:T(8,128)(2,1)S(1)} %bitcast.244, bf16[384,512]{1,0:T(8,128)(2,1)S(1)} %copy-done.17, bf16[384,512]{1,0:T(8,128)(2,1)S(1)} %bitcast.239, f32[512,1]{1,0:T(8,128)S(1)} %bitcast.241, ...), custom_call_target="tpu_custom_call" | custom-call | flops 503316480 | bytes 4194304 | tf_op jit(solution)/shard_map/pallas_call | solution.py:461
  436.5 29.9 %all-to-all-done.6.d_ref = bf16[8,704,128]{2,1,0:T(8,128)(2,1)} async-done(((bf16[8,704,128]{2,1,0:T(8,128)(2,1)}), bf16[8,704,128]{2,1,0:T(8,128)(2,1)}, u32[]{:S(2)}, u32[]{:S(2)}) %all-to-all-start.6) | async-done | bytes 1441824 | tf_op jit(solution)/shard_map/all_to_all | solution.py:845
  501.5 5.6 collective-permute-done.39
  507.1 5.9 collective-permute-done.40
  538.1 7.3 %all-to-all-start.7 = ((f32[32,7,128]{2,1,0:T(8,128)}), f32[32,7,128]{2,1,0:T(8,128)S(1)}, u32[]{:S(2)}, u32[]{:S(2)}) async-start(f32[32,7,128]{2,1,0:T(8,128)} %reshape.728), calls=%async_computation.10 | async-start | bytes 262144 | tf_op jit(solution)/shard_map/all_to_all | solution.py:840
  556.0 5.4 collective-permute-done.46
  581.6 9.5 %collective-permute-done.43 = bf16[192,1152]{1,0:T(8,128)(2,1)S(1)} collective-permute-done((bf16[192,1152]{1,0:T(8,128)(2,1)}, bf16[192,1152]{1,0:T(8,128)(2,1)S(1)}, u32[]{:S(2)}, u32[]{:S(2)}) %collective-permute-start.43) | collective-permute-done | bytes 442400 | tf_op jit(solution)/shard_map/ppermute | solution.py:71
  591.1 13.5 %collective-permute-done.42 = bf16[704,384]{1,0:T(8,128)(2,1)S(1)} collective-permute-done((bf16[704,384]{1,0:T(8,128)(2,1)}, bf16[704,384]{1,0:T(8,128)(2,1)S(1)}, u32[]{:S(2)}, u32[]{:S(2)}) %collective-permute-start.42) | collective-permute-done | bytes 540704 | tf_op jit(solution)/shard_map/ppermute | solution.py:71
  (583 shorter events, 278.7 us)
Async XLA Ops:
  7.2 57.6 %all-gather.5.cloned.1.call-start = ((), (), s32[]{:S(2)}) async-start(), calls=%async_computation.11 | async-start | bytes 3981312 | tf_op jit(solution)/shard_map/all_gather | solution.py:97
  21.4 37.0 %collective-permute-start = (bf16[2,64,1536]{2,1,0:T(8,128)(2,1)S(1)}, bf16[2,64,1536]{2,1,0:T(8,128)(2,1)S(1)}, u32[]{:S(2)}, u32[]{:S(2)}) collective-permute-start(bf16[2,64,1536]{2,1,0:T(8,128)(2,1)S(1)} %bitcast.246), channel_id=1, source_target_pairs={{0,1},{1,0},{16,17},{17,16},{2,3},{3,2},{18,19},{19,18},{4,5},{5,4... | collective-permute-start | bytes 1179656 | tf_op jit(solution)/shard_map/ppermute | solution.py:29
  22.8 35.6 %collective-permute-start.1 = (bf16[2,64,1536]{2,1,0:T(8,128)(2,1)S(1)}, bf16[2,64,1536]{2,1,0:T(8,128)(2,1)S(1)}, u32[]{:S(2)}, u32[]{:S(2)}) collective-permute-start(bf16[2,64,1536]{2,1,0:T(8,128)(2,1)S(1)} %bitcast.247), channel_id=1, source_target_pairs={{0,16},{1,17},{16,0},{17,1},{2,18},{3,19},{18,2},{19,3},{4,20},{5,... | collective-permute-start | bytes 1179656 | tf_op jit(solution)/shard_map/ppermute | solution.py:29
  23.5 34.9 %collective-permute-start.2 = (bf16[2,64,1536]{2,1,0:T(8,128)(2,1)S(1)}, bf16[2,64,1536]{2,1,0:T(8,128)(2,1)}, u32[]{:S(2)}, u32[]{:S(2)}) collective-permute-start(bf16[2,64,1536]{2,1,0:T(8,128)(2,1)S(1)} %bitcast.248), channel_id=1, source_target_pairs={{0,17},{1,16},{16,1},{17,0},{2,19},{3,18},{18,3},{19,2},{4,21},{5,... | collective-permute-start | bytes 1179656 | tf_op jit(solution)/shard_map/ppermute | solution.py:29
  32.2 69.4 %all-gather.7.cloned.1.call-start = ((), (), s32[]{:S(2)}) async-start(), calls=%async_computation.12 | async-start | bytes 2654208 | tf_op jit(solution)/shard_map/all_gather | solution.py:97
  54.8 29.2 %all-to-all-start.3 = ((bf16[4,48,2048]{2,1,0:T(8,128)(2,1)}), bf16[4,48,2048]{2,1,0:T(8,128)(2,1)S(1)}, u32[]{:S(2)}, u32[]{:S(2)}) async-start(bf16[4,48,2048]{2,1,0:T(8,128)(2,1)} %copy.150), calls=%async_computation.3 | async-start | bytes 1572864 | tf_op jit(solution)/shard_map/all_to_all | solution.py:581
  84.0 43.1 %all-to-all-start.2 = ((bf16[8,704,128]{2,1,0:T(8,128)(2,1)}), bf16[8,704,128]{2,1,0:T(8,128)(2,1)}, u32[]{:S(2)}, u32[]{:S(2)}) async-start(bf16[8,704,128]{2,1,0:T(8,128)(2,1)} %copy-done.20), calls=%async_computation.2 | async-start | bytes 2883584 | tf_op jit(solution)/shard_map/all_to_all | solution.py:672
  88.8 118.2 %all-gather.9.cloned.1.call-start = ((), (), s32[]{:S(2)}) async-start(), calls=%async_computation.13 | async-start | bytes 7077888 | tf_op jit(solution)/shard_map/all_gather | solution.py:97
  92.3 32.4 %collective-permute-start.11 = (bf16[2,2,1,32,1536]{4,3,2,1,0:T(8,128)(2,1)}, bf16[2,2,1,32,1536]{4,3,2,1,0:T(8,128)(2,1)}, u32[]{:S(2)}, u32[]{:S(2)}) collective-permute-start(bf16[2,2,1,32,1536]{4,3,2,1,0:T(8,128)(2,1)} %param.45), channel_id=1, source_target_pairs={{0,1},{1,2},{2,3},{3,4},{4,5},{5,6},{6,7},{8,9},{9,10},{10,11},{11... | collective-permute-start | bytes 1179656 | tf_op jit(solution)/shard_map/ppermute | solution.py:108
  94.4 30.4 %collective-permute-start.12 = (bf16[2,2,1,32,1536]{4,3,2,1,0:T(8,128)(2,1)}, bf16[2,2,1,32,1536]{4,3,2,1,0:T(8,128)(2,1)}, u32[]{:S(2)}, u32[]{:S(2)}) collective-permute-start(bf16[2,2,1,32,1536]{4,3,2,1,0:T(8,128)(2,1)} %param.45), channel_id=1, source_target_pairs={{1,0},{2,1},{3,2},{4,3},{5,4},{6,5},{7,6},{9,8},{10,9},{11,10},{12... | collective-permute-start | bytes 1179656 | tf_op jit(solution)/shard_map/ppermute | solution.py:109
  149.1 33.5 %all-to-all-start.4 = ((bf16[8,192,128]{2,1,0:T(8,128)(2,1)}), bf16[8,192,128]{2,1,0:T(8,128)(2,1)S(1)}, u32[]{:S(2)}, u32[]{:S(2)}) async-start(bf16[8,192,128]{2,1,0:T(8,128)(2,1)} %get-tuple-element.99), calls=%async_computation.4 | async-start | bytes 786432 | tf_op jit(solution)/shard_map/all_to_all | solution.py:690
  159.3 86.5 %all-gather.11.cloned.1.call-start = ((), (), s32[]{:S(2)}) async-start(), calls=%async_computation.14 | async-start | bytes 3538944 | tf_op jit(solution)/shard_map/all_gather | solution.py:97
  188.4 18.6 %collective-permute-start.14 = (bf16[2,64,1536]{2,1,0:T(8,128)(2,1)S(1)}, bf16[2,64,1536]{2,1,0:T(8,128)(2,1)S(1)}, u32[]{:S(2)}, u32[]{:S(2)}) collective-permute-start(bf16[2,64,1536]{2,1,0:T(8,128)(2,1)S(1)} %bitcast.302), channel_id=1, source_target_pairs={{0,16},{1,17},{16,0},{17,1},{2,18},{3,19},{18,2},{19,3},{4,20},{5,... | collective-permute-start | bytes 1179656 | tf_op jit(solution)/shard_map/ppermute | solution.py:29
  189.0 18.1 %collective-permute-start.15 = (bf16[2,64,1536]{2,1,0:T(8,128)(2,1)S(1)}, bf16[2,64,1536]{2,1,0:T(8,128)(2,1)S(1)}, u32[]{:S(2)}, u32[]{:S(2)}) collective-permute-start(bf16[2,64,1536]{2,1,0:T(8,128)(2,1)S(1)} %bitcast.299), channel_id=1, source_target_pairs={{0,1},{1,0},{16,17},{17,16},{2,3},{3,2},{18,19},{19,18},{4,5},{5,4... | collective-permute-start | bytes 1179656 | tf_op jit(solution)/shard_map/ppermute | solution.py:29
  207.1 259.3 %reduce-scatter.4.cloned.1.call-start = ((), (), s32[]{:S(2)}) async-start(), calls=%async_computation.15 | async-start | bytes 10616832 | tf_op jit(solution)/shard_map/reduce_scatter | solution.py:102
  214.2 18.6 %collective-permute-start.17 = (bf16[2,64,1536]{2,1,0:T(8,128)(2,1)S(1)}, bf16[2,64,1536]{2,1,0:T(8,128)(2,1)S(1)}, u32[]{:S(2)}, u32[]{:S(2)}) collective-permute-start(bf16[2,64,1536]{2,1,0:T(8,128)(2,1)S(1)} %multiply_convert_fusion), channel_id=1, source_target_pairs={{0,16},{1,17},{16,0},{17,1},{2,18},{3,19},{18,2},{19,3},{4,20},{5,... | collective-permute-start | bytes 1179656 | tf_op jit(solution)/shard_map/ppermute | solution.py:29
  215.0 17.9 %collective-permute-start.18 = (bf16[2,64,1536]{2,1,0:T(8,128)(2,1)S(1)}, bf16[2,64,1536]{2,1,0:T(8,128)(2,1)S(1)}, u32[]{:S(2)}, u32[]{:S(2)}) collective-permute-start(bf16[2,64,1536]{2,1,0:T(8,128)(2,1)S(1)} %multiply_convert_fusion), channel_id=1, source_target_pairs={{0,1},{1,0},{16,17},{17,16},{2,3},{3,2},{18,19},{19,18},{4,5},{5,4... | collective-permute-start | bytes 1179656 | tf_op jit(solution)/shard_map/ppermute | solution.py:29
  258.9 19.1 %collective-permute-start.20 = (bf16[2,64,1536]{2,1,0:T(8,128)(2,1)S(1)}, bf16[2,64,1536]{2,1,0:T(8,128)(2,1)S(1)}, u32[]{:S(2)}, u32[]{:S(2)}) collective-permute-start(bf16[2,64,1536]{2,1,0:T(8,128)(2,1)S(1)} %bitcast.301), channel_id=1, source_target_pairs={{0,16},{1,17},{16,0},{17,1},{2,18},{3,19},{18,2},{19,3},{4,20},{5,... | collective-permute-start | bytes 1179656 | tf_op jit(solution)/shard_map/ppermute | solution.py:29
  259.4 18.6 %collective-permute-start.21 = (bf16[2,64,1536]{2,1,0:T(8,128)(2,1)S(1)}, bf16[2,64,1536]{2,1,0:T(8,128)(2,1)S(1)}, u32[]{:S(2)}, u32[]{:S(2)}) collective-permute-start(bf16[2,64,1536]{2,1,0:T(8,128)(2,1)S(1)} %bitcast.297), channel_id=1, source_target_pairs={{0,1},{1,0},{16,17},{17,16},{2,3},{3,2},{18,19},{19,18},{4,5},{5,4... | collective-permute-start | bytes 1179656 | tf_op jit(solution)/shard_map/ppermute | solution.py:29
  281.4 19.1 %collective-permute-start.23 = (bf16[2,64,1536]{2,1,0:T(8,128)(2,1)S(1)}, bf16[2,64,1536]{2,1,0:T(8,128)(2,1)S(1)}, u32[]{:S(2)}, u32[]{:S(2)}) collective-permute-start(bf16[2,64,1536]{2,1,0:T(8,128)(2,1)S(1)} %fusion.14), channel_id=1, source_target_pairs={{0,16},{1,17},{16,0},{17,1},{2,18},{3,19},{18,2},{19,3},{4,20},{5,... | collective-permute-start | bytes 1179656 | tf_op jit(solution)/shard_map/ppermute | solution.py:29
  339.6 19.2 %collective-permute-start.29 = (bf16[2,64,1536]{2,1,0:T(8,128)(2,1)S(1)}, bf16[2,64,1536]{2,1,0:T(8,128)(2,1)S(1)}, u32[]{:S(2)}, u32[]{:S(2)}) collective-permute-start(bf16[2,64,1536]{2,1,0:T(8,128)(2,1)S(1)} %fusion.15), channel_id=1, source_target_pairs={{0,16},{1,17},{16,0},{17,1},{2,18},{3,19},{18,2},{19,3},{4,20},{5,... | collective-permute-start | bytes 1179656 | tf_op jit(solution)/shard_map/ppermute | solution.py:29
  340.1 18.8 %collective-permute-start.30 = (bf16[2,64,1536]{2,1,0:T(8,128)(2,1)S(1)}, bf16[2,64,1536]{2,1,0:T(8,128)(2,1)S(1)}, u32[]{:S(2)}, u32[]{:S(2)}) collective-permute-start(bf16[2,64,1536]{2,1,0:T(8,128)(2,1)S(1)} %fusion.15), channel_id=1, source_target_pairs={{0,17},{1,16},{16,1},{17,0},{2,19},{3,18},{18,3},{19,2},{4,21},{5,... | collective-permute-start | bytes 1179656 | tf_op jit(solution)/shard_map/ppermute | solution.py:29
  363.6 23.3 %all-to-all-start.5 = ((bf16[8,192,128]{2,1,0:T(8,128)(2,1)}), bf16[8,192,128]{2,1,0:T(8,128)(2,1)}, u32[]{:S(2)}, u32[]{:S(2)}) async-start(bf16[8,192,128]{2,1,0:T(8,128)(2,1)} %copy-done.26), calls=%async_computation.5 | async-start | bytes 786432 | tf_op jit(solution)/shard_map/all_to_all | solution.py:769
  369.6 41.5 %collective-permute-start.31 = (bf16[2,2,1,32,1536]{4,3,2,1,0:T(8,128)(2,1)}, bf16[2,2,1,32,1536]{4,3,2,1,0:T(8,128)(2,1)}, u32[]{:S(2)}, u32[]{:S(2)}) collective-permute-start(bf16[2,2,1,32,1536]{4,3,2,1,0:T(8,128)(2,1)} %convert_element_type.243), channel_id=1, source_target_pairs={{0,1},{1,2},{2,3},{3,4},{4,5},{5,6},{6,7},{8,9},{9,10},{10,11},{11... | collective-permute-start | bytes 1179656 | tf_op jit(solution)/shard_map/ppermute | solution.py:108
  373.2 37.8 %collective-permute-start.32 = (bf16[2,2,1,32,1536]{4,3,2,1,0:T(8,128)(2,1)}, bf16[2,2,1,32,1536]{4,3,2,1,0:T(8,128)(2,1)}, u32[]{:S(2)}, u32[]{:S(2)}) collective-permute-start(bf16[2,2,1,32,1536]{4,3,2,1,0:T(8,128)(2,1)} %convert_element_type.243), channel_id=1, source_target_pairs={{1,0},{2,1},{3,2},{4,3},{5,4},{6,5},{7,6},{9,8},{10,9},{11,10},{12... | collective-permute-start | bytes 1179656 | tf_op jit(solution)/shard_map/ppermute | solution.py:109
  411.1 55.3 %all-to-all-start.6 = ((bf16[8,704,128]{2,1,0:T(8,128)(2,1)}), bf16[8,704,128]{2,1,0:T(8,128)(2,1)}, u32[]{:S(2)}, u32[]{:S(2)}) async-start(bf16[8,704,128]{2,1,0:T(8,128)(2,1)} %copy-done.21), calls=%async_computation.6 | async-start | bytes 2883584 | tf_op jit(solution)/shard_map/all_to_all | solution.py:845
  415.3 97.8 %reduce-scatter.6.cloned.1.call-start = ((), (), s32[]{:S(2)}) async-start(), calls=%async_computation.16 | async-start | bytes 2359296 | tf_op jit(solution)/shard_map/reduce_scatter | solution.py:102
  466.4 101.0 %reduce-scatter.8.cloned.1.call-start = ((), (), s32[]{:S(2)}) async-start(), calls=%async_computation.17 | async-start | bytes 3981312 | tf_op jit(solution)/shard_map/reduce_scatter | solution.py:102
  531.1 25.0 %collective-permute-start.45 = (bf16[96,512]{1,0:T(8,128)(2,1)S(1)}, bf16[96,512]{1,0:T(8,128)(2,1)}, u32[]{:S(2)}, u32[]{:S(2)}) collective-permute-start(bf16[96,512]{1,0:T(8,128)(2,1)S(1)} %pad_maximum_fusion.7), channel_id=1, source_target_pairs={{1,8},{3,10},{5,12},{7,14},{8,1},{10,3},{12,5},{14,7},{17,24},{19,... | collective-permute-start | bytes 294920 | tf_op jit(solution)/shard_map/ppermute | solution.py:71
  534.1 21.9 %collective-permute-start.44 = (f32[1,48]{1,0:T(1,128)}, f32[1,48]{1,0:T(1,128)}, u32[]{:S(2)}, u32[]{:S(2)}) collective-permute-start(f32[1,48]{1,0:T(1,128)} %bitcast.98), channel_id=1, source_target_pairs={{1,8},{3,10},{5,12},{7,14},{8,1},{10,3},{12,5},{14,7},{17,24},{19,... | collective-permute-start | bytes 584 | tf_op jit(solution)/shard_map/ppermute | solution.py:71
  568.5 36.1 %collective-permute-start.42 = (bf16[704,384]{1,0:T(8,128)(2,1)}, bf16[704,384]{1,0:T(8,128)(2,1)S(1)}, u32[]{:S(2)}, u32[]{:S(2)}) collective-permute-start(bf16[704,384]{1,0:T(8,128)(2,1)} %copy.160), channel_id=1, source_target_pairs={{1,2},{2,1},{4,8},{5,10},{6,9},{7,11},{8,17},{9,19},{10,16},{11,18... | collective-permute-start | bytes 1622024 | tf_op jit(solution)/shard_map/ppermute | solution.py:71
  570.6 20.5 %collective-permute-start.43 = (bf16[192,1152]{1,0:T(8,128)(2,1)}, bf16[192,1152]{1,0:T(8,128)(2,1)S(1)}, u32[]{:S(2)}, u32[]{:S(2)}) collective-permute-start(bf16[192,1152]{1,0:T(8,128)(2,1)} %reduce-scatter.8.cloned.1.call-done), channel_id=1, source_target_pairs={{1,8},{3,10},{5,12},{7,14},{8,1},{10,3},{12,5},{14,7},{17,24},{19,... | collective-permute-start | bytes 1327112 | tf_op jit(solution)/shard_map/ppermute | solution.py:71
  (159 other events, 1221.1 us)
Sparse Core Ops, SparseCore 0:
  21.5 43.2 all-gather.4
  67.0 33.4 all-gather.6
  127.2 79.6 all-gather.8
  208.9 36.8 all-gather.10
  331.7 132.7 reduce-scatter.3
  466.6 46.4 reduce-scatter.5
  515.5 46.1 reduce-scatter.7
